TPU v7x, 512 devices: a whole 4x4x16 slice. The times are simulated.
512 devices in a mesh: inp: 8 (over z_hi, y), hid: 8 (over x, core), tok: 8 (over z_lo).
Axes of the slice: x: 4, y: 4, z: 16 (z_hi: 2, z_lo: 8; z = z_hi * 8 + z_lo), core: 2. Of those that a mesh axis runs over, the one named last changes fastest.
Arguments:
- tokens: float32 [1024, 3072], P(('tok', 'hid'), 'inp'), may hold values from -6 to 6
- targets: float32 [1024, 3072], P(('tok', 'hid'), 'inp'), may hold values from -6 to 6
- sample_ids: int32 [1024], P(('tok', 'hid')), may hold values from 0 to 15, never falling along the last dimension, each value on 1 to 128 neighbouring positions
- labels: int32 [16], replicated, may hold values from 0 to 1
- utility: float32 [16], replicated, may hold values from 0.5 to 4
- ref_loss: float32 [16], replicated, may hold values from 0.9 to 1.9
- w_in: float32 [3072, 6144], P(('inp', 'tok'), 'hid'), may hold values from -0.109375 to 0.109375
- w_out: float32 [6144, 3072], P(('hid', 'tok'), 'inp'), may hold values from -0.078125 to 0.078125
- m_in: float32 [3072, 6144], P(('inp', 'tok'), 'hid'), may hold values from -6 to 6
- m_out: float32 [6144, 3072], P(('hid', 'tok'), 'inp'), may hold values from -6 to 6
- v_in: float32 [3072, 6144], P(('inp', 'tok'), 'hid'), may hold values from 0.5 to 20
- v_out: float32 [6144, 3072], P(('hid', 'tok'), 'inp'), may hold values from 0.5 to 20
- e_in: float32 [3072, 6144], P(('inp', 'tok'), 'hid'), may hold values from -0.109375 to 0.109375
- e_out: float32 [6144, 3072], P(('hid', 'tok'), 'inp'), may hold values from -0.078125 to 0.078125
Outputs:
- loss: float32 [], replicated
- new_w_in: float32 [3072, 6144], P('inp', 'hid')
- new_w_out: float32 [6144, 3072], P('hid', 'inp')
- new_m_in: float32 [3072, 6144], P(('inp', 'tok'), 'hid')
- new_m_out: float32 [6144, 3072], P(('hid', 'tok'), 'inp')
- new_v_in: float32 [3072, 6144], P(('inp', 'tok'), 'hid')
- new_v_out: float32 [6144, 3072], P(('hid', 'tok'), 'inp')
- new_e_in: float32 [3072, 6144], P(('inp', 'tok'), 'hid')
- new_e_out: float32 [6144, 3072], P(('hid', 'tok'), 'inp')
Inputs may be any that keep to these rules, and one draw needn't show every extreme that they name: `sample_ids`: sample numbers never fall along the tokens; every sample has 1 to 128 tokens, one exactly that many.
All inputs are finite; a program needn't handle non-finite values.
Results may differ from a plain program's by a relative error of at most 0.00022.
Values sent between devices are 32-bit elements; how exact they have to be, the bound alone decides.
No kernel may reach another device: no remote copies, remote signals or barrier semaphores. Data moves between devices by JAX's collectives and lax.ppermute only.
A program may use at most 64 MiB of HBM per device.

v0:
```python
import jax
import jax.numpy as jnp
from jax import lax
from jax.sharding import PartitionSpec as P


D = 3072
SAMPLES = 16


mixed = lax.Precision.HIGH
gelu_c = 0.7978845608028654
gelu_k = 0.044715
kto_beta = 4.0
loss_scale = 1048576.0
beta_one = 0.9
beta_two = 0.95
adam_eps = 1e-08
learn_rate = 0.001
decay_rate = 0.1
ema_rate = 0.99
bias_one = 1.0 - 0.9**10
bias_two = 1.0 - 0.95**10


QUADS = [[0, 1, 2, 3], [4, 5, 6, 7]]
FAR_HALF = [(i, (i + 4) % 8) for i in range(8)]
FOLD = (0, 2, 4, 6, 7, 5, 3, 1)


def gelu_parts(hidden):
    inner = gelu_c * (hidden + gelu_k * hidden * hidden * hidden)
    tangent = jnp.tanh(inner)
    active = 0.5 * hidden * (1.0 + tangent)
    slope = 0.5 * (1.0 + tangent) + 0.5 * hidden * (1.0 - tangent * tangent) * gelu_c * (
        1.0 + 3.0 * gelu_k * hidden * hidden
    )
    return (active, slope)


def adamw(weight, moment_one, moment_two, average, gradient):
    moment_one = beta_one * moment_one + (1.0 - beta_one) * gradient
    moment_two = beta_two * moment_two + (1.0 - beta_two) * gradient * gradient
    update = learn_rate * (moment_one / bias_one) / (jnp.sqrt(moment_two / bias_two) + adam_eps)
    weight = weight - update - learn_rate * decay_rate * weight
    average = ema_rate * average + (1.0 - ema_rate) * weight
    return (weight, moment_one, moment_two, average)


def kto_terms(sq_sums, counts, labels, utility, ref_loss):
    sample_loss = sq_sums / (counts * D)
    signs = 2.0 * labels.astype(jnp.float32) - 1.0
    chosen = jax.nn.sigmoid(signs * kto_beta * (ref_loss - sample_loss))
    loss = -jnp.sum(utility * chosen) / SAMPLES
    dloss = utility * chosen * (1.0 - chosen) * signs * kto_beta / SAMPLES
    sample_coef = loss_scale * 2.0 * dloss / (counts * D)
    return (loss, sample_coef)


def product(left, right, left_dim, right_dim):
    return lax.dot_general(
        left,
        right,
        (((left_dim,), (right_dim,)), ((), ())),
        precision=mixed,
        preferred_element_type=jnp.float32,
    )


def scatter_sum(part, axis, size, groups=None):
    blocks = part.reshape(size, part.shape[0] // size, part.shape[1])
    return jnp.sum(lax.all_to_all(blocks, axis, 0, 0, axis_index_groups=groups), axis=0)


def spread(block, axis, size, groups=None):
    copies = jnp.broadcast_to(block[None], (size,) + block.shape)
    return lax.all_to_all(copies, axis, 0, 0, axis_index_groups=groups)


def y_sum(part):
    return scatter_sum(part, "inp", 4, QUADS)


def far_sum(quarter):
    return quarter + lax.ppermute(quarter, "inp", FAR_HALF)


def y_gather(block):
    every = spread(block, "inp", 4, QUADS)
    return every.reshape(4 * block.shape[0], block.shape[1])


def queue_gather(shard, after=None):
    folded = lax.all_gather(shard, "tok", axis=0, tiled=False, axis_index_groups=[list(FOLD)])
    if after is not None:
        folded, after = lax.optimization_barrier((folded, after))
    return ring_order(folded).reshape(8 * shard.shape[0], shard.shape[1]), after


def fold_rows(full):
    pairs = full.reshape(4, 2, full.shape[0] // 8, full.shape[1])
    folded = jnp.concatenate([pairs[:, 0], jnp.flip(pairs[:, 1], axis=0)], axis=0)
    return folded.reshape(full.shape)


def queue_scatter(folded):
    return lax.psum_scatter(
        folded, "tok", scatter_dimension=0, tiled=True, axis_index_groups=[list(FOLD)]
    )


def ring_order(folded):
    pairs = jnp.stack([folded[:4], jnp.flip(folded[4:], axis=0)], axis=1)
    return pairs.reshape((8,) + folded.shape[1:])


def core_gather(shard, split):
    small = spread(shard[split:], "tok", 8)
    large = lax.all_gather(
        shard[:split], "tok", axis=0, tiled=False, axis_index_groups=[list(FOLD)]
    )
    every = jnp.concatenate([ring_order(large), small], axis=1)
    return every.reshape(8 * shard.shape[0], shard.shape[1])


def core_scatter(full, partner):
    upper = lax.axis_index("tok") >= 4
    rows = full.shape[0] // 8
    blocks = jnp.transpose(full.reshape(2, 4, rows, full.shape[1]), (1, 0, 2, 3))
    pair = jnp.sum(lax.all_to_all(blocks, "tok", 0, 0, axis_index_groups=QUADS), axis=0)
    keep = jnp.where(upper, pair[1], pair[0])
    send = jnp.where(upper, pair[0], pair[1])
    keep, partner = lax.optimization_barrier((keep, partner))
    other = lax.ppermute(send, "tok", FAR_HALF)
    return keep + other, partner


def on_device(
    tokens,
    targets,
    sample_ids,
    labels,
    utility,
    ref_loss,
    w_in,
    w_out,
    m_in,
    m_out,
    v_in,
    v_out,
    e_in,
    e_out,
):
    w_in_block = core_gather(w_in, 40)
    id_lanes = jnp.broadcast_to(sample_ids.astype(jnp.float32)[:, None], (16, 128))
    rows_and_ids = spread(jnp.concatenate([tokens, id_lanes], axis=1), "hid", 8)
    rows_and_ids = rows_and_ids.reshape(128, 512)
    all_rows = rows_and_ids[:, :384]
    all_ids = rows_and_ids[:, 384].astype(jnp.int32)
    onehot = (all_ids[:, None] == jnp.arange(SAMPLES, dtype=jnp.int32)[None, :]).astype(
        jnp.float32
    )
    hidden = far_sum(y_sum(product(all_rows, w_in_block, 1, 0)))
    active_rows, slope_rows = gelu_parts(hidden)
    active = y_gather(active_rows)
    w_out_block, active = queue_gather(w_out, active)

    output = scatter_sum(product(active, w_out_block, 1, 0), "hid", 8)
    error = spread(output - targets, "hid", 8).reshape(128, 384)
    token_sq = jnp.sum(error * error, axis=1)
    local_sq = jnp.sum(token_sq[:, None] * onehot, axis=0)
    leading = lax.axis_index("inp") == 0
    local_counts = jnp.sum(onehot, axis=0) * jnp.where(leading, 1.0, 0.0)
    stats = jnp.concatenate([local_sq, local_counts, jnp.zeros((96,), jnp.float32)])[None, :]
    d_quarter = y_sum(product(error, w_out_block, 1, 1))
    stats, d_quarter = lax.optimization_barrier((stats, d_quarter))
    stats = jnp.sum(spread(stats, ("inp", "tok"), 64), axis=(0, 1))
    d_active = far_sum(d_quarter)
    loss, sample_coef = kto_terms(
        stats[:SAMPLES], stats[SAMPLES : 2 * SAMPLES], labels, utility, ref_loss
    )
    coef = jnp.sum(onehot * sample_coef[None, :], axis=1)[:, None]
    own_rows = lax.rem(lax.axis_index("inp"), 4) * 32
    own_coef = lax.dynamic_slice(coef, (own_rows, 0), (32, 1))

    grad_fold = fold_rows(product(active, error * coef, 0, 0))
    d_rows = d_active * own_coef * slope_rows
    grad_fold, d_rows = lax.optimization_barrier((grad_fold, d_rows))
    grad_out = queue_scatter(grad_fold)
    d_hidden = y_gather(d_rows)
    grad_in, grad_out = core_scatter(product(all_rows, d_hidden, 0, 0), grad_out)

    weight_out, new_m_out, new_v_out, new_e_out = adamw(w_out, m_out, v_out, e_out, grad_out)
    new_w_out, _ = queue_gather(weight_out)
    weight_in, new_m_in, new_v_in, new_e_in = adamw(w_in, m_in, v_in, e_in, grad_in)
    new_w_in = core_gather(weight_in, 40)
    return (
        loss,
        new_w_in,
        new_w_out,
        new_m_in,
        new_m_out,
        new_v_in,
        new_v_out,
        new_e_in,
        new_e_out,
    )


def solution(mesh):
    in_specs = (
        P(("tok", "hid"), "inp"),
        P(("tok", "hid"), "inp"),
        P(("tok", "hid")),
        P(),
        P(),
        P(),
        P(("inp", "tok"), "hid"),
        P(("hid", "tok"), "inp"),
        P(("inp", "tok"), "hid"),
        P(("hid", "tok"), "inp"),
        P(("inp", "tok"), "hid"),
        P(("hid", "tok"), "inp"),
        P(("inp", "tok"), "hid"),
        P(("hid", "tok"), "inp"),
    )
    out_specs = (
        P(),
        P("inp", "hid"),
        P("hid", "inp"),
        P(("inp", "tok"), "hid"),
        P(("hid", "tok"), "inp"),
        P(("inp", "tok"), "hid"),
        P(("hid", "tok"), "inp"),
        P(("inp", "tok"), "hid"),
        P(("hid", "tok"), "inp"),
    )
    return jax.shard_map(
        on_device, mesh=mesh, in_specs=in_specs, out_specs=out_specs, check_vma=False
    )
```

profile of v0, /device:TPU:6, one launch (start us, length us, event | category | flops | bytes accessed | tf_op | source)
XLA Modules:
  0.0 348.0 jit_solution(15094653769869569640)
XLA Ops:
  7.2 0.7 all-gather.7.cloned.1.call-update
  7.9 0.7 convert_element_type.14
  8.7 0.7 pad_maximum_fusion.7
  9.4 0.7 broadcast_in_dim.23
  10.1 9.2 %all-to-all-start = ((f32[8,16,512]{2,1,0:T(8,128)}), f32[8,16,512]{2,1,0:T(8,128)S(1)}, u32[]{:S(2)}, u32[]{:S(2)}) async-start(f32[8,16,512]{2,1,0:T(8,128)} %broadcast_in_dim.23), calls=%async_computation | async-start | bytes 524288 | tf_op jit(solution)/shard_map/all_to_all | solution.py:77
  19.3 40.3 %all-gather.1 = f32[320,768]{1,0:T(8,128)S(1)} all-gather(f32[40,768]{1,0:T(8,128)S(1)} %slice-done.1), channel_id=3, replica_groups={{0,2,4,6,7,5,3,1},{8,10,12,14,15,13,11,9},{16,18,20,22,23,21,19,17},{24..., dimensions={0}, use_global_device_ids=true | all-gather | bytes 1105920 | tf_op jit(solution)/shard_map/all_gather | solution.py:119
  59.7 0.7 broadcast_in_dim.24
  60.4 5.6 %all-to-all-start.1 = ((f32[8,8,768]{2,1,0:T(8,128)}), f32[8,8,768]{2,1,0:T(8,128)S(1)}, u32[]{:S(2)}, u32[]{:S(2)}) async-start(f32[8,8,768]{2,1,0:T(8,128)} %broadcast_in_dim.24), calls=%async_computation.1 | async-start | bytes 393216 | tf_op jit(solution)/shard_map/all_to_all | solution.py:77
  66.2 0.1 copy.57
  66.3 13.9 %all-to-all-done.1 = f32[8,8,768]{2,1,0:T(8,128)S(1)} async-done(((f32[8,8,768]{2,1,0:T(8,128)}), f32[8,8,768]{2,1,0:T(8,128)S(1)}, u32[]{:S(2)}, u32[]{:S(2)}) %all-to-all-start.1) | async-done | bytes 196640 | tf_op jit(solution)/shard_map/all_to_all | solution.py:77
  80.2 0.1 pad_maximum_fusion
  80.3 0.5 fusion.14
  80.8 11.1 %all_to_all.55 = f32[4,32,768]{2,1,0:T(8,128)S(1)} all-to-all(f32[4,32,768]{2,1,0:T(8,128)S(1)} %fusion.14), channel_id=1, replica_groups={{0,64,128,192},{256,320,384,448},{1,65,129,193},{257,321,385,449},{2,66..., dimensions={0} | all-to-all | bytes 786432 | tf_op jit(solution)/shard_map/all_to_all | solution.py:72
  91.9 9.3 %collective-permute-start = (f32[32,768]{1,0:T(8,128)S(1)}, f32[32,768]{1,0:T(8,128)S(1)}, u32[]{:S(2)}, u32[]{:S(2)}) collective-permute-start(f32[32,768]{1,0:T(8,128)S(1)} %reduce_sum.90), channel_id=1, source_target_pairs={{0,256},{64,320},{128,384},{192,448},{256,0},{320,64},{384,128},{4... | collective-permute-start | bytes 294920 | tf_op jit(solution)/shard_map/ppermute | solution.py:85
  101.3 6.9 %collective-permute-done = f32[32,768]{1,0:T(8,128)S(1)} collective-permute-done((f32[32,768]{1,0:T(8,128)S(1)}, f32[32,768]{1,0:T(8,128)S(1)}, u32[]{:S(2)}, u32[]{:S(2)}) %collective-permute-start) | collective-permute-done | bytes 98336 | tf_op jit(solution)/shard_map/ppermute | solution.py:85
  108.3 9.8 %all_to_all.56 = f32[4,32,768]{2,1,0:T(8,128)S(1)} all-to-all(f32[4,32,768]{2,1,0:T(8,128)S(1)} %broadcast_in_dim.25), channel_id=1, replica_groups={{0,64,128,192},{256,320,384,448},{1,65,129,193},{257,321,385,449},{2,66..., dimensions={0} | all-to-all | bytes 786432 | tf_op jit(solution)/shard_map/all_to_all | solution.py:77
  118.1 1.3 slice_bitcast_fusion.2
  119.5 0.5 fusion.15
  120.1 12.9 %all_to_all.57 = f32[8,16,384]{2,1,0:T(8,128)S(1)} all-to-all(f32[8,16,384]{2,1,0:T(8,128)S(1)} %fusion.15), channel_id=1, replica_groups=mesh['inp'=8,'hid'=8,'tok'=8] {'hid'}, dimensions={0} | all-to-all | bytes 393216 | tf_op jit(solution)/shard_map/all_to_all | solution.py:72
  133.0 0.7 broadcast_in_dim.26
  133.7 5.4 %all-to-all-start.5 = ((f32[8,16,384]{2,1,0:T(8,128)}), f32[8,16,384]{2,1,0:T(8,128)S(1)}, u32[]{:S(2)}, u32[]{:S(2)}) async-start(f32[8,16,384]{2,1,0:T(8,128)} %broadcast_in_dim.26), calls=%async_computation.5 | async-start | bytes 393216 | tf_op jit(solution)/shard_map/all_to_all | solution.py:77
  139.1 0.1 fusion.8
  139.2 4.6 %all-to-all-done.5 = f32[8,16,384]{2,1,0:T(8,128)S(1)} async-done(((f32[8,16,384]{2,1,0:T(8,128)}), f32[8,16,384]{2,1,0:T(8,128)S(1)}, u32[]{:S(2)}, u32[]{:S(2)}) %all-to-all-start.5) | async-done | bytes 196640 | tf_op jit(solution)/shard_map/all_to_all | solution.py:77
  143.8 1.4 fusion.16
  145.2 0.1 multiply_reduce_fusion
  145.4 3.5 all-to-all-start.6
  148.8 0.1 select_reduce_fusion.1
  149.0 7.8 %all-to-all-done.6 = f32[4,32,768]{2,1,0:T(8,128)S(1)} async-done(((f32[4,32,768]{2,1,0:T(8,128)}), f32[4,32,768]{2,1,0:T(8,128)S(1)}, u32[]{:S(2)}, u32[]{:S(2)}) %all-to-all-start.6) | async-done | bytes 393248 | tf_op jit(solution)/shard_map/all_to_all | solution.py:72
  156.9 0.6 broadcast_in_dim.30
  157.5 7.6 %all-to-all-start.7 = ((f32[64,1,128]{2,1,0:T(1,128)}), f32[64,1,128]{2,1,0:T(1,128)S(1)}, u32[]{:S(2)}, u32[]{:S(2)}) async-start(f32[64,1,128]{2,1,0:T(1,128)} %broadcast_in_dim.30), calls=%async_computation.7 | async-start | bytes 65536 | tf_op jit(solution)/shard_map/all_to_all | solution.py:77
  165.2 0.2 copy.61
  165.3 12.3 %collective-permute-start.1 = (f32[32,768]{1,0:T(8,128)S(1)}, f32[32,768]{1,0:T(8,128)S(1)}, u32[]{:S(2)}, u32[]{:S(2)}) collective-permute-start(f32[32,768]{1,0:T(8,128)S(1)} %reduce_sum.95), channel_id=1, source_target_pairs={{0,256},{64,320},{128,384},{192,448},{256,0},{320,64},{384,128},{4... | collective-permute-start | bytes 294920 | tf_op jit(solution)/shard_map/ppermute | solution.py:85
  177.6 2.4 all-to-all-done.7
  180.1 0.1 multiply_divide_fusion
  180.2 0.1 select_reduce_fusion
  180.3 0.1 mul.258
  180.4 0.1 dynamic-slice.3
  180.5 0.1 broadcast_multiply_fusion
  180.6 0.6 fusion.17
  181.3 1.1 pad_maximum_fusion.2
  182.4 0.4 collective-permute-done.1
  182.9 0.1 fusion.7
  183.0 0.8 broadcast_in_dim.31
  183.7 4.4 %all-to-all-start.8 = ((f32[4,32,768]{2,1,0:T(8,128)}), f32[4,32,768]{2,1,0:T(8,128)S(1)}, u32[]{:S(2)}, u32[]{:S(2)}) async-start(f32[4,32,768]{2,1,0:T(8,128)} %broadcast_in_dim.31), calls=%async_computation.8 | async-start | bytes 786432 | tf_op jit(solution)/shard_map/all_to_all | solution.py:77
  188.1 0.1 copy.60
  188.2 7.3 %all-to-all-done.8 = f32[4,32,768]{2,1,0:T(8,128)S(1)} async-done(((f32[4,32,768]{2,1,0:T(8,128)}), f32[4,32,768]{2,1,0:T(8,128)S(1)}, u32[]{:S(2)}, u32[]{:S(2)}) %all-to-all-start.8) | async-done | bytes 393248 | tf_op jit(solution)/shard_map/all_to_all | solution.py:77
  195.5 0.6 convolution_bitcast_fusion
  196.1 1.1 copy.63
  197.2 5.6 %all-to-all-start.9 = ((f32[4,2,48,768]{3,2,1,0:T(8,128)}), f32[4,2,48,768]{3,2,1,0:T(8,128)S(1)}, u32[]{:S(2)}, u32[]{:S(2)}) async-start(f32[4,2,48,768]{3,2,1,0:T(8,128)} %copy.63), calls=%async_computation.9 | async-start | bytes 2359296 | tf_op jit(solution)/shard_map/all_to_all | solution.py:130
  202.8 0.7 reduce-scatter.2.cloned.1.call-update
  203.7 20.5 %all-to-all-done.9 = f32[4,2,48,768]{3,2,1,0:T(8,128)S(1)} async-done(((f32[4,2,48,768]{3,2,1,0:T(8,128)}), f32[4,2,48,768]{3,2,1,0:T(8,128)S(1)}, u32[]{:S(2)}, u32[]{:S(2)}) %all-to-all-start.9) | async-done | bytes 1179680 | tf_op jit(solution)/shard_map/all_to_all | solution.py:130
  224.1 0.1 reduce_sum.99
  224.3 34.6 %reduce-scatter.2.cloned.1.call-done = f32[96,384]{1,0:T(8,128)} async-done(((f32[768,384]{1,0:T(8,128)}), f32[96,384]{1,0:T(8,128)}) %reduce-scatter.2.cloned.1.call-update) | async-done | bytes 147472 | tf_op jit(solution)/shard_map/reduce_scatter | solution.py:107
  258.9 1.8 multiply_add_fusion.1
  260.8 5.2 %collective-permute-start.2 = (f32[48,768]{1,0:T(8,128)S(1)}, f32[48,768]{1,0:T(8,128)S(1)}, u32[]{:S(2)}, u32[]{:S(2)}) collective-permute-start(f32[48,768]{1,0:T(8,128)S(1)} %get-tuple-element.47), channel_id=1, source_target_pairs={{0,4},{1,5},{2,6},{3,7},{4,0},{5,1},{6,2},{7,3},{8,12},{9,13},{10,... | collective-permute-start | bytes 442376 | tf_op jit(solution)/shard_map/ppermute | solution.py:134
  266.0 0.6 multiply_reduce_fusion.1
  267.3 12.2 %collective-permute-done.2 = f32[48,768]{1,0:T(8,128)S(1)} collective-permute-done((f32[48,768]{1,0:T(8,128)S(1)}, f32[48,768]{1,0:T(8,128)S(1)}, u32[]{:S(2)}, u32[]{:S(2)}) %collective-permute-start.2) | collective-permute-done | bytes 147488 | tf_op jit(solution)/shard_map/ppermute | solution.py:134
  279.5 0.8 multiply_add_fusion.2
  280.3 0.7 broadcast_in_dim.32
  281.0 5.7 %all-to-all-start.10 = ((f32[8,8,768]{2,1,0:T(8,128)}), f32[8,8,768]{2,1,0:T(8,128)S(1)}, u32[]{:S(2)}, u32[]{:S(2)}) async-start(f32[8,8,768]{2,1,0:T(8,128)} %broadcast_in_dim.32), calls=%async_computation.11 | async-start | bytes 393216 | tf_op jit(solution)/shard_map/all_to_all | solution.py:77
  286.7 49.7 %all-gather.2 = f32[320,768]{1,0:T(8,128)S(1)} all-gather(f32[40,768]{1,0:T(8,128)S(1)} %slice.96), channel_id=4, replica_groups={{0,2,4,6,7,5,3,1},{8,10,12,14,15,13,11,9},{16,18,20,22,23,21,19,17},{24..., dimensions={0}, use_global_device_ids=true | all-gather | bytes 1105920 | tf_op jit(solution)/shard_map/all_gather | solution.py:119
  336.7 1.1 pad_maximum_fusion.3
  337.8 1.3 fusion.11
  339.3 1.1 copy.64
  (64 shorter events, 1.3 us)
Async XLA Ops:
  7.2 12.1 %slice-start.1 = ((f32[48,768]{1,0:T(8,128)}), f32[40,768]{1,0:T(8,128)S(1)}, s32[]{:S(2)}) async-start(f32[48,768]{1,0:T(8,128)} %param.20), calls=%async_computation.16 | async-start | bytes 245760 | tf_op jit(solution)/shard_map/slice | solution.py:120
  7.2 110.9 %all-gather.7.cloned.1.call-start = ((), (), s32[]{:S(2)}) async-start(), calls=%async_computation.13 | async-start | bytes 1327104 | tf_op jit(solution)/shard_map/all_gather | solution.py:94
  7.9 51.7 %slice-start = ((f32[48,768]{1,0:T(8,128)}), f32[8,768]{1,0:T(8,128)S(1)}, s32[]{:S(2)}) async-start(f32[48,768]{1,0:T(8,128)} %param.20), calls=%async_computation.15 | async-start | bytes 49152 | tf_op jit(solution)/shard_map/slice | solution.py:118
  10.1 49.5 %all-to-all-start = ((f32[8,16,512]{2,1,0:T(8,128)}), f32[8,16,512]{2,1,0:T(8,128)S(1)}, u32[]{:S(2)}, u32[]{:S(2)}) async-start(f32[8,16,512]{2,1,0:T(8,128)} %broadcast_in_dim.23), calls=%async_computation | async-start | bytes 524288 | tf_op jit(solution)/shard_map/all_to_all | solution.py:77
  60.4 19.8 %all-to-all-start.1 = ((f32[8,8,768]{2,1,0:T(8,128)}), f32[8,8,768]{2,1,0:T(8,128)S(1)}, u32[]{:S(2)}, u32[]{:S(2)}) async-start(f32[8,8,768]{2,1,0:T(8,128)} %broadcast_in_dim.24), calls=%async_computation.1 | async-start | bytes 393216 | tf_op jit(solution)/shard_map/all_to_all | solution.py:77
  91.9 16.3 %collective-permute-start = (f32[32,768]{1,0:T(8,128)S(1)}, f32[32,768]{1,0:T(8,128)S(1)}, u32[]{:S(2)}, u32[]{:S(2)}) collective-permute-start(f32[32,768]{1,0:T(8,128)S(1)} %reduce_sum.90), channel_id=1, source_target_pairs={{0,256},{64,320},{128,384},{192,448},{256,0},{320,64},{384,128},{4... | collective-permute-start | bytes 294920 | tf_op jit(solution)/shard_map/ppermute | solution.py:85
  119.5 13.4 %copy-start.8 = (f32[16,384]{1,0:T(8,128)S(1)}, f32[16,384]{1,0:T(8,128)}, u32[]{:S(2)}) copy-start(f32[16,384]{1,0:T(8,128)} %param.15) | copy-start | bytes 73732
  133.7 10.1 %all-to-all-start.5 = ((f32[8,16,384]{2,1,0:T(8,128)}), f32[8,16,384]{2,1,0:T(8,128)S(1)}, u32[]{:S(2)}, u32[]{:S(2)}) async-start(f32[8,16,384]{2,1,0:T(8,128)} %broadcast_in_dim.26), calls=%async_computation.5 | async-start | bytes 393216 | tf_op jit(solution)/shard_map/all_to_all | solution.py:77
  145.2 34.9 %copy-start.9 = (s32[16]{0:T(128)S(1)}, s32[16]{0:T(128)}, u32[]{:S(2)}) copy-start(s32[16]{0:T(128)} %param.17) | copy-start | bytes 196
  145.2 34.9 %copy-start.10 = (f32[16]{0:T(128)S(1)}, f32[16]{0:T(128)}, u32[]{:S(2)}) copy-start(f32[16]{0:T(128)} %param.19) | copy-start | bytes 196
  145.2 34.9 %copy-start.11 = (f32[16]{0:T(128)S(1)}, f32[16]{0:T(128)}, u32[]{:S(2)}) copy-start(f32[16]{0:T(128)} %param.18) | copy-start | bytes 196
  145.4 11.5 %all-to-all-start.6 = ((f32[4,32,768]{2,1,0:T(8,128)}), f32[4,32,768]{2,1,0:T(8,128)S(1)}, u32[]{:S(2)}, u32[]{:S(2)}) async-start(f32[4,32,768]{2,1,0:T(8,128)} %fusion.16), calls=%async_computation.6 | async-start | bytes 786432 | tf_op jit(solution)/shard_map/all_to_all | solution.py:72
  157.5 22.6 %all-to-all-start.7 = ((f32[64,1,128]{2,1,0:T(1,128)}), f32[64,1,128]{2,1,0:T(1,128)S(1)}, u32[]{:S(2)}, u32[]{:S(2)}) async-start(f32[64,1,128]{2,1,0:T(1,128)} %broadcast_in_dim.30), calls=%async_computation.7 | async-start | bytes 65536 | tf_op jit(solution)/shard_map/all_to_all | solution.py:77
  165.3 17.5 %collective-permute-start.1 = (f32[32,768]{1,0:T(8,128)S(1)}, f32[32,768]{1,0:T(8,128)S(1)}, u32[]{:S(2)}, u32[]{:S(2)}) collective-permute-start(f32[32,768]{1,0:T(8,128)S(1)} %reduce_sum.95), channel_id=1, source_target_pairs={{0,256},{64,320},{128,384},{192,448},{256,0},{320,64},{384,128},{4... | collective-permute-start | bytes 294920 | tf_op jit(solution)/shard_map/ppermute | solution.py:85
  183.7 11.7 %all-to-all-start.8 = ((f32[4,32,768]{2,1,0:T(8,128)}), f32[4,32,768]{2,1,0:T(8,128)S(1)}, u32[]{:S(2)}, u32[]{:S(2)}) async-start(f32[4,32,768]{2,1,0:T(8,128)} %broadcast_in_dim.31), calls=%async_computation.8 | async-start | bytes 786432 | tf_op jit(solution)/shard_map/all_to_all | solution.py:77
  197.2 26.9 %all-to-all-start.9 = ((f32[4,2,48,768]{3,2,1,0:T(8,128)}), f32[4,2,48,768]{3,2,1,0:T(8,128)S(1)}, u32[]{:S(2)}, u32[]{:S(2)}) async-start(f32[4,2,48,768]{3,2,1,0:T(8,128)} %copy.63), calls=%async_computation.9 | async-start | bytes 2359296 | tf_op jit(solution)/shard_map/all_to_all | solution.py:130
  202.8 56.1 %reduce-scatter.2.cloned.1.call-start = ((), (), s32[]{:S(2)}) async-start(), calls=%async_computation.12 | async-start | bytes 1327104 | tf_op jit(solution)/shard_map/reduce_scatter | solution.py:107
  203.6 55.4 %copy-start.1 = (f32[96,384]{1,0:T(8,128)S(1)}, f32[96,384]{1,0:T(8,128)}, u32[]{:S(2)}) copy-start(f32[96,384]{1,0:T(8,128)} %param.21) | copy-start | bytes 442372
  203.6 55.4 %copy-start.5 = (f32[96,384]{1,0:T(8,128)S(1)}, f32[96,384]{1,0:T(8,128)}, u32[]{:S(2)}) copy-start(f32[96,384]{1,0:T(8,128)} %param.27) | copy-start | bytes 442372
  203.6 55.4 %copy-start.6 = (f32[96,384]{1,0:T(8,128)S(1)}, f32[96,384]{1,0:T(8,128)}, u32[]{:S(2)}) copy-start(f32[96,384]{1,0:T(8,128)} %param.23) | copy-start | bytes 442372
  203.6 55.3 %copy-start.7 = (f32[96,384]{1,0:T(8,128)S(1)}, f32[96,384]{1,0:T(8,128)}, u32[]{:S(2)}) copy-start(f32[96,384]{1,0:T(8,128)} %param.25) | copy-start | bytes 442372
  203.6 134.2 %all-gather.9.cloned.1.call-start = ((), (), s32[]{:S(2)}) async-start(), calls=%async_computation.14 | async-start | bytes 1327104 | tf_op jit(solution)/shard_map/all_gather | solution.py:94
  224.2 55.2 %copy-start = (f32[48,768]{1,0:T(8,128)S(1)}, f32[48,768]{1,0:T(8,128)}, u32[]{:S(2)}) copy-start(f32[48,768]{1,0:T(8,128)} %param.20) | copy-start | bytes 442372
  224.2 55.2 %copy-start.2 = (f32[48,768]{1,0:T(8,128)S(1)}, f32[48,768]{1,0:T(8,128)}, u32[]{:S(2)}) copy-start(f32[48,768]{1,0:T(8,128)} %param.26) | copy-start | bytes 442372
  224.2 55.2 %copy-start.3 = (f32[48,768]{1,0:T(8,128)S(1)}, f32[48,768]{1,0:T(8,128)}, u32[]{:S(2)}) copy-start(f32[48,768]{1,0:T(8,128)} %param.22) | copy-start | bytes 442372
  224.2 55.2 %copy-start.4 = (f32[48,768]{1,0:T(8,128)S(1)}, f32[48,768]{1,0:T(8,128)}, u32[]{:S(2)}) copy-start(f32[48,768]{1,0:T(8,128)} %param.24) | copy-start | bytes 442372
  260.8 18.7 %collective-permute-start.2 = (f32[48,768]{1,0:T(8,128)S(1)}, f32[48,768]{1,0:T(8,128)S(1)}, u32[]{:S(2)}, u32[]{:S(2)}) collective-permute-start(f32[48,768]{1,0:T(8,128)S(1)} %get-tuple-element.47), channel_id=1, source_target_pairs={{0,4},{1,5},{2,6},{3,7},{4,0},{5,1},{6,2},{7,3},{8,12},{9,13},{10,... | collective-permute-start | bytes 442376 | tf_op jit(solution)/shard_map/ppermute | solution.py:134
  281.0 55.7 %all-to-all-start.10 = ((f32[8,8,768]{2,1,0:T(8,128)}), f32[8,8,768]{2,1,0:T(8,128)S(1)}, u32[]{:S(2)}, u32[]{:S(2)}) async-start(f32[8,8,768]{2,1,0:T(8,128)} %broadcast_in_dim.32), calls=%async_computation.11 | async-start | bytes 393216 | tf_op jit(solution)/shard_map/all_to_all | solution.py:77
Sparse Core Ops, SparseCore 0:
  10.1 62.4 all-gather.6
  207.0 51.8 reduce-scatter.1
  261.0 58.6 all-gather.8
where the time goes:
time: 351 us; the launch traced here: 348 us
  blocking collectives  124 us (35%)
  waiting for transfers between devices  112 us (32%)
  starting transfers between devices  73.9 us (21%)
  between operations  16 us (5%)
  local copies, waits for them, and re-layouts  10.3 us (3%)
  other arithmetic  8.23 us (2%)
  matrix products  3.63 us (1%)
    all_gather x2, blocking collectives, core_gather(): lax.all_gather(shard[:split], 'tok', axis=0, tiled=False, axis_index_grou...  90.1 us
    all_to_all x6, starting transfers between devices, spread(): return lax.all_to_all(copies, axis, 0, 0, axis_index_groups=groups)  37.9 us
    reduce_scatter x1, waiting for transfers between devices, queue_scatter(): lax.psum_scatter(folded, 'tok', scatter_dimension=0, tiled=True, axis_ind...  34.6 us
    all_to_all x6, waiting for transfers between devices, spread(): return lax.all_to_all(copies, axis, 0, 0, axis_index_groups=groups)  28.2 us
    all_to_all x2, blocking collectives, scatter_sum(): lax.all_to_all(blocks, axis, 0, 0, axis_index_groups=groups)  24 us
    ppermute x2, starting transfers between devices, far_sum(): return quarter + lax.ppermute(quarter, 'inp', FAR_HALF)  21.6 us
    all_to_all x1, waiting for transfers between devices, core_scatter(): lax.all_to_all(blocks, 'tok', 0, 0, axis_index_groups=QUADS)  20.5 us
    ppermute x1, waiting for transfers between devices, core_scatter(): other = lax.ppermute(send, 'tok', FAR_HALF)  12.2 us
  transfers between devices with their start and end apart: 14, of which 10 were waited for; matrix products, arithmetic and copies ran while one was open for 3% of the time, Pallas kernels for 0%

commit v1 on v0

--- a/solution.py
+++ b/solution.py
@@ -123,13 +123,22 @@
     return every.reshape(8 * shard.shape[0], shard.shape[1])
 
 
-def core_scatter(full, partner):
+def quad_columns(rows):
+    blocks = jnp.transpose(rows.reshape(128, 2, 4, 48), (2, 0, 1, 3)).reshape(4, 128, 96)
+    every = lax.all_to_all(blocks, "tok", 0, 0, axis_index_groups=QUADS)
+    return jnp.transpose(every.reshape(4, 4, 32, 96), (1, 0, 2, 3)).reshape(512, 96)
+
+
+def quad_rows(block):
+    near = spread(block, "tok", 4, QUADS).reshape(128, 768)
+    return spread(near, "inp", 4, QUADS).reshape(512, 768)
+
+
+def half_sum(pair, partner):
     upper = lax.axis_index("tok") >= 4
-    rows = full.shape[0] // 8
-    blocks = jnp.transpose(full.reshape(2, 4, rows, full.shape[1]), (1, 0, 2, 3))
-    pair = jnp.sum(lax.all_to_all(blocks, "tok", 0, 0, axis_index_groups=QUADS), axis=0)
-    keep = jnp.where(upper, pair[1], pair[0])
-    send = jnp.where(upper, pair[0], pair[1])
+    rows = pair.shape[0] // 2
+    keep = jnp.where(upper, pair[rows:], pair[:rows])
+    send = jnp.where(upper, pair[:rows], pair[rows:])
     keep, partner = lax.optimization_barrier((keep, partner))
     other = lax.ppermute(send, "tok", FAR_HALF)
     return keep + other, partner
@@ -151,11 +160,12 @@
     e_in,
     e_out,
 ):
-    w_in_block = core_gather(w_in, 40)
+    w_in_block, _ = queue_gather(w_in)
     id_lanes = jnp.broadcast_to(sample_ids.astype(jnp.float32)[:, None], (16, 128))
     rows_and_ids = spread(jnp.concatenate([tokens, id_lanes], axis=1), "hid", 8)
     rows_and_ids = rows_and_ids.reshape(128, 512)
     all_rows = rows_and_ids[:, :384]
+    all_rows, columns = lax.optimization_barrier((all_rows, quad_columns(all_rows)))
     all_ids = rows_and_ids[:, 384].astype(jnp.int32)
     onehot = (all_ids[:, None] == jnp.arange(SAMPLES, dtype=jnp.int32)[None, :]).astype(
         jnp.float32
@@ -187,8 +197,7 @@
     d_rows = d_active * own_coef * slope_rows
     grad_fold, d_rows = lax.optimization_barrier((grad_fold, d_rows))
     grad_out = queue_scatter(grad_fold)
-    d_hidden = y_gather(d_rows)
-    grad_in, grad_out = core_scatter(product(all_rows, d_hidden, 0, 0), grad_out)
+    grad_in, grad_out = half_sum(product(columns, quad_rows(d_rows), 0, 0), grad_out)
 
     weight_out, new_m_out, new_v_out, new_e_out = adamw(w_out, m_out, v_out, e_out, grad_out)
     new_w_out, _ = queue_gather(weight_out)

time: 351 us -> 336 us (0.957)
  blocking collectives: 124 us -> 83.7 us
  waiting for transfers between devices: 112 us -> 145 us
  starting transfers between devices: 73.9 us -> 65.9 us
    all_gather x2 -> x3, waiting for transfers between devices: 0.01 us -> 50.3 us  [queue_gather(): lax.all_gather(shard, 'tok', axis=0, tiled=False, axis_index_groups=[list...]
    all_gather x2 -> x1, blocking collectives: 90.1 us -> 50.3 us  [core_gather(): lax.all_gather(shard[:split], 'tok', axis=0, tiled=False, axis_index_grou...]
    all_to_all x1, waiting for transfers between devices: 20.5 us -> 8.96 us  [quad_columns(): every = lax.all_to_all(blocks, 'tok', 0, 0, axis_index_groups=QUADS)]
    reduce_scatter x1, waiting for transfers between devices: 34.6 us -> 26.6 us  [queue_scatter(): lax.psum_scatter(folded, 'tok', scatter_dimension=0, tiled=True, axis_ind...]
    all_to_all x2, blocking collectives: 24 us -> 19.7 us  [scatter_sum(): lax.all_to_all(blocks, axis, 0, 0, axis_index_groups=groups)]
    all_to_all x6, starting transfers between devices: 37.9 us -> 33.7 us  [spread(): return lax.all_to_all(copies, axis, 0, 0, axis_index_groups=groups)]
    all_to_all x1, blocking collectives: 9.77 us -> 13.7 us  [spread(): return lax.all_to_all(copies, axis, 0, 0, axis_index_groups=groups)]
  transfers between devices with their start and end apart: 14 -> 15, of which waited for: 10 -> 12; matrix products, arithmetic and copies ran while one was open for 3% -> 4% of each run, Pallas kernels for 0% -> 0%
where the time goes in v1:
time: 336 us; the launch traced here: 334 us
  waiting for transfers between devices  145 us (43%)
  blocking collectives  83.7 us (25%)
  starting transfers between devices  65.9 us (20%)
  between operations  16 us (5%)
  local copies, waits for them, and re-layouts  11.8 us (4%)
  other arithmetic  8.06 us (2%)
  matrix products  3.61 us (1%)
    all_gather x3, waiting for transfers between devices, queue_gather(): lax.all_gather(shard, 'tok', axis=0, tiled=False, axis_index_groups=[list...  50.3 us
    all_gather x1, blocking collectives, core_gather(): lax.all_gather(shard[:split], 'tok', axis=0, tiled=False, axis_index_grou...  50.3 us
    all_to_all x6, starting transfers between devices, spread(): return lax.all_to_all(copies, axis, 0, 0, axis_index_groups=groups)  33.7 us
    all_to_all x6, waiting for transfers between devices, spread(): return lax.all_to_all(copies, axis, 0, 0, axis_index_groups=groups)  28.9 us
    reduce_scatter x1, waiting for transfers between devices, queue_scatter(): lax.psum_scatter(folded, 'tok', scatter_dimension=0, tiled=True, axis_ind...  26.6 us
    ppermute x2, starting transfers between devices, far_sum(): return quarter + lax.ppermute(quarter, 'inp', FAR_HALF)  20.6 us
    all_to_all x2, blocking collectives, scatter_sum(): lax.all_to_all(blocks, axis, 0, 0, axis_index_groups=groups)  19.7 us
    all_to_all x1, blocking collectives, spread(): return lax.all_to_all(copies, axis, 0, 0, axis_index_groups=groups)  13.7 us
  transfers between devices with their start and end apart: 15, of which 12 were waited for; matrix products, arithmetic and copies ran while one was open for 4% of the time, Pallas kernels for 0%

profile of v1, /device:TPU:6, one launch (start us, length us, event | category | flops | bytes accessed | tf_op | source)
XLA Modules:
  0.0 333.9 jit_solution(4922872784613007607)
XLA Ops:
  7.2 0.7 all-gather.10.cloned.1.call-update
  7.9 0.7 convert_element_type.14
  8.6 0.7 pad_maximum_fusion.6
  9.4 13.7 %all_to_all.55 = f32[8,16,512]{2,1,0:T(8,128)S(1)} all-to-all(f32[8,16,512]{2,1,0:T(8,128)S(1)} %broadcast_in_dim.25), channel_id=1, replica_groups=mesh['inp'=8,'hid'=8,'tok'=8] {'hid'}, dimensions={0} | all-to-all | bytes 524288 | tf_op jit(solution)/shard_map/all_to_all | solution.py:77
  23.1 0.1 copy.59
  23.2 0.7 copy.60
  23.9 3.4 %all-to-all-start.1 = ((f32[4,128,96]{1,2,0:T(8,128)}), f32[4,128,96]{1,2,0:T(8,128)S(1)}, u32[]{:S(2)}, u32[]{:S(2)}) async-start(f32[4,128,96]{1,2,0:T(8,128)} %bitcast.4), calls=%async_computation.1 | async-start | bytes 393216 | tf_op jit(solution)/shard_map/all_to_all | solution.py:128
  27.3 0.7 all-gather.8.cloned.1.call-update
  28.0 9.0 %all-to-all-done.1 = f32[4,128,96]{1,2,0:T(8,128)S(1)} async-done(((f32[4,128,96]{1,2,0:T(8,128)}), f32[4,128,96]{1,2,0:T(8,128)S(1)}, u32[]{:S(2)}, u32[]{:S(2)}) %all-to-all-start.1) | async-done | bytes 196640 | tf_op jit(solution)/shard_map/all_to_all | solution.py:128
  37.0 0.1 copy.61
  37.2 29.4 %all-gather.10.cloned.1.call-done = f32[384,768]{1,0:T(8,128)} async-done(((f32[48,768]{1,0:T(8,128)}), f32[384,768]{1,0:T(8,128)}) %all-gather.10.cloned.1.call-update) | async-done | bytes 1179664 | tf_op jit(solution)/shard_map/all_gather | solution.py:94
  66.5 1.3 fusion.12
  67.9 0.1 pad_maximum_fusion
  68.0 0.5 fusion.14
  68.5 10.7 %all_to_all.56 = f32[4,32,768]{2,1,0:T(8,128)S(1)} all-to-all(f32[4,32,768]{2,1,0:T(8,128)S(1)} %fusion.14), channel_id=1, replica_groups={{0,64,128,192},{256,320,384,448},{1,65,129,193},{257,321,385,449},{2,66..., dimensions={0} | all-to-all | bytes 786432 | tf_op jit(solution)/shard_map/all_to_all | solution.py:72
  79.2 8.3 %collective-permute-start = (f32[32,768]{1,0:T(8,128)S(1)}, f32[32,768]{1,0:T(8,128)S(1)}, u32[]{:S(2)}, u32[]{:S(2)}) collective-permute-start(f32[32,768]{1,0:T(8,128)S(1)} %reduce_sum.81), channel_id=1, source_target_pairs={{0,256},{64,320},{128,384},{192,448},{256,0},{320,64},{384,128},{4... | collective-permute-start | bytes 294920 | tf_op jit(solution)/shard_map/ppermute | solution.py:85
  87.5 9.4 %collective-permute-done = f32[32,768]{1,0:T(8,128)S(1)} collective-permute-done((f32[32,768]{1,0:T(8,128)S(1)}, f32[32,768]{1,0:T(8,128)S(1)}, u32[]{:S(2)}, u32[]{:S(2)}) %collective-permute-start) | collective-permute-done | bytes 98336 | tf_op jit(solution)/shard_map/ppermute | solution.py:85
  96.9 0.8 broadcast_in_dim.26
  97.7 3.5 %all-to-all-start.3 = ((f32[4,32,768]{2,1,0:T(8,128)}), f32[4,32,768]{2,1,0:T(8,128)S(1)}, u32[]{:S(2)}, u32[]{:S(2)}) async-start(f32[4,32,768]{2,1,0:T(8,128)} %broadcast_in_dim.26), calls=%async_computation.3 | async-start | bytes 786432 | tf_op jit(solution)/shard_map/all_to_all | solution.py:77
  101.1 20.9 %all-gather.8.cloned.1.call-done = f32[768,384]{1,0:T(8,128)} async-done(((f32[96,384]{1,0:T(8,128)}), f32[768,384]{1,0:T(8,128)}) %all-gather.8.cloned.1.call-update) | async-done | bytes 1179664 | tf_op jit(solution)/shard_map/all_gather | solution.py:94
  122.1 1.3 slice_bitcast_fusion.2
  123.6 0.5 fusion.15
  124.1 9.0 %all_to_all.57 = f32[8,16,384]{2,1,0:T(8,128)S(1)} all-to-all(f32[8,16,384]{2,1,0:T(8,128)S(1)} %fusion.15), channel_id=1, replica_groups=mesh['inp'=8,'hid'=8,'tok'=8] {'hid'}, dimensions={0} | all-to-all | bytes 393216 | tf_op jit(solution)/shard_map/all_to_all | solution.py:72
  133.2 0.7 broadcast_in_dim.27
  133.9 5.4 %all-to-all-start.5 = ((f32[8,16,384]{2,1,0:T(8,128)}), f32[8,16,384]{2,1,0:T(8,128)S(1)}, u32[]{:S(2)}, u32[]{:S(2)}) async-start(f32[8,16,384]{2,1,0:T(8,128)} %broadcast_in_dim.27), calls=%async_computation.5 | async-start | bytes 393216 | tf_op jit(solution)/shard_map/all_to_all | solution.py:77
  139.3 0.1 fusion.8
  139.4 4.6 %all-to-all-done.5 = f32[8,16,384]{2,1,0:T(8,128)S(1)} async-done(((f32[8,16,384]{2,1,0:T(8,128)}), f32[8,16,384]{2,1,0:T(8,128)S(1)}, u32[]{:S(2)}, u32[]{:S(2)}) %all-to-all-start.5) | async-done | bytes 196640 | tf_op jit(solution)/shard_map/all_to_all | solution.py:77
  144.0 1.4 fusion.16
  145.4 0.1 multiply_reduce_fusion
  145.6 3.5 %all-to-all-start.6 = ((f32[4,32,768]{2,1,0:T(8,128)}), f32[4,32,768]{2,1,0:T(8,128)S(1)}, u32[]{:S(2)}, u32[]{:S(2)}) async-start(f32[4,32,768]{2,1,0:T(8,128)} %fusion.16), calls=%async_computation.6 | async-start | bytes 786432 | tf_op jit(solution)/shard_map/all_to_all | solution.py:72
  149.0 0.1 select_reduce_fusion.1
  149.2 7.8 %all-to-all-done.6 = f32[4,32,768]{2,1,0:T(8,128)S(1)} async-done(((f32[4,32,768]{2,1,0:T(8,128)}), f32[4,32,768]{2,1,0:T(8,128)S(1)}, u32[]{:S(2)}, u32[]{:S(2)}) %all-to-all-start.6) | async-done | bytes 393248 | tf_op jit(solution)/shard_map/all_to_all | solution.py:72
  157.1 0.6 broadcast_in_dim.31
  157.7 8.3 %all-to-all-start.7 = ((f32[64,1,128]{2,1,0:T(1,128)}), f32[64,1,128]{2,1,0:T(1,128)S(1)}, u32[]{:S(2)}, u32[]{:S(2)}) async-start(f32[64,1,128]{2,1,0:T(1,128)} %broadcast_in_dim.31), calls=%async_computation.7 | async-start | bytes 65536 | tf_op jit(solution)/shard_map/all_to_all | solution.py:77
  166.0 0.2 copy.66
  166.2 12.3 %collective-permute-start.1 = (f32[32,768]{1,0:T(8,128)S(1)}, f32[32,768]{1,0:T(8,128)S(1)}, u32[]{:S(2)}, u32[]{:S(2)}) collective-permute-start(f32[32,768]{1,0:T(8,128)S(1)} %reduce_sum.86), channel_id=1, source_target_pairs={{0,256},{64,320},{128,384},{192,448},{256,0},{320,64},{384,128},{4... | collective-permute-start | bytes 294920 | tf_op jit(solution)/shard_map/ppermute | solution.py:85
  178.5 2.4 all-to-all-done.7
  181.0 0.1 multiply_divide_fusion
  181.1 0.1 select_reduce_fusion
  181.2 0.1 dynamic-slice.3
  181.3 0.1 broadcast_multiply_fusion
  181.4 0.6 fusion.17
  182.2 1.1 pad_maximum_fusion.2
  183.3 0.4 collective-permute-done.1
  183.8 0.8 broadcast_in_dim.32
  184.6 5.6 %all-to-all-start.8 = ((f32[4,32,768]{2,1,0:T(8,128)}), f32[4,32,768]{2,1,0:T(8,128)S(1)}, u32[]{:S(2)}, u32[]{:S(2)}) async-start(f32[4,32,768]{2,1,0:T(8,128)} %broadcast_in_dim.32), calls=%async_computation.8 | async-start | bytes 786432 | tf_op jit(solution)/shard_map/all_to_all | solution.py:77
  190.2 0.7 reduce-scatter.2.cloned.1.call-update
  190.9 8.2 %all-to-all-done.8 = f32[4,32,768]{2,1,0:T(8,128)S(1)} async-done(((f32[4,32,768]{2,1,0:T(8,128)}), f32[4,32,768]{2,1,0:T(8,128)S(1)}, u32[]{:S(2)}, u32[]{:S(2)}) %all-to-all-start.8) | async-done | bytes 393248 | tf_op jit(solution)/shard_map/all_to_all | solution.py:77
  199.1 1.3 broadcast_in_dim.34
  200.4 4.4 %all-to-all-start.9 = ((f32[4,128,768]{2,1,0:T(8,128)}), f32[4,128,768]{2,1,0:T(8,128)S(1)}, u32[]{:S(2)}, u32[]{:S(2)}) async-start(f32[4,128,768]{2,1,0:T(8,128)} %broadcast_in_dim.34), calls=%async_computation.9 | async-start | bytes 3145728 | tf_op jit(solution)/shard_map/all_to_all | solution.py:77
  204.8 13.7 %all-to-all-done.9 = f32[4,128,768]{2,1,0:T(8,128)S(1)} async-done(((f32[4,128,768]{2,1,0:T(8,128)}), f32[4,128,768]{2,1,0:T(8,128)S(1)}, u32[]{:S(2)}, u32[]{:S(2)}) %all-to-all-start.9) | async-done | bytes 1572896 | tf_op jit(solution)/shard_map/all_to_all | solution.py:77
  218.5 0.6 fusion.18
  219.2 26.6 %reduce-scatter.2.cloned.1.call-done = f32[96,384]{1,0:T(8,128)} async-done(((f32[768,384]{1,0:T(8,128)}), f32[96,384]{1,0:T(8,128)}) %reduce-scatter.2.cloned.1.call-update) | async-done | bytes 147472 | tf_op jit(solution)/shard_map/reduce_scatter | solution.py:107
  245.8 1.8 multiply_add_fusion.1
  247.6 4.7 %collective-permute-start.2 = (f32[48,768]{1,0:T(8,128)S(1)}, f32[48,768]{1,0:T(8,128)S(1)}, u32[]{:S(2)}, u32[]{:S(2)}) collective-permute-start(f32[48,768]{1,0:T(8,128)S(1)} %get-tuple-element.51), channel_id=1, source_target_pairs={{0,4},{1,5},{2,6},{3,7},{4,0},{5,1},{6,2},{7,3},{8,12},{9,13},{10,... | collective-permute-start | bytes 442376 | tf_op jit(solution)/shard_map/ppermute | solution.py:143
  252.3 0.6 multiply_reduce_fusion.1
  253.6 10.4 %collective-permute-done.2 = f32[48,768]{1,0:T(8,128)S(1)} collective-permute-done((f32[48,768]{1,0:T(8,128)S(1)}, f32[48,768]{1,0:T(8,128)S(1)}, u32[]{:S(2)}, u32[]{:S(2)}) %collective-permute-start.2) | collective-permute-done | bytes 147488 | tf_op jit(solution)/shard_map/ppermute | solution.py:143
  264.0 0.8 multiply_add_fusion.2
  264.8 0.7 broadcast_in_dim.35
  265.5 6.6 %all-to-all-start.10 = ((f32[8,8,768]{2,1,0:T(8,128)}), f32[8,8,768]{2,1,0:T(8,128)S(1)}, u32[]{:S(2)}, u32[]{:S(2)}) async-start(f32[8,8,768]{2,1,0:T(8,128)} %broadcast_in_dim.35), calls=%async_computation.11 | async-start | bytes 393216 | tf_op jit(solution)/shard_map/all_to_all | solution.py:77
  272.1 50.3 %all-gather.2 = f32[320,768]{1,0:T(8,128)S(1)} all-gather(f32[40,768]{1,0:T(8,128)S(1)} %slice.88), channel_id=4, replica_groups={{0,2,4,6,7,5,3,1},{8,10,12,14,15,13,11,9},{16,18,20,22,23,21,19,17},{24..., dimensions={0}, use_global_device_ids=true | all-gather | bytes 1105920 | tf_op jit(solution)/shard_map/all_gather | solution.py:119
  322.6 1.1 pad_maximum_fusion.3
  323.7 1.3 fusion.11
  325.2 1.1 copy.69
  (61 shorter events, 1.4 us)
Async XLA Ops:
  7.2 59.4 %all-gather.10.cloned.1.call-start = ((), (), s32[]{:S(2)}) async-start(), calls=%async_computation.14 | async-start | bytes 1327104 | tf_op jit(solution)/shard_map/all_gather | solution.py:94
  23.9 13.1 %all-to-all-start.1 = ((f32[4,128,96]{1,2,0:T(8,128)}), f32[4,128,96]{1,2,0:T(8,128)S(1)}, u32[]{:S(2)}, u32[]{:S(2)}) async-start(f32[4,128,96]{1,2,0:T(8,128)} %bitcast.4), calls=%async_computation.1 | async-start | bytes 393216 | tf_op jit(solution)/shard_map/all_to_all | solution.py:128
  27.3 94.8 %all-gather.8.cloned.1.call-start = ((), (), s32[]{:S(2)}) async-start(), calls=%async_computation.13 | async-start | bytes 1327104 | tf_op jit(solution)/shard_map/all_gather | solution.py:94
  79.2 17.7 %collective-permute-start = (f32[32,768]{1,0:T(8,128)S(1)}, f32[32,768]{1,0:T(8,128)S(1)}, u32[]{:S(2)}, u32[]{:S(2)}) collective-permute-start(f32[32,768]{1,0:T(8,128)S(1)} %reduce_sum.81), channel_id=1, source_target_pairs={{0,256},{64,320},{128,384},{192,448},{256,0},{320,64},{384,128},{4... | collective-permute-start | bytes 294920 | tf_op jit(solution)/shard_map/ppermute | solution.py:85
  97.7 24.4 %all-to-all-start.3 = ((f32[4,32,768]{2,1,0:T(8,128)}), f32[4,32,768]{2,1,0:T(8,128)S(1)}, u32[]{:S(2)}, u32[]{:S(2)}) async-start(f32[4,32,768]{2,1,0:T(8,128)} %broadcast_in_dim.26), calls=%async_computation.3 | async-start | bytes 786432 | tf_op jit(solution)/shard_map/all_to_all | solution.py:77
  123.6 9.6 %copy-start.8 = (f32[16,384]{1,0:T(8,128)S(1)}, f32[16,384]{1,0:T(8,128)}, u32[]{:S(2)}) copy-start(f32[16,384]{1,0:T(8,128)} %param.15) | copy-start | bytes 73732
  133.9 10.1 %all-to-all-start.5 = ((f32[8,16,384]{2,1,0:T(8,128)}), f32[8,16,384]{2,1,0:T(8,128)S(1)}, u32[]{:S(2)}, u32[]{:S(2)}) async-start(f32[8,16,384]{2,1,0:T(8,128)} %broadcast_in_dim.27), calls=%async_computation.5 | async-start | bytes 393216 | tf_op jit(solution)/shard_map/all_to_all | solution.py:77
  145.4 35.6 %copy-start.9 = (s32[16]{0:T(128)S(1)}, s32[16]{0:T(128)}, u32[]{:S(2)}) copy-start(s32[16]{0:T(128)} %param.17) | copy-start | bytes 196
  145.4 35.6 %copy-start.10 = (f32[16]{0:T(128)S(1)}, f32[16]{0:T(128)}, u32[]{:S(2)}) copy-start(f32[16]{0:T(128)} %param.19) | copy-start | bytes 196
  145.4 35.6 %copy-start.11 = (f32[16]{0:T(128)S(1)}, f32[16]{0:T(128)}, u32[]{:S(2)}) copy-start(f32[16]{0:T(128)} %param.18) | copy-start | bytes 196
  145.6 11.5 %all-to-all-start.6 = ((f32[4,32,768]{2,1,0:T(8,128)}), f32[4,32,768]{2,1,0:T(8,128)S(1)}, u32[]{:S(2)}, u32[]{:S(2)}) async-start(f32[4,32,768]{2,1,0:T(8,128)} %fusion.16), calls=%async_computation.6 | async-start | bytes 786432 | tf_op jit(solution)/shard_map/all_to_all | solution.py:72
  157.7 23.2 %all-to-all-start.7 = ((f32[64,1,128]{2,1,0:T(1,128)}), f32[64,1,128]{2,1,0:T(1,128)S(1)}, u32[]{:S(2)}, u32[]{:S(2)}) async-start(f32[64,1,128]{2,1,0:T(1,128)} %broadcast_in_dim.31), calls=%async_computation.7 | async-start | bytes 65536 | tf_op jit(solution)/shard_map/all_to_all | solution.py:77
  166.2 17.5 %collective-permute-start.1 = (f32[32,768]{1,0:T(8,128)S(1)}, f32[32,768]{1,0:T(8,128)S(1)}, u32[]{:S(2)}, u32[]{:S(2)}) collective-permute-start(f32[32,768]{1,0:T(8,128)S(1)} %reduce_sum.86), channel_id=1, source_target_pairs={{0,256},{64,320},{128,384},{192,448},{256,0},{320,64},{384,128},{4... | collective-permute-start | bytes 294920 | tf_op jit(solution)/shard_map/ppermute | solution.py:85
  184.6 14.5 %all-to-all-start.8 = ((f32[4,32,768]{2,1,0:T(8,128)}), f32[4,32,768]{2,1,0:T(8,128)S(1)}, u32[]{:S(2)}, u32[]{:S(2)}) async-start(f32[4,32,768]{2,1,0:T(8,128)} %broadcast_in_dim.32), calls=%async_computation.8 | async-start | bytes 786432 | tf_op jit(solution)/shard_map/all_to_all | solution.py:77
  190.2 55.5 %reduce-scatter.2.cloned.1.call-start = ((), (), s32[]{:S(2)}) async-start(), calls=%async_computation.12 | async-start | bytes 1327104 | tf_op jit(solution)/shard_map/reduce_scatter | solution.py:107
  200.4 18.1 %all-to-all-start.9 = ((f32[4,128,768]{2,1,0:T(8,128)}), f32[4,128,768]{2,1,0:T(8,128)S(1)}, u32[]{:S(2)}, u32[]{:S(2)}) async-start(f32[4,128,768]{2,1,0:T(8,128)} %broadcast_in_dim.34), calls=%async_computation.9 | async-start | bytes 3145728 | tf_op jit(solution)/shard_map/all_to_all | solution.py:77
  204.8 119.0 %all-gather.12.cloned.1.call-start = ((), (), s32[]{:S(2)}) async-start(), calls=%async_computation.15 | async-start | bytes 1327104 | tf_op jit(solution)/shard_map/all_gather | solution.py:94
  218.5 27.3 %copy-start.1 = (f32[96,384]{1,0:T(8,128)S(1)}, f32[96,384]{1,0:T(8,128)}, u32[]{:S(2)}) copy-start(f32[96,384]{1,0:T(8,128)} %param.21) | copy-start | bytes 442372
  218.5 27.3 %copy-start.5 = (f32[96,384]{1,0:T(8,128)S(1)}, f32[96,384]{1,0:T(8,128)}, u32[]{:S(2)}) copy-start(f32[96,384]{1,0:T(8,128)} %param.27) | copy-start | bytes 442372
  218.5 27.3 %copy-start.6 = (f32[96,384]{1,0:T(8,128)S(1)}, f32[96,384]{1,0:T(8,128)}, u32[]{:S(2)}) copy-start(f32[96,384]{1,0:T(8,128)} %param.23) | copy-start | bytes 442372
  218.5 27.3 %copy-start.7 = (f32[96,384]{1,0:T(8,128)S(1)}, f32[96,384]{1,0:T(8,128)}, u32[]{:S(2)}) copy-start(f32[96,384]{1,0:T(8,128)} %param.25) | copy-start | bytes 442372
  219.1 44.9 %copy-start = (f32[48,768]{1,0:T(8,128)S(1)}, f32[48,768]{1,0:T(8,128)}, u32[]{:S(2)}) copy-start(f32[48,768]{1,0:T(8,128)} %param.20) | copy-start | bytes 442372
  219.1 44.9 %copy-start.2 = (f32[48,768]{1,0:T(8,128)S(1)}, f32[48,768]{1,0:T(8,128)}, u32[]{:S(2)}) copy-start(f32[48,768]{1,0:T(8,128)} %param.26) | copy-start | bytes 442372
  219.1 44.9 %copy-start.3 = (f32[48,768]{1,0:T(8,128)S(1)}, f32[48,768]{1,0:T(8,128)}, u32[]{:S(2)}) copy-start(f32[48,768]{1,0:T(8,128)} %param.22) | copy-start | bytes 442372
  219.1 44.9 %copy-start.4 = (f32[48,768]{1,0:T(8,128)S(1)}, f32[48,768]{1,0:T(8,128)}, u32[]{:S(2)}) copy-start(f32[48,768]{1,0:T(8,128)} %param.24) | copy-start | bytes 442372
  247.6 16.4 %collective-permute-start.2 = (f32[48,768]{1,0:T(8,128)S(1)}, f32[48,768]{1,0:T(8,128)S(1)}, u32[]{:S(2)}, u32[]{:S(2)}) collective-permute-start(f32[48,768]{1,0:T(8,128)S(1)} %get-tuple-element.51), channel_id=1, source_target_pairs={{0,4},{1,5},{2,6},{3,7},{4,0},{5,1},{6,2},{7,3},{8,12},{9,13},{10,... | collective-permute-start | bytes 442376 | tf_op jit(solution)/shard_map/ppermute | solution.py:143
  265.5 57.1 %all-to-all-start.10 = ((f32[8,8,768]{2,1,0:T(8,128)}), f32[8,8,768]{2,1,0:T(8,128)S(1)}, u32[]{:S(2)}, u32[]{:S(2)}) async-start(f32[8,8,768]{2,1,0:T(8,128)} %broadcast_in_dim.35), calls=%async_computation.11 | async-start | bytes 393216 | tf_op jit(solution)/shard_map/all_to_all | solution.py:77
Sparse Core Ops, SparseCore 0:
  10.1 56.4 all-gather.9
  68.6 53.4 all-gather.7
  194.4 51.2 reduce-scatter.1
  247.7 60.4 all-gather.11

commit v2 on v1

--- a/solution.py
+++ b/solution.py
@@ -123,10 +123,19 @@
     return every.reshape(8 * shard.shape[0], shard.shape[1])
 
 
-def quad_columns(rows):
-    blocks = jnp.transpose(rows.reshape(128, 2, 4, 48), (2, 0, 1, 3)).reshape(4, 128, 96)
-    every = lax.all_to_all(blocks, "tok", 0, 0, axis_index_groups=QUADS)
-    return jnp.transpose(every.reshape(4, 4, 32, 96), (1, 0, 2, 3)).reshape(512, 96)
+def half_pair(shard):
+    upper = lax.axis_index("tok") >= 4
+    other = lax.ppermute(shard, "tok", FAR_HALF)
+    return jnp.concatenate([jnp.where(upper, other, shard), jnp.where(upper, shard, other)])
+
+
+def quad_columns(tokens, sample_ids):
+    blocks = jnp.transpose(tokens.reshape(16, 2, 4, 48), (2, 0, 1, 3)).reshape(4, 16, 96)
+    id_lanes = jnp.broadcast_to(sample_ids.astype(jnp.float32)[None, :, None], (4, 16, 32))
+    blocks = jnp.concatenate([blocks, id_lanes], axis=2)
+    near = lax.all_to_all(blocks, "tok", 0, 0, axis_index_groups=QUADS)
+    every = spread(near, "hid", 8).reshape(4, 2, 4, 16, 128)
+    return jnp.transpose(every, (0, 2, 1, 3, 4)).reshape(512, 128)
 
 
 def quad_rows(block):
@@ -160,17 +169,18 @@
     e_in,
     e_out,
 ):
-    w_in_block, _ = queue_gather(w_in)
-    id_lanes = jnp.broadcast_to(sample_ids.astype(jnp.float32)[:, None], (16, 128))
-    rows_and_ids = spread(jnp.concatenate([tokens, id_lanes], axis=1), "hid", 8)
-    rows_and_ids = rows_and_ids.reshape(128, 512)
-    all_rows = rows_and_ids[:, :384]
-    all_rows, columns = lax.optimization_barrier((all_rows, quad_columns(all_rows)))
-    all_ids = rows_and_ids[:, 384].astype(jnp.int32)
+    w_in_pair = half_pair(w_in)
+    table = quad_columns(tokens, sample_ids)
+    columns = table[:, :96]
+    quad_ids = table[:, 96].reshape(4, 4, 32)
+    own_quad = lax.rem(lax.axis_index("tok"), 4)
+    all_ids = lax.dynamic_index_in_dim(quad_ids, own_quad, axis=1, keepdims=False)
+    all_ids = all_ids.reshape(-1).astype(jnp.int32)
     onehot = (all_ids[:, None] == jnp.arange(SAMPLES, dtype=jnp.int32)[None, :]).astype(
         jnp.float32
     )
-    hidden = far_sum(y_sum(product(all_rows, w_in_block, 1, 0)))
+    quad_part = y_sum(product(columns, w_in_pair, 1, 0))
+    hidden = far_sum(scatter_sum(quad_part, "tok", 4, QUADS))
     active_rows, slope_rows = gelu_parts(hidden)
     active = y_gather(active_rows)
     w_out_block, active = queue_gather(w_out, active)

time: 336 us -> 346 us (1.030)
  waiting for transfers between devices: 145 us -> 109 us
  starting transfers between devices: 65.9 us -> 94 us
  blocking collectives: 83.7 us -> 101 us
    all_gather x3 -> x2, waiting for transfers between devices: 50.3 us -> 0.02 us  [queue_gather(): lax.all_gather(shard, 'tok', axis=0, tiled=False, axis_index_groups=[list...]
    all_to_all x1 -> x2, waiting for transfers between devices: 7.83 us -> 27.5 us  [scatter_sum(): lax.all_to_all(blocks, axis, 0, 0, axis_index_groups=groups)]
    all_to_all x2, blocking collectives: 19.7 us -> 31.8 us  [scatter_sum(): lax.all_to_all(blocks, axis, 0, 0, axis_index_groups=groups)]
    ppermute x0 -> x1, starting transfers between devices: none -> 9.23 us  [half_pair(): other = lax.ppermute(shard, 'tok', FAR_HALF)]
    all_to_all x6, starting transfers between devices: 33.7 us -> 40.2 us  [spread(): return lax.all_to_all(copies, axis, 0, 0, axis_index_groups=groups)]
    ppermute x2, starting transfers between devices: 20.6 us -> 25.6 us  [far_sum(): return quarter + lax.ppermute(quarter, 'inp', FAR_HALF)]
    all_to_all x1 -> x2, starting transfers between devices: 3.46 us -> 8.05 us  [scatter_sum(): lax.all_to_all(blocks, axis, 0, 0, axis_index_groups=groups)]
    all_to_all x1, blocking collectives: 13.7 us -> 17.9 us  [spread(): return lax.all_to_all(copies, axis, 0, 0, axis_index_groups=groups)]
  transfers between devices with their start and end apart: 15 -> 16, of which waited for: 12 -> 12; matrix products, arithmetic and copies ran while one was open for 4% -> 3% of each run, Pallas kernels for 0% -> 0%
where the time goes in v2:
time: 346 us; the launch traced here: 343 us
  waiting for transfers between devices  109 us (32%)
  blocking collectives  101 us (29%)
  starting transfers between devices  94 us (27%)
  between operations  15.9 us (5%)
  local copies, waits for them, and re-layouts  10.4 us (3%)
  other arithmetic  7.99 us (2%)
  matrix products  5.04 us (1%)
    all_gather x1, blocking collectives, core_gather(): lax.all_gather(shard[:split], 'tok', axis=0, tiled=False, axis_index_grou...  51.5 us
    all_to_all x6, starting transfers between devices, spread(): return lax.all_to_all(copies, axis, 0, 0, axis_index_groups=groups)  40.2 us
    all_to_all x2, blocking collectives, scatter_sum(): lax.all_to_all(blocks, axis, 0, 0, axis_index_groups=groups)  31.8 us
    reduce_scatter x1, waiting for transfers between devices, queue_scatter(): lax.psum_scatter(folded, 'tok', scatter_dimension=0, tiled=True, axis_ind...  27.7 us
    all_to_all x6, waiting for transfers between devices, spread(): return lax.all_to_all(copies, axis, 0, 0, axis_index_groups=groups)  27.5 us
    all_to_all x2, waiting for transfers between devices, scatter_sum(): lax.all_to_all(blocks, axis, 0, 0, axis_index_groups=groups)  27.5 us
    ppermute x2, starting transfers between devices, far_sum(): return quarter + lax.ppermute(quarter, 'inp', FAR_HALF)  25.6 us
    all_to_all x1, blocking collectives, spread(): return lax.all_to_all(copies, axis, 0, 0, axis_index_groups=groups)  17.9 us
  transfers between devices with their start and end apart: 16, of which 12 were waited for; matrix products, arithmetic and copies ran while one was open for 3% of the time, Pallas kernels for 0%

profile of v2, /device:TPU:6, one launch (start us, length us, event | category | flops | bytes accessed | tf_op | source)
XLA Modules:
  0.0 343.0 jit_solution(6744207091179807880)
XLA Ops:
  7.2 9.2 %collective-permute-start = (f32[48,768]{1,0:T(8,128)}, f32[48,768]{1,0:T(8,128)S(1)}, u32[]{:S(2)}, u32[]{:S(2)}) collective-permute-start(f32[48,768]{1,0:T(8,128)} %param.20), channel_id=1, source_target_pairs={{0,4},{1,5},{2,6},{3,7},{4,0},{5,1},{6,2},{7,3},{8,12},{9,13},{10,... | collective-permute-start | bytes 442376 | tf_op jit(solution)/shard_map/ppermute | solution.py:128
  16.4 0.8 reshape.90
  17.3 0.1 reshape.91
  17.4 0.7 convert_element_type.20
  18.1 0.7 pad_maximum_fusion.5
  18.8 5.9 %all-to-all-start = ((f32[4,16,128]{2,1,0:T(8,128)}), f32[4,16,128]{2,1,0:T(8,128)S(1)}, u32[]{:S(2)}, u32[]{:S(2)}) async-start(f32[4,16,128]{2,1,0:T(8,128)} %pad_maximum_fusion.5), calls=%async_computation | async-start | bytes 65536 | tf_op jit(solution)/shard_map/all_to_all | solution.py:136
  24.7 5.9 %all-to-all-done = f32[4,16,128]{2,1,0:T(8,128)S(1)} async-done(((f32[4,16,128]{2,1,0:T(8,128)}), f32[4,16,128]{2,1,0:T(8,128)S(1)}, u32[]{:S(2)}, u32[]{:S(2)}) %all-to-all-start) | async-done | bytes 32800 | tf_op jit(solution)/shard_map/all_to_all | solution.py:136
  30.6 0.7 broadcast_in_dim.25
  31.4 4.8 %all-to-all-start.1 = ((f32[8,4,16,128]{3,2,1,0:T(8,128)}), f32[8,4,16,128]{3,2,1,0:T(8,128)S(1)}, u32[]{:S(2)}, u32[]{:S(2)}) async-start(f32[8,4,16,128]{3,2,1,0:T(8,128)} %broadcast_in_dim.25), calls=%async_computation.1 | async-start | bytes 524288 | tf_op jit(solution)/shard_map/all_to_all | solution.py:77
  36.2 5.4 %all-to-all-done.1 = f32[8,4,16,128]{3,2,1,0:T(8,128)S(1)} async-done(((f32[8,4,16,128]{3,2,1,0:T(8,128)}), f32[8,4,16,128]{3,2,1,0:T(8,128)S(1)}, u32[]{:S(2)}, u32[]{:S(2)}) %all-to-all-start.1) | async-done | bytes 262176 | tf_op jit(solution)/shard_map/all_to_all | solution.py:77
  41.6 1.9 fusion
  43.5 4.5 %all-to-all-start.2 = ((f32[4,128,768]{2,1,0:T(8,128)}), f32[4,128,768]{2,1,0:T(8,128)S(1)}, u32[]{:S(2)}, u32[]{:S(2)}) async-start(f32[4,128,768]{2,1,0:T(8,128)} %bitcast.5), calls=%async_computation.2 | async-start | bytes 3145728 | tf_op jit(solution)/shard_map/all_to_all | solution.py:72
  48.0 0.7 all-gather.6.cloned.1.call-update
  48.7 19.6 %all-to-all-done.2 = f32[4,128,768]{2,1,0:T(8,128)S(1)} async-done(((f32[4,128,768]{2,1,0:T(8,128)}), f32[4,128,768]{2,1,0:T(8,128)S(1)}, u32[]{:S(2)}, u32[]{:S(2)}) %all-to-all-start.2) | async-done | bytes 1572896 | tf_op jit(solution)/shard_map/all_to_all | solution.py:72
  68.4 0.1 reduce_sum.90
  68.5 22.8 %all_to_all.60 = f32[4,32,768]{2,1,0:T(8,128)S(1)} all-to-all(f32[4,32,768]{2,1,0:T(8,128)S(1)} %bitcast.78), channel_id=1, replica_groups={{0,1,2,3},{4,5,6,7},{8,9,10,11},{12,13,14,15},{16,17,18,19},{20,21,22,2..., dimensions={0} | all-to-all | bytes 786432 | tf_op jit(solution)/shard_map/all_to_all | solution.py:72
  91.3 13.3 %collective-permute-start.1 = (f32[32,768]{1,0:T(8,128)S(1)}, f32[32,768]{1,0:T(8,128)S(1)}, u32[]{:S(2)}, u32[]{:S(2)}) collective-permute-start(f32[32,768]{1,0:T(8,128)S(1)} %reduce_sum.91), channel_id=1, source_target_pairs={{0,256},{64,320},{128,384},{192,448},{256,0},{320,64},{384,128},{4... | collective-permute-start | bytes 294920 | tf_op jit(solution)/shard_map/ppermute | solution.py:85
  104.6 7.1 %collective-permute-done.1 = f32[32,768]{1,0:T(8,128)S(1)} collective-permute-done((f32[32,768]{1,0:T(8,128)S(1)}, f32[32,768]{1,0:T(8,128)S(1)}, u32[]{:S(2)}, u32[]{:S(2)}) %collective-permute-start.1) | collective-permute-done | bytes 98336 | tf_op jit(solution)/shard_map/ppermute | solution.py:85
  111.8 0.8 broadcast_in_dim.26
  112.6 3.5 %all-to-all-start.4 = ((f32[4,32,768]{2,1,0:T(8,128)}), f32[4,32,768]{2,1,0:T(8,128)S(1)}, u32[]{:S(2)}, u32[]{:S(2)}) async-start(f32[4,32,768]{2,1,0:T(8,128)} %broadcast_in_dim.26), calls=%async_computation.4 | async-start | bytes 786432 | tf_op jit(solution)/shard_map/all_to_all | solution.py:77
  116.1 7.3 %all-to-all-done.4 = f32[4,32,768]{2,1,0:T(8,128)S(1)} async-done(((f32[4,32,768]{2,1,0:T(8,128)}), f32[4,32,768]{2,1,0:T(8,128)S(1)}, u32[]{:S(2)}, u32[]{:S(2)}) %all-to-all-start.4) | async-done | bytes 393248 | tf_op jit(solution)/shard_map/all_to_all | solution.py:77
  123.4 1.3 slice_bitcast_fusion.2
  124.9 0.5 fusion.20
  125.4 9.0 %all_to_all.61 = f32[8,16,384]{2,1,0:T(8,128)S(1)} all-to-all(f32[8,16,384]{2,1,0:T(8,128)S(1)} %fusion.20), channel_id=1, replica_groups=mesh['inp'=8,'hid'=8,'tok'=8] {'hid'}, dimensions={0} | all-to-all | bytes 393216 | tf_op jit(solution)/shard_map/all_to_all | solution.py:72
  134.5 0.7 broadcast_in_dim.27
  135.2 5.4 %all-to-all-start.6 = ((f32[8,16,384]{2,1,0:T(8,128)}), f32[8,16,384]{2,1,0:T(8,128)S(1)}, u32[]{:S(2)}, u32[]{:S(2)}) async-start(f32[8,16,384]{2,1,0:T(8,128)} %broadcast_in_dim.27), calls=%async_computation.6 | async-start | bytes 393216 | tf_op jit(solution)/shard_map/all_to_all | solution.py:77
  140.6 0.2 slice_reduce_fusion
  140.9 0.1 convert_element_type.22
  141.0 4.3 %all-to-all-done.6 = f32[8,16,384]{2,1,0:T(8,128)S(1)} async-done(((f32[8,16,384]{2,1,0:T(8,128)}), f32[8,16,384]{2,1,0:T(8,128)S(1)}, u32[]{:S(2)}, u32[]{:S(2)}) %all-to-all-start.6) | async-done | bytes 196640 | tf_op jit(solution)/shard_map/all_to_all | solution.py:77
  145.3 0.1 multiply_reduce_fusion
  145.5 1.4 fusion.21
  146.8 3.6 %all-to-all-start.7 = ((f32[4,32,768]{2,1,0:T(8,128)}), f32[4,32,768]{2,1,0:T(8,128)S(1)}, u32[]{:S(2)}, u32[]{:S(2)}) async-start(f32[4,32,768]{2,1,0:T(8,128)} %fusion.21), calls=%async_computation.7 | async-start | bytes 786432 | tf_op jit(solution)/shard_map/all_to_all | solution.py:72
  150.4 0.1 select_reduce_fusion.1
  150.7 7.8 %all-to-all-done.7 = f32[4,32,768]{2,1,0:T(8,128)S(1)} async-done(((f32[4,32,768]{2,1,0:T(8,128)}), f32[4,32,768]{2,1,0:T(8,128)S(1)}, u32[]{:S(2)}, u32[]{:S(2)}) %all-to-all-start.7) | async-done | bytes 393248 | tf_op jit(solution)/shard_map/all_to_all | solution.py:72
  158.5 0.6 broadcast_in_dim.31
  159.1 15.3 %all-to-all-start.8 = ((f32[64,1,128]{2,1,0:T(1,128)}), f32[64,1,128]{2,1,0:T(1,128)S(1)}, u32[]{:S(2)}, u32[]{:S(2)}) async-start(f32[64,1,128]{2,1,0:T(1,128)} %broadcast_in_dim.31), calls=%async_computation.8 | async-start | bytes 65536 | tf_op jit(solution)/shard_map/all_to_all | solution.py:77
  174.5 0.2 copy.52
  174.7 12.3 %collective-permute-start.2 = (f32[32,768]{1,0:T(8,128)S(1)}, f32[32,768]{1,0:T(8,128)S(1)}, u32[]{:S(2)}, u32[]{:S(2)}) collective-permute-start(f32[32,768]{1,0:T(8,128)S(1)} %reduce_sum.96), channel_id=1, source_target_pairs={{0,256},{64,320},{128,384},{192,448},{256,0},{320,64},{384,128},{4... | collective-permute-start | bytes 294920 | tf_op jit(solution)/shard_map/ppermute | solution.py:85
  187.0 2.4 all-to-all-done.8
  189.4 0.1 multiply_divide_fusion
  189.5 0.1 select_reduce_fusion
  189.8 0.1 broadcast_multiply_fusion
  189.9 0.6 fusion.22
  190.6 1.1 pad_maximum_fusion.1
  191.7 0.4 collective-permute-done.2
  192.3 0.8 broadcast_in_dim.32
  193.0 5.6 %all-to-all-start.9 = ((f32[4,32,768]{2,1,0:T(8,128)}), f32[4,32,768]{2,1,0:T(8,128)S(1)}, u32[]{:S(2)}, u32[]{:S(2)}) async-start(f32[4,32,768]{2,1,0:T(8,128)} %broadcast_in_dim.32), calls=%async_computation.9 | async-start | bytes 786432 | tf_op jit(solution)/shard_map/all_to_all | solution.py:77
  198.7 0.7 reduce-scatter.2.cloned.1.call-update
  199.5 8.1 %all-to-all-done.9 = f32[4,32,768]{2,1,0:T(8,128)S(1)} async-done(((f32[4,32,768]{2,1,0:T(8,128)}), f32[4,32,768]{2,1,0:T(8,128)S(1)}, u32[]{:S(2)}, u32[]{:S(2)}) %all-to-all-start.9) | async-done | bytes 393248 | tf_op jit(solution)/shard_map/all_to_all | solution.py:77
  207.6 0.1 broadcast_in_dim.34
  207.7 17.9 %all_to_all.62 = f32[4,128,768]{2,1,0:T(8,128)S(1)} all-to-all(f32[4,128,768]{2,1,0:T(8,128)S(1)} %broadcast_in_dim.34), channel_id=1, replica_groups={{0,64,128,192},{256,320,384,448},{1,65,129,193},{257,321,385,449},{2,66..., dimensions={0} | all-to-all | bytes 3145728 | tf_op jit(solution)/shard_map/all_to_all | solution.py:77
  225.6 0.6 fusion.4
  226.2 27.7 %reduce-scatter.2.cloned.1.call-done = f32[96,384]{1,0:T(8,128)} async-done(((f32[768,384]{1,0:T(8,128)}), f32[96,384]{1,0:T(8,128)}) %reduce-scatter.2.cloned.1.call-update) | async-done | bytes 147472 | tf_op jit(solution)/shard_map/reduce_scatter | solution.py:107
  253.9 1.8 multiply_add_fusion.1
  255.7 5.0 %collective-permute-start.3 = (f32[48,768]{1,0:T(8,128)S(1)}, f32[48,768]{1,0:T(8,128)S(1)}, u32[]{:S(2)}, u32[]{:S(2)}) collective-permute-start(f32[48,768]{1,0:T(8,128)S(1)} %get-tuple-element.45), channel_id=1, source_target_pairs={{0,4},{1,5},{2,6},{3,7},{4,0},{5,1},{6,2},{7,3},{8,12},{9,13},{10,... | collective-permute-start | bytes 442376 | tf_op jit(solution)/shard_map/ppermute | solution.py:152
  260.7 0.6 multiply_reduce_fusion.1
  262.0 10.9 %collective-permute-done.3 = f32[48,768]{1,0:T(8,128)S(1)} collective-permute-done((f32[48,768]{1,0:T(8,128)S(1)}, f32[48,768]{1,0:T(8,128)S(1)}, u32[]{:S(2)}, u32[]{:S(2)}) %collective-permute-start.3) | collective-permute-done | bytes 147488 | tf_op jit(solution)/shard_map/ppermute | solution.py:152
  272.9 0.8 multiply_add_fusion.2
  273.8 0.7 broadcast_in_dim.35
  274.4 5.6 %all-to-all-start.11 = ((f32[8,8,768]{2,1,0:T(8,128)}), f32[8,8,768]{2,1,0:T(8,128)S(1)}, u32[]{:S(2)}, u32[]{:S(2)}) async-start(f32[8,8,768]{2,1,0:T(8,128)} %broadcast_in_dim.35), calls=%async_computation.12 | async-start | bytes 393216 | tf_op jit(solution)/shard_map/all_to_all | solution.py:77
  280.0 51.5 %all-gather.1 = f32[320,768]{1,0:T(8,128)S(1)} all-gather(f32[40,768]{1,0:T(8,128)S(1)} %slice.76), channel_id=3, replica_groups={{0,2,4,6,7,5,3,1},{8,10,12,14,15,13,11,9},{16,18,20,22,23,21,19,17},{24..., dimensions={0}, use_global_device_ids=true | all-gather | bytes 1105920 | tf_op jit(solution)/shard_map/all_gather | solution.py:119
  331.7 1.1 pad_maximum_fusion.2
  332.8 1.3 fusion.18
  334.3 1.1 copy.55
  (63 shorter events, 1.5 us)
Async XLA Ops:
  7.2 29.0 %copy-start = (f32[48,768]{1,0:T(8,128)S(1)}, f32[48,768]{1,0:T(8,128)}, u32[]{:S(2)}) copy-start(f32[48,768]{1,0:T(8,128)} %param.20) | copy-start | bytes 442372
  7.2 29.0 %collective-permute-start = (f32[48,768]{1,0:T(8,128)}, f32[48,768]{1,0:T(8,128)S(1)}, u32[]{:S(2)}, u32[]{:S(2)}) collective-permute-start(f32[48,768]{1,0:T(8,128)} %param.20), channel_id=1, source_target_pairs={{0,4},{1,5},{2,6},{3,7},{4,0},{5,1},{6,2},{7,3},{8,12},{9,13},{10,... | collective-permute-start | bytes 442376 | tf_op jit(solution)/shard_map/ppermute | solution.py:128
  18.8 11.8 %all-to-all-start = ((f32[4,16,128]{2,1,0:T(8,128)}), f32[4,16,128]{2,1,0:T(8,128)S(1)}, u32[]{:S(2)}, u32[]{:S(2)}) async-start(f32[4,16,128]{2,1,0:T(8,128)} %pad_maximum_fusion.5), calls=%async_computation | async-start | bytes 65536 | tf_op jit(solution)/shard_map/all_to_all | solution.py:136
  31.4 10.2 %all-to-all-start.1 = ((f32[8,4,16,128]{3,2,1,0:T(8,128)}), f32[8,4,16,128]{3,2,1,0:T(8,128)S(1)}, u32[]{:S(2)}, u32[]{:S(2)}) async-start(f32[8,4,16,128]{3,2,1,0:T(8,128)} %broadcast_in_dim.25), calls=%async_computation.1 | async-start | bytes 524288 | tf_op jit(solution)/shard_map/all_to_all | solution.py:77
  43.5 24.8 %all-to-all-start.2 = ((f32[4,128,768]{2,1,0:T(8,128)}), f32[4,128,768]{2,1,0:T(8,128)S(1)}, u32[]{:S(2)}, u32[]{:S(2)}) async-start(f32[4,128,768]{2,1,0:T(8,128)} %bitcast.5), calls=%async_computation.2 | async-start | bytes 3145728 | tf_op jit(solution)/shard_map/all_to_all | solution.py:72
  48.0 68.1 %all-gather.6.cloned.1.call-start = ((), (), s32[]{:S(2)}) async-start(), calls=%async_computation.14 | async-start | bytes 1327104 | tf_op jit(solution)/shard_map/all_gather | solution.py:94
  91.3 20.5 %collective-permute-start.1 = (f32[32,768]{1,0:T(8,128)S(1)}, f32[32,768]{1,0:T(8,128)S(1)}, u32[]{:S(2)}, u32[]{:S(2)}) collective-permute-start(f32[32,768]{1,0:T(8,128)S(1)} %reduce_sum.91), channel_id=1, source_target_pairs={{0,256},{64,320},{128,384},{192,448},{256,0},{320,64},{384,128},{4... | collective-permute-start | bytes 294920 | tf_op jit(solution)/shard_map/ppermute | solution.py:85
  112.6 10.8 %all-to-all-start.4 = ((f32[4,32,768]{2,1,0:T(8,128)}), f32[4,32,768]{2,1,0:T(8,128)S(1)}, u32[]{:S(2)}, u32[]{:S(2)}) async-start(f32[4,32,768]{2,1,0:T(8,128)} %broadcast_in_dim.26), calls=%async_computation.4 | async-start | bytes 786432 | tf_op jit(solution)/shard_map/all_to_all | solution.py:77
  124.9 9.6 %copy-start.8 = (f32[16,384]{1,0:T(8,128)S(1)}, f32[16,384]{1,0:T(8,128)}, u32[]{:S(2)}) copy-start(f32[16,384]{1,0:T(8,128)} %param.15) | copy-start | bytes 73732
  135.2 10.1 %all-to-all-start.6 = ((f32[8,16,384]{2,1,0:T(8,128)}), f32[8,16,384]{2,1,0:T(8,128)S(1)}, u32[]{:S(2)}, u32[]{:S(2)}) async-start(f32[8,16,384]{2,1,0:T(8,128)} %broadcast_in_dim.27), calls=%async_computation.6 | async-start | bytes 393216 | tf_op jit(solution)/shard_map/all_to_all | solution.py:77
  146.8 42.6 %copy-start.9 = (s32[16]{0:T(128)S(1)}, s32[16]{0:T(128)}, u32[]{:S(2)}) copy-start(s32[16]{0:T(128)} %param.17) | copy-start | bytes 196
  146.8 42.6 %copy-start.10 = (f32[16]{0:T(128)S(1)}, f32[16]{0:T(128)}, u32[]{:S(2)}) copy-start(f32[16]{0:T(128)} %param.19) | copy-start | bytes 196
  146.8 42.6 %copy-start.11 = (f32[16]{0:T(128)S(1)}, f32[16]{0:T(128)}, u32[]{:S(2)}) copy-start(f32[16]{0:T(128)} %param.18) | copy-start | bytes 196
  146.8 11.6 %all-to-all-start.7 = ((f32[4,32,768]{2,1,0:T(8,128)}), f32[4,32,768]{2,1,0:T(8,128)S(1)}, u32[]{:S(2)}, u32[]{:S(2)}) async-start(f32[4,32,768]{2,1,0:T(8,128)} %fusion.21), calls=%async_computation.7 | async-start | bytes 786432 | tf_op jit(solution)/shard_map/all_to_all | solution.py:72
  159.1 30.3 %all-to-all-start.8 = ((f32[64,1,128]{2,1,0:T(1,128)}), f32[64,1,128]{2,1,0:T(1,128)S(1)}, u32[]{:S(2)}, u32[]{:S(2)}) async-start(f32[64,1,128]{2,1,0:T(1,128)} %broadcast_in_dim.31), calls=%async_computation.8 | async-start | bytes 65536 | tf_op jit(solution)/shard_map/all_to_all | solution.py:77
  174.7 17.5 %collective-permute-start.2 = (f32[32,768]{1,0:T(8,128)S(1)}, f32[32,768]{1,0:T(8,128)S(1)}, u32[]{:S(2)}, u32[]{:S(2)}) collective-permute-start(f32[32,768]{1,0:T(8,128)S(1)} %reduce_sum.96), channel_id=1, source_target_pairs={{0,256},{64,320},{128,384},{192,448},{256,0},{320,64},{384,128},{4... | collective-permute-start | bytes 294920 | tf_op jit(solution)/shard_map/ppermute | solution.py:85
  193.0 14.5 %all-to-all-start.9 = ((f32[4,32,768]{2,1,0:T(8,128)}), f32[4,32,768]{2,1,0:T(8,128)S(1)}, u32[]{:S(2)}, u32[]{:S(2)}) async-start(f32[4,32,768]{2,1,0:T(8,128)} %broadcast_in_dim.32), calls=%async_computation.9 | async-start | bytes 786432 | tf_op jit(solution)/shard_map/all_to_all | solution.py:77
  198.7 55.2 %reduce-scatter.2.cloned.1.call-start = ((), (), s32[]{:S(2)}) async-start(), calls=%async_computation.13 | async-start | bytes 1327104 | tf_op jit(solution)/shard_map/reduce_scatter | solution.py:107
  199.4 133.4 %all-gather.8.cloned.1.call-start = ((), (), s32[]{:S(2)}) async-start(), calls=%async_computation.15 | async-start | bytes 1327104 | tf_op jit(solution)/shard_map/all_gather | solution.py:94
  225.5 28.4 %copy-start.1 = (f32[96,384]{1,0:T(8,128)S(1)}, f32[96,384]{1,0:T(8,128)}, u32[]{:S(2)}) copy-start(f32[96,384]{1,0:T(8,128)} %param.21) | copy-start | bytes 442372
  225.5 28.4 %copy-start.5 = (f32[96,384]{1,0:T(8,128)S(1)}, f32[96,384]{1,0:T(8,128)}, u32[]{:S(2)}) copy-start(f32[96,384]{1,0:T(8,128)} %param.27) | copy-start | bytes 442372
  225.5 28.4 %copy-start.6 = (f32[96,384]{1,0:T(8,128)S(1)}, f32[96,384]{1,0:T(8,128)}, u32[]{:S(2)}) copy-start(f32[96,384]{1,0:T(8,128)} %param.23) | copy-start | bytes 442372
  225.5 28.4 %copy-start.7 = (f32[96,384]{1,0:T(8,128)S(1)}, f32[96,384]{1,0:T(8,128)}, u32[]{:S(2)}) copy-start(f32[96,384]{1,0:T(8,128)} %param.25) | copy-start | bytes 442372
  226.2 46.7 %copy-start.2 = (f32[48,768]{1,0:T(8,128)S(1)}, f32[48,768]{1,0:T(8,128)}, u32[]{:S(2)}) copy-start(f32[48,768]{1,0:T(8,128)} %param.26) | copy-start | bytes 442372
  226.2 46.7 %copy-start.3 = (f32[48,768]{1,0:T(8,128)S(1)}, f32[48,768]{1,0:T(8,128)}, u32[]{:S(2)}) copy-start(f32[48,768]{1,0:T(8,128)} %param.22) | copy-start | bytes 442372
  226.2 46.7 %copy-start.4 = (f32[48,768]{1,0:T(8,128)S(1)}, f32[48,768]{1,0:T(8,128)}, u32[]{:S(2)}) copy-start(f32[48,768]{1,0:T(8,128)} %param.24) | copy-start | bytes 442372
  255.7 17.2 %collective-permute-start.3 = (f32[48,768]{1,0:T(8,128)S(1)}, f32[48,768]{1,0:T(8,128)S(1)}, u32[]{:S(2)}, u32[]{:S(2)}) collective-permute-start(f32[48,768]{1,0:T(8,128)S(1)} %get-tuple-element.45), channel_id=1, source_target_pairs={{0,4},{1,5},{2,6},{3,7},{4,0},{5,1},{6,2},{7,3},{8,12},{9,13},{10,... | collective-permute-start | bytes 442376 | tf_op jit(solution)/shard_map/ppermute | solution.py:152
  274.4 57.2 %all-to-all-start.11 = ((f32[8,8,768]{2,1,0:T(8,128)}), f32[8,8,768]{2,1,0:T(8,128)S(1)}, u32[]{:S(2)}, u32[]{:S(2)}) async-start(f32[8,8,768]{2,1,0:T(8,128)} %broadcast_in_dim.35), calls=%async_computation.12 | async-start | bytes 393216 | tf_op jit(solution)/shard_map/all_to_all | solution.py:77
Sparse Core Ops, SparseCore 0:
  50.9 64.2 all-gather.5
  202.9 50.9 reduce-scatter.1
  256.0 60.7 all-gather.7

commit v3 on v2

--- a/solution.py
+++ b/solution.py
@@ -143,14 +143,12 @@
     return spread(near, "inp", 4, QUADS).reshape(512, 768)
 
 
-def half_sum(pair, partner):
+def half_sum(pair):
     upper = lax.axis_index("tok") >= 4
     rows = pair.shape[0] // 2
     keep = jnp.where(upper, pair[rows:], pair[:rows])
     send = jnp.where(upper, pair[:rows], pair[rows:])
-    keep, partner = lax.optimization_barrier((keep, partner))
-    other = lax.ppermute(send, "tok", FAR_HALF)
-    return keep + other, partner
+    return keep + lax.ppermute(send, "tok", FAR_HALF)
 
 
 def on_device(
@@ -192,10 +190,7 @@
     leading = lax.axis_index("inp") == 0
     local_counts = jnp.sum(onehot, axis=0) * jnp.where(leading, 1.0, 0.0)
     stats = jnp.concatenate([local_sq, local_counts, jnp.zeros((96,), jnp.float32)])[None, :]
-    d_quarter = y_sum(product(error, w_out_block, 1, 1))
-    stats, d_quarter = lax.optimization_barrier((stats, d_quarter))
     stats = jnp.sum(spread(stats, ("inp", "tok"), 64), axis=(0, 1))
-    d_active = far_sum(d_quarter)
     loss, sample_coef = kto_terms(
         stats[:SAMPLES], stats[SAMPLES : 2 * SAMPLES], labels, utility, ref_loss
     )
@@ -204,10 +199,12 @@
     own_coef = lax.dynamic_slice(coef, (own_rows, 0), (32, 1))
 
     grad_fold = fold_rows(product(active, error * coef, 0, 0))
-    d_rows = d_active * own_coef * slope_rows
-    grad_fold, d_rows = lax.optimization_barrier((grad_fold, d_rows))
+    grad_fold, error = lax.optimization_barrier((grad_fold, error))
     grad_out = queue_scatter(grad_fold)
-    grad_in, grad_out = half_sum(product(columns, quad_rows(d_rows), 0, 0), grad_out)
+    d_active = far_sum(y_sum(product(error, w_out_block, 1, 1)))
+    d_hidden = quad_rows(d_active * own_coef * slope_rows)
+    d_hidden, grad_out = lax.optimization_barrier((d_hidden, grad_out))
+    grad_in = half_sum(product(columns, d_hidden, 0, 0))
 
     weight_out, new_m_out, new_v_out, new_e_out = adamw(w_out, m_out, v_out, e_out, grad_out)
     new_w_out, _ = queue_gather(weight_out)

time: 346 us -> 351 us (1.014)
  waiting for transfers between devices: 109 us -> 133 us
  starting transfers between devices: 94 us -> 83.8 us
  blocking collectives: 101 us -> 92.4 us
    all_to_all x1 -> x0, blocking collectives: 17.9 us -> none  [spread(): return lax.all_to_all(copies, axis, 0, 0, axis_index_groups=groups)]
    ppermute x2, waiting for transfers between devices: 7.58 us -> 21.3 us  [far_sum(): return quarter + lax.ppermute(quarter, 'inp', FAR_HALF)]
    all_to_all x6 -> x7, waiting for transfers between devices: 27.5 us -> 39.7 us  [spread(): return lax.all_to_all(copies, axis, 0, 0, axis_index_groups=groups)]
    all_to_all x2 -> x3, blocking collectives: 31.8 us -> 41.6 us  [scatter_sum(): lax.all_to_all(blocks, axis, 0, 0, axis_index_groups=groups)]
    ppermute x2, starting transfers between devices: 25.6 us -> 15.8 us  [far_sum(): return quarter + lax.ppermute(quarter, 'inp', FAR_HALF)]
    all_to_all x2 -> x1, waiting for transfers between devices: 27.5 us -> 19.6 us  [scatter_sum(): lax.all_to_all(blocks, axis, 0, 0, axis_index_groups=groups)]
    reduce_scatter x1, waiting for transfers between devices: 27.7 us -> 34.3 us  [queue_scatter(): lax.psum_scatter(folded, 'tok', scatter_dimension=0, tiled=True, axis_ind...]
    all_to_all x2 -> x1, starting transfers between devices: 8.05 us -> 4.47 us  [scatter_sum(): lax.all_to_all(blocks, axis, 0, 0, axis_index_groups=groups)]
  transfers between devices with their start and end apart: 16 -> 16, of which waited for: 12 -> 11; matrix products, arithmetic and copies ran while one was open for 3% -> 3% of each run, Pallas kernels for 0% -> 0%
where the time goes in v3:
time: 351 us; the launch traced here: 350 us
  waiting for transfers between devices  133 us (38%)
  blocking collectives  92.4 us (26%)
  starting transfers between devices  83.8 us (24%)
  between operations  15.9 us (5%)
  local copies, waits for them, and re-layouts  12.2 us (3%)
  other arithmetic  8.01 us (2%)
  matrix products  4.3 us (1%)
    all_gather x1, blocking collectives, core_gather(): lax.all_gather(shard[:split], 'tok', axis=0, tiled=False, axis_index_grou...  50.8 us
    all_to_all x7, starting transfers between devices, spread(): return lax.all_to_all(copies, axis, 0, 0, axis_index_groups=groups)  43.7 us
    all_to_all x3, blocking collectives, scatter_sum(): lax.all_to_all(blocks, axis, 0, 0, axis_index_groups=groups)  41.6 us
    all_to_all x7, waiting for transfers between devices, spread(): return lax.all_to_all(copies, axis, 0, 0, axis_index_groups=groups)  39.7 us
    reduce_scatter x1, waiting for transfers between devices, queue_scatter(): lax.psum_scatter(folded, 'tok', scatter_dimension=0, tiled=True, axis_ind...  34.3 us
    ppermute x2, waiting for transfers between devices, far_sum(): return quarter + lax.ppermute(quarter, 'inp', FAR_HALF)  21.3 us
    all_to_all x1, waiting for transfers between devices, scatter_sum(): lax.all_to_all(blocks, axis, 0, 0, axis_index_groups=groups)  19.6 us
    ppermute x2, starting transfers between devices, far_sum(): return quarter + lax.ppermute(quarter, 'inp', FAR_HALF)  15.8 us
  transfers between devices with their start and end apart: 16, of which 11 were waited for; matrix products, arithmetic and copies ran while one was open for 3% of the time, Pallas kernels for 0%

profile of v3, /device:TPU:6, one launch (start us, length us, event | category | flops | bytes accessed | tf_op | source)
XLA Modules:
  0.0 350.1 jit_solution(17862530114253786874)
XLA Ops:
  7.2 9.2 %collective-permute-start = (f32[48,768]{1,0:T(8,128)}, f32[48,768]{1,0:T(8,128)S(1)}, u32[]{:S(2)}, u32[]{:S(2)}) collective-permute-start(f32[48,768]{1,0:T(8,128)} %param.20), channel_id=1, source_target_pairs={{0,4},{1,5},{2,6},{3,7},{4,0},{5,1},{6,2},{7,3},{8,12},{9,13},{10,... | collective-permute-start | bytes 442376 | tf_op jit(solution)/shard_map/ppermute | solution.py:128
  16.4 0.7 convert_element_type.20
  17.1 0.8 reshape.91
  18.0 0.1 reshape.92
  18.1 0.7 pad_maximum_fusion.5
  18.8 5.9 %all-to-all-start = ((f32[4,16,128]{2,1,0:T(8,128)}), f32[4,16,128]{2,1,0:T(8,128)S(1)}, u32[]{:S(2)}, u32[]{:S(2)}) async-start(f32[4,16,128]{2,1,0:T(8,128)} %pad_maximum_fusion.5), calls=%async_computation | async-start | bytes 65536 | tf_op jit(solution)/shard_map/all_to_all | solution.py:136
  24.7 5.9 %all-to-all-done = f32[4,16,128]{2,1,0:T(8,128)S(1)} async-done(((f32[4,16,128]{2,1,0:T(8,128)}), f32[4,16,128]{2,1,0:T(8,128)S(1)}, u32[]{:S(2)}, u32[]{:S(2)}) %all-to-all-start) | async-done | bytes 32800 | tf_op jit(solution)/shard_map/all_to_all | solution.py:136
  30.7 0.7 broadcast_in_dim.21
  31.4 4.8 %all-to-all-start.1 = ((f32[8,4,16,128]{3,2,1,0:T(8,128)}), f32[8,4,16,128]{3,2,1,0:T(8,128)S(1)}, u32[]{:S(2)}, u32[]{:S(2)}) async-start(f32[8,4,16,128]{3,2,1,0:T(8,128)} %broadcast_in_dim.21), calls=%async_computation.1 | async-start | bytes 524288 | tf_op jit(solution)/shard_map/all_to_all | solution.py:77
  36.2 5.4 %all-to-all-done.1 = f32[8,4,16,128]{3,2,1,0:T(8,128)S(1)} async-done(((f32[8,4,16,128]{3,2,1,0:T(8,128)}), f32[8,4,16,128]{3,2,1,0:T(8,128)S(1)}, u32[]{:S(2)}, u32[]{:S(2)}) %all-to-all-start.1) | async-done | bytes 262176 | tf_op jit(solution)/shard_map/all_to_all | solution.py:77
  41.6 1.9 fusion
  43.6 4.5 %all-to-all-start.2 = ((f32[4,128,768]{2,1,0:T(8,128)}), f32[4,128,768]{2,1,0:T(8,128)S(1)}, u32[]{:S(2)}, u32[]{:S(2)}) async-start(f32[4,128,768]{2,1,0:T(8,128)} %bitcast.5), calls=%async_computation.2 | async-start | bytes 3145728 | tf_op jit(solution)/shard_map/all_to_all | solution.py:72
  48.0 0.7 all-gather.6.cloned.1.call-update
  48.8 19.6 %all-to-all-done.2 = f32[4,128,768]{2,1,0:T(8,128)S(1)} async-done(((f32[4,128,768]{2,1,0:T(8,128)}), f32[4,128,768]{2,1,0:T(8,128)S(1)}, u32[]{:S(2)}, u32[]{:S(2)}) %all-to-all-start.2) | async-done | bytes 1572896 | tf_op jit(solution)/shard_map/all_to_all | solution.py:72
  68.4 0.1 reduce_sum.90
  68.5 22.8 %all_to_all.60 = f32[4,32,768]{2,1,0:T(8,128)S(1)} all-to-all(f32[4,32,768]{2,1,0:T(8,128)S(1)} %bitcast.76), channel_id=1, replica_groups={{0,1,2,3},{4,5,6,7},{8,9,10,11},{12,13,14,15},{16,17,18,19},{20,21,22,2..., dimensions={0} | all-to-all | bytes 786432 | tf_op jit(solution)/shard_map/all_to_all | solution.py:72
  91.3 13.3 %collective-permute-start.1 = (f32[32,768]{1,0:T(8,128)S(1)}, f32[32,768]{1,0:T(8,128)S(1)}, u32[]{:S(2)}, u32[]{:S(2)}) collective-permute-start(f32[32,768]{1,0:T(8,128)S(1)} %reduce_sum.91), channel_id=1, source_target_pairs={{0,256},{64,320},{128,384},{192,448},{256,0},{320,64},{384,128},{4... | collective-permute-start | bytes 294920 | tf_op jit(solution)/shard_map/ppermute | solution.py:85
  104.6 7.2 %collective-permute-done.1 = f32[32,768]{1,0:T(8,128)S(1)} collective-permute-done((f32[32,768]{1,0:T(8,128)S(1)}, f32[32,768]{1,0:T(8,128)S(1)}, u32[]{:S(2)}, u32[]{:S(2)}) %collective-permute-start.1) | collective-permute-done | bytes 98336 | tf_op jit(solution)/shard_map/ppermute | solution.py:85
  111.9 0.6 copy-done.3
  112.5 0.8 broadcast_in_dim.22
  113.3 3.5 all-to-all-start.4
  116.8 7.3 %all-to-all-done.4 = f32[4,32,768]{2,1,0:T(8,128)S(1)} async-done(((f32[4,32,768]{2,1,0:T(8,128)}), f32[4,32,768]{2,1,0:T(8,128)S(1)}, u32[]{:S(2)}, u32[]{:S(2)}) %all-to-all-start.4) | async-done | bytes 393248 | tf_op jit(solution)/shard_map/all_to_all | solution.py:77
  124.1 1.3 slice_bitcast_fusion.2
  125.6 0.5 fusion.20
  126.1 9.0 %all_to_all.61 = f32[8,16,384]{2,1,0:T(8,128)S(1)} all-to-all(f32[8,16,384]{2,1,0:T(8,128)S(1)} %fusion.20), channel_id=1, replica_groups=mesh['inp'=8,'hid'=8,'tok'=8] {'hid'}, dimensions={0} | all-to-all | bytes 393216 | tf_op jit(solution)/shard_map/all_to_all | solution.py:72
  135.2 0.7 broadcast_in_dim.23
  135.9 5.4 %all-to-all-start.6 = ((f32[8,16,384]{2,1,0:T(8,128)}), f32[8,16,384]{2,1,0:T(8,128)S(1)}, u32[]{:S(2)}, u32[]{:S(2)}) async-start(f32[8,16,384]{2,1,0:T(8,128)} %broadcast_in_dim.23), calls=%async_computation.6 | async-start | bytes 393216 | tf_op jit(solution)/shard_map/all_to_all | solution.py:77
  141.3 0.2 slice_reduce_fusion
  141.5 0.1 reshape_squeeze.3
  141.7 4.3 %all-to-all-done.6 = f32[8,16,384]{2,1,0:T(8,128)S(1)} async-done(((f32[8,16,384]{2,1,0:T(8,128)}), f32[8,16,384]{2,1,0:T(8,128)S(1)}, u32[]{:S(2)}, u32[]{:S(2)}) %all-to-all-start.6) | async-done | bytes 196640 | tf_op jit(solution)/shard_map/all_to_all | solution.py:77
  146.0 0.1 multiply_reduce_fusion
  146.2 0.1 select_reduce_fusion.1
  146.4 0.6 broadcast_in_dim.25
  147.1 15.2 %all-to-all-start.7 = ((f32[64,1,128]{2,1,0:T(1,128)}), f32[64,1,128]{2,1,0:T(1,128)S(1)}, u32[]{:S(2)}, u32[]{:S(2)}) async-start(f32[64,1,128]{2,1,0:T(1,128)} %broadcast_in_dim.25), calls=%async_computation.7 | async-start | bytes 65536 | tf_op jit(solution)/shard_map/all_to_all | solution.py:77
  162.3 0.2 copy.52
  162.4 14.6 %all-to-all-done.7 = f32[64,1,128]{2,1,0:T(1,128)S(1)} async-done(((f32[64,1,128]{2,1,0:T(1,128)}), f32[64,1,128]{2,1,0:T(1,128)S(1)}, u32[]{:S(2)}, u32[]{:S(2)}) %all-to-all-start.7) | async-done | bytes 32800 | tf_op jit(solution)/shard_map/all_to_all | solution.py:77
  177.1 0.1 multiply_divide_fusion
  177.1 0.1 select_reduce_fusion
  177.3 0.1 broadcast_multiply_fusion
  177.4 0.6 fusion.21
  178.2 1.1 pad_maximum_fusion.1
  179.3 0.6 fusion.22
  179.9 9.8 %all_to_all.62 = f32[4,32,768]{2,1,0:T(8,128)S(1)} all-to-all(f32[4,32,768]{2,1,0:T(8,128)S(1)} %fusion.22), channel_id=1, replica_groups={{0,64,128,192},{256,320,384,448},{1,65,129,193},{257,321,385,449},{2,66..., dimensions={0} | all-to-all | bytes 786432 | tf_op jit(solution)/shard_map/all_to_all | solution.py:72
  189.7 2.5 collective-permute-start.2
  192.4 14.0 %collective-permute-done.2 = f32[32,768]{1,0:T(8,128)S(1)} collective-permute-done((f32[32,768]{1,0:T(8,128)S(1)}, f32[32,768]{1,0:T(8,128)S(1)}, u32[]{:S(2)}, u32[]{:S(2)}) %collective-permute-start.2) | collective-permute-done | bytes 98336 | tf_op jit(solution)/shard_map/ppermute | solution.py:85
  206.5 0.8 broadcast_in_dim.26
  207.2 4.6 %all-to-all-start.9 = ((f32[4,32,768]{2,1,0:T(8,128)}), f32[4,32,768]{2,1,0:T(8,128)S(1)}, u32[]{:S(2)}, u32[]{:S(2)}) async-start(f32[4,32,768]{2,1,0:T(8,128)} %broadcast_in_dim.26), calls=%async_computation.9 | async-start | bytes 786432 | tf_op jit(solution)/shard_map/all_to_all | solution.py:77
  211.8 0.7 reduce-scatter.2.cloned.1.call-update
  212.5 8.1 %all-to-all-done.9 = f32[4,32,768]{2,1,0:T(8,128)S(1)} async-done(((f32[4,32,768]{2,1,0:T(8,128)}), f32[4,32,768]{2,1,0:T(8,128)S(1)}, u32[]{:S(2)}, u32[]{:S(2)}) %all-to-all-start.9) | async-done | bytes 393248 | tf_op jit(solution)/shard_map/all_to_all | solution.py:77
  220.7 1.3 broadcast_in_dim.28
  222.0 3.7 %all-to-all-start.10 = ((f32[4,128,768]{2,1,0:T(8,128)}), f32[4,128,768]{2,1,0:T(8,128)S(1)}, u32[]{:S(2)}, u32[]{:S(2)}) async-start(f32[4,128,768]{2,1,0:T(8,128)} %broadcast_in_dim.28), calls=%async_computation.10 | async-start | bytes 3145728 | tf_op jit(solution)/shard_map/all_to_all | solution.py:77
  225.7 34.3 %reduce-scatter.2.cloned.1.call-done = f32[96,384]{1,0:T(8,128)} async-done(((f32[768,384]{1,0:T(8,128)}), f32[96,384]{1,0:T(8,128)}) %reduce-scatter.2.cloned.1.call-update) | async-done | bytes 147472 | tf_op jit(solution)/shard_map/reduce_scatter | solution.py:107
  260.1 1.8 multiply_add_fusion.1
  261.9 0.6 fusion.4
  262.6 4.7 %collective-permute-start.3 = (f32[48,768]{1,0:T(8,128)S(1)}, f32[48,768]{1,0:T(8,128)S(1)}, u32[]{:S(2)}, u32[]{:S(2)}) collective-permute-start(f32[48,768]{1,0:T(8,128)S(1)} %slice_select_fusion), channel_id=1, source_target_pairs={{0,4},{1,5},{2,6},{3,7},{4,0},{5,1},{6,2},{7,3},{8,12},{9,13},{10,... | collective-permute-start | bytes 442376 | tf_op jit(solution)/shard_map/ppermute | solution.py:151
  267.3 0.6 multiply_reduce_fusion.1
  268.5 11.1 %collective-permute-done.3 = f32[48,768]{1,0:T(8,128)S(1)} collective-permute-done((f32[48,768]{1,0:T(8,128)S(1)}, f32[48,768]{1,0:T(8,128)S(1)}, u32[]{:S(2)}, u32[]{:S(2)}) %collective-permute-start.3) | collective-permute-done | bytes 147488 | tf_op jit(solution)/shard_map/ppermute | solution.py:151
  279.7 0.9 multiply_add_fusion.2
  280.6 0.7 broadcast_in_dim.29
  281.2 6.5 %all-to-all-start.11 = ((f32[8,8,768]{2,1,0:T(8,128)}), f32[8,8,768]{2,1,0:T(8,128)S(1)}, u32[]{:S(2)}, u32[]{:S(2)}) async-start(f32[8,8,768]{2,1,0:T(8,128)} %broadcast_in_dim.29), calls=%async_computation.12 | async-start | bytes 393216 | tf_op jit(solution)/shard_map/all_to_all | solution.py:77
  287.8 50.8 %all-gather.1 = f32[320,768]{1,0:T(8,128)S(1)} all-gather(f32[40,768]{1,0:T(8,128)S(1)} %slice.76), channel_id=3, replica_groups={{0,2,4,6,7,5,3,1},{8,10,12,14,15,13,11,9},{16,18,20,22,23,21,19,17},{24..., dimensions={0}, use_global_device_ids=true | all-gather | bytes 1105920 | tf_op jit(solution)/shard_map/all_gather | solution.py:119
  338.8 1.1 pad_maximum_fusion.2
  339.9 1.3 fusion.18
  341.4 1.1 copy.55
  (69 shorter events, 1.5 us)
Async XLA Ops:
  7.2 29.0 %copy-start = (f32[48,768]{1,0:T(8,128)S(1)}, f32[48,768]{1,0:T(8,128)}, u32[]{:S(2)}) copy-start(f32[48,768]{1,0:T(8,128)} %param.20) | copy-start | bytes 442372
  7.2 29.0 %collective-permute-start = (f32[48,768]{1,0:T(8,128)}, f32[48,768]{1,0:T(8,128)S(1)}, u32[]{:S(2)}, u32[]{:S(2)}) collective-permute-start(f32[48,768]{1,0:T(8,128)} %param.20), channel_id=1, source_target_pairs={{0,4},{1,5},{2,6},{3,7},{4,0},{5,1},{6,2},{7,3},{8,12},{9,13},{10,... | collective-permute-start | bytes 442376 | tf_op jit(solution)/shard_map/ppermute | solution.py:128
  18.8 11.8 %all-to-all-start = ((f32[4,16,128]{2,1,0:T(8,128)}), f32[4,16,128]{2,1,0:T(8,128)S(1)}, u32[]{:S(2)}, u32[]{:S(2)}) async-start(f32[4,16,128]{2,1,0:T(8,128)} %pad_maximum_fusion.5), calls=%async_computation | async-start | bytes 65536 | tf_op jit(solution)/shard_map/all_to_all | solution.py:136
  31.4 10.2 %all-to-all-start.1 = ((f32[8,4,16,128]{3,2,1,0:T(8,128)}), f32[8,4,16,128]{3,2,1,0:T(8,128)S(1)}, u32[]{:S(2)}, u32[]{:S(2)}) async-start(f32[8,4,16,128]{3,2,1,0:T(8,128)} %broadcast_in_dim.21), calls=%async_computation.1 | async-start | bytes 524288 | tf_op jit(solution)/shard_map/all_to_all | solution.py:77
  43.6 24.8 %all-to-all-start.2 = ((f32[4,128,768]{2,1,0:T(8,128)}), f32[4,128,768]{2,1,0:T(8,128)S(1)}, u32[]{:S(2)}, u32[]{:S(2)}) async-start(f32[4,128,768]{2,1,0:T(8,128)} %bitcast.5), calls=%async_computation.2 | async-start | bytes 3145728 | tf_op jit(solution)/shard_map/all_to_all | solution.py:72
  48.0 68.8 %all-gather.6.cloned.1.call-start = ((), (), s32[]{:S(2)}) async-start(), calls=%async_computation.14 | async-start | bytes 1327104 | tf_op jit(solution)/shard_map/all_gather | solution.py:94
  91.3 20.5 %collective-permute-start.1 = (f32[32,768]{1,0:T(8,128)S(1)}, f32[32,768]{1,0:T(8,128)S(1)}, u32[]{:S(2)}, u32[]{:S(2)}) collective-permute-start(f32[32,768]{1,0:T(8,128)S(1)} %reduce_sum.91), channel_id=1, source_target_pairs={{0,256},{64,320},{128,384},{192,448},{256,0},{320,64},{384,128},{4... | collective-permute-start | bytes 294920 | tf_op jit(solution)/shard_map/ppermute | solution.py:85
  111.8 0.6 copy-start.3
  113.3 10.8 %all-to-all-start.4 = ((f32[4,32,768]{2,1,0:T(8,128)}), f32[4,32,768]{2,1,0:T(8,128)S(1)}, u32[]{:S(2)}, u32[]{:S(2)}) async-start(f32[4,32,768]{2,1,0:T(8,128)} %broadcast_in_dim.22), calls=%async_computation.4 | async-start | bytes 786432 | tf_op jit(solution)/shard_map/all_to_all | solution.py:77
  125.6 9.6 %copy-start.11 = (f32[16,384]{1,0:T(8,128)S(1)}, f32[16,384]{1,0:T(8,128)}, u32[]{:S(2)}) copy-start(f32[16,384]{1,0:T(8,128)} %param.15) | copy-start | bytes 73732
  135.2 41.9 %copy-start.12 = (s32[16]{0:T(128)S(1)}, s32[16]{0:T(128)}, u32[]{:S(2)}) copy-start(s32[16]{0:T(128)} %param.17) | copy-start | bytes 196
  135.2 41.9 %copy-start.13 = (f32[16]{0:T(128)S(1)}, f32[16]{0:T(128)}, u32[]{:S(2)}) copy-start(f32[16]{0:T(128)} %param.19) | copy-start | bytes 196
  135.2 41.9 %copy-start.14 = (f32[16]{0:T(128)S(1)}, f32[16]{0:T(128)}, u32[]{:S(2)}) copy-start(f32[16]{0:T(128)} %param.18) | copy-start | bytes 196
  135.9 10.1 %all-to-all-start.6 = ((f32[8,16,384]{2,1,0:T(8,128)}), f32[8,16,384]{2,1,0:T(8,128)S(1)}, u32[]{:S(2)}, u32[]{:S(2)}) async-start(f32[8,16,384]{2,1,0:T(8,128)} %broadcast_in_dim.23), calls=%async_computation.6 | async-start | bytes 393216 | tf_op jit(solution)/shard_map/all_to_all | solution.py:77
  147.1 30.0 %all-to-all-start.7 = ((f32[64,1,128]{2,1,0:T(1,128)}), f32[64,1,128]{2,1,0:T(1,128)S(1)}, u32[]{:S(2)}, u32[]{:S(2)}) async-start(f32[64,1,128]{2,1,0:T(1,128)} %broadcast_in_dim.25), calls=%async_computation.7 | async-start | bytes 65536 | tf_op jit(solution)/shard_map/all_to_all | solution.py:77
  179.3 27.1 %copy-start.4 = (f32[32,768]{1,0:T(8,128)S(1)}, f32[32,768]{1,0:T(8,128)}, u32[]{:S(2)}) copy-start(f32[32,768]{1,0:T(8,128)} %copy-done.3) | copy-start | bytes 294916
  189.7 16.6 %collective-permute-start.2 = (f32[32,768]{1,0:T(8,128)S(1)}, f32[32,768]{1,0:T(8,128)S(1)}, u32[]{:S(2)}, u32[]{:S(2)}) collective-permute-start(f32[32,768]{1,0:T(8,128)S(1)} %reduce_sum.99), channel_id=1, source_target_pairs={{0,256},{64,320},{128,384},{192,448},{256,0},{320,64},{384,128},{4... | collective-permute-start | bytes 294920 | tf_op jit(solution)/shard_map/ppermute | solution.py:85
  207.2 13.4 %all-to-all-start.9 = ((f32[4,32,768]{2,1,0:T(8,128)}), f32[4,32,768]{2,1,0:T(8,128)S(1)}, u32[]{:S(2)}, u32[]{:S(2)}) async-start(f32[4,32,768]{2,1,0:T(8,128)} %broadcast_in_dim.26), calls=%async_computation.9 | async-start | bytes 786432 | tf_op jit(solution)/shard_map/all_to_all | solution.py:77
  211.8 48.3 %reduce-scatter.2.cloned.1.call-start = ((), (), s32[]{:S(2)}) async-start(), calls=%async_computation.13 | async-start | bytes 1327104 | tf_op jit(solution)/shard_map/reduce_scatter | solution.py:107
  222.0 38.1 %copy-start.2 = (f32[96,384]{1,0:T(8,128)S(1)}, f32[96,384]{1,0:T(8,128)}, u32[]{:S(2)}) copy-start(f32[96,384]{1,0:T(8,128)} %param.21) | copy-start | bytes 442372
  222.0 38.1 %copy-start.8 = (f32[96,384]{1,0:T(8,128)S(1)}, f32[96,384]{1,0:T(8,128)}, u32[]{:S(2)}) copy-start(f32[96,384]{1,0:T(8,128)} %param.27) | copy-start | bytes 442372
  222.0 38.1 %copy-start.9 = (f32[96,384]{1,0:T(8,128)S(1)}, f32[96,384]{1,0:T(8,128)}, u32[]{:S(2)}) copy-start(f32[96,384]{1,0:T(8,128)} %param.23) | copy-start | bytes 442372
  222.0 38.1 %copy-start.10 = (f32[96,384]{1,0:T(8,128)S(1)}, f32[96,384]{1,0:T(8,128)}, u32[]{:S(2)}) copy-start(f32[96,384]{1,0:T(8,128)} %param.25) | copy-start | bytes 442372
  222.0 38.1 %all-to-all-start.10 = ((f32[4,128,768]{2,1,0:T(8,128)}), f32[4,128,768]{2,1,0:T(8,128)S(1)}, u32[]{:S(2)}, u32[]{:S(2)}) async-start(f32[4,128,768]{2,1,0:T(8,128)} %broadcast_in_dim.28), calls=%async_computation.10 | async-start | bytes 3145728 | tf_op jit(solution)/shard_map/all_to_all | solution.py:77
  225.7 114.2 %all-gather.8.cloned.1.call-start = ((), (), s32[]{:S(2)}) async-start(), calls=%async_computation.15 | async-start | bytes 1327104 | tf_op jit(solution)/shard_map/all_gather | solution.py:94
  261.9 17.8 %copy-start.1 = (f32[48,768]{1,0:T(8,128)S(1)}, f32[48,768]{1,0:T(8,128)}, u32[]{:S(2)}) copy-start(f32[48,768]{1,0:T(8,128)} %param.20) | copy-start | bytes 442372
  261.9 17.8 %copy-start.5 = (f32[48,768]{1,0:T(8,128)S(1)}, f32[48,768]{1,0:T(8,128)}, u32[]{:S(2)}) copy-start(f32[48,768]{1,0:T(8,128)} %param.26) | copy-start | bytes 442372
  261.9 17.8 %copy-start.6 = (f32[48,768]{1,0:T(8,128)S(1)}, f32[48,768]{1,0:T(8,128)}, u32[]{:S(2)}) copy-start(f32[48,768]{1,0:T(8,128)} %param.22) | copy-start | bytes 442372
  261.9 17.8 %copy-start.7 = (f32[48,768]{1,0:T(8,128)S(1)}, f32[48,768]{1,0:T(8,128)}, u32[]{:S(2)}) copy-start(f32[48,768]{1,0:T(8,128)} %param.24) | copy-start | bytes 442372
  262.6 17.1 %collective-permute-start.3 = (f32[48,768]{1,0:T(8,128)S(1)}, f32[48,768]{1,0:T(8,128)S(1)}, u32[]{:S(2)}, u32[]{:S(2)}) collective-permute-start(f32[48,768]{1,0:T(8,128)S(1)} %slice_select_fusion), channel_id=1, source_target_pairs={{0,4},{1,5},{2,6},{3,7},{4,0},{5,1},{6,2},{7,3},{8,12},{9,13},{10,... | collective-permute-start | bytes 442376 | tf_op jit(solution)/shard_map/ppermute | solution.py:151
  281.2 57.5 %all-to-all-start.11 = ((f32[8,8,768]{2,1,0:T(8,128)}), f32[8,8,768]{2,1,0:T(8,128)S(1)}, u32[]{:S(2)}, u32[]{:S(2)}) async-start(f32[8,8,768]{2,1,0:T(8,128)} %broadcast_in_dim.29), calls=%async_computation.12 | async-start | bytes 393216 | tf_op jit(solution)/shard_map/all_to_all | solution.py:77
Sparse Core Ops, SparseCore 0:
  50.9 63.9 all-gather.5
  216.0 44.0 reduce-scatter.1
  262.1 60.1 all-gather.7

commit v4 on v2

--- a/solution.py
+++ b/solution.py
@@ -24,6 +24,7 @@
 
 
 QUADS = [[0, 1, 2, 3], [4, 5, 6, 7]]
+HID_QUADS = [[h * 8 + half + q for h in range(8) for q in range(4)] for half in (0, 4)]
 FAR_HALF = [(i, (i + 4) % 8) for i in range(8)]
 FOLD = (0, 2, 4, 6, 7, 5, 3, 1)
 
@@ -133,8 +134,9 @@
     blocks = jnp.transpose(tokens.reshape(16, 2, 4, 48), (2, 0, 1, 3)).reshape(4, 16, 96)
     id_lanes = jnp.broadcast_to(sample_ids.astype(jnp.float32)[None, :, None], (4, 16, 32))
     blocks = jnp.concatenate([blocks, id_lanes], axis=2)
-    near = lax.all_to_all(blocks, "tok", 0, 0, axis_index_groups=QUADS)
-    every = spread(near, "hid", 8).reshape(4, 2, 4, 16, 128)
+    copies = jnp.broadcast_to(blocks[None], (8, 4, 16, 128)).reshape(32, 16, 128)
+    every = lax.all_to_all(copies, ("hid", "tok"), 0, 0, axis_index_groups=HID_QUADS)
+    every = every.reshape(4, 2, 4, 16, 128)
     return jnp.transpose(every, (0, 2, 1, 3, 4)).reshape(512, 128)
 
 
@@ -143,14 +145,13 @@
     return spread(near, "inp", 4, QUADS).reshape(512, 768)
 
 
-def half_sum(pair, partner):
+def half_sum(pair):
     upper = lax.axis_index("tok") >= 4
     rows = pair.shape[0] // 2
     keep = jnp.where(upper, pair[rows:], pair[:rows])
     send = jnp.where(upper, pair[:rows], pair[rows:])
-    keep, partner = lax.optimization_barrier((keep, partner))
     other = lax.ppermute(send, "tok", FAR_HALF)
-    return keep + other, partner
+    return keep + other
 
 
 def on_device(
@@ -207,7 +208,7 @@
     d_rows = d_active * own_coef * slope_rows
     grad_fold, d_rows = lax.optimization_barrier((grad_fold, d_rows))
     grad_out = queue_scatter(grad_fold)
-    grad_in, grad_out = half_sum(product(columns, quad_rows(d_rows), 0, 0), grad_out)
+    grad_in = half_sum(product(columns, quad_rows(d_rows), 0, 0))
 
     weight_out, new_m_out, new_v_out, new_e_out = adamw(w_out, m_out, v_out, e_out, grad_out)
     new_w_out, _ = queue_gather(weight_out)

time: 346 us -> 336 us (0.971)
  starting transfers between devices: 94 us -> 83.9 us
  blocking collectives: 101 us -> 108 us
  waiting for transfers between devices: 109 us -> 103 us
    all_to_all x6 -> x5, waiting for transfers between devices: 27.5 us -> 14 us  [spread(): return lax.all_to_all(copies, axis, 0, 0, axis_index_groups=groups)]
    all_to_all x2, blocking collectives: 31.8 us -> 43 us  [scatter_sum(): lax.all_to_all(blocks, axis, 0, 0, axis_index_groups=groups)]
    ppermute x1, waiting for transfers between devices: 0.01 us -> 9.66 us  [half_pair(): other = lax.ppermute(shard, 'tok', FAR_HALF)]
    all_to_all x6 -> x5, starting transfers between devices: 40.2 us -> 31.5 us  [spread(): return lax.all_to_all(copies, axis, 0, 0, axis_index_groups=groups)]
    reduce_scatter x1, waiting for transfers between devices: 27.7 us -> 33.9 us  [queue_scatter(): lax.psum_scatter(folded, 'tok', scatter_dimension=0, tiled=True, axis_ind...]
    all_to_all x1, waiting for transfers between devices: 5.91 us -> 0.01 us  [quad_columns(): lax.all_to_all(copies, ('hid', 'tok'), 0, 0, axis_index_groups=HID_QUADS)]
    ppermute x2, starting transfers between devices: 25.6 us -> 20.4 us  [far_sum(): return quarter + lax.ppermute(quarter, 'inp', FAR_HALF)]
    ppermute x2, waiting for transfers between devices: 7.58 us -> 11.4 us  [far_sum(): return quarter + lax.ppermute(quarter, 'inp', FAR_HALF)]
  transfers between devices with their start and end apart: 16 -> 15, of which waited for: 12 -> 10; matrix products, arithmetic and copies ran while one was open for 3% -> 3% of each run, Pallas kernels for 0% -> 0%
where the time goes in v4:
time: 336 us; the launch traced here: 334 us
  blocking collectives  108 us (32%)
  waiting for transfers between devices  103 us (31%)
  starting transfers between devices  83.9 us (25%)
  between operations  15.9 us (5%)
  local copies, waits for them, and re-layouts  10.8 us (3%)
  other arithmetic  7.43 us (2%)
  matrix products  5.02 us (1%)
    all_gather x1, blocking collectives, core_gather(): lax.all_gather(shard[:split], 'tok', axis=0, tiled=False, axis_index_grou...  50.5 us
    all_to_all x2, blocking collectives, scatter_sum(): lax.all_to_all(blocks, axis, 0, 0, axis_index_groups=groups)  43 us
    reduce_scatter x1, waiting for transfers between devices, queue_scatter(): lax.psum_scatter(folded, 'tok', scatter_dimension=0, tiled=True, axis_ind...  33.9 us
    all_to_all x5, starting transfers between devices, spread(): return lax.all_to_all(copies, axis, 0, 0, axis_index_groups=groups)  31.5 us
    all_to_all x2, waiting for transfers between devices, scatter_sum(): lax.all_to_all(blocks, axis, 0, 0, axis_index_groups=groups)  23.7 us
    ppermute x2, starting transfers between devices, far_sum(): return quarter + lax.ppermute(quarter, 'inp', FAR_HALF)  20.4 us
    all_to_all x1, blocking collectives, spread(): return lax.all_to_all(copies, axis, 0, 0, axis_index_groups=groups)  14.4 us
    all_to_all x5, waiting for transfers between devices, spread(): return lax.all_to_all(copies, axis, 0, 0, axis_index_groups=groups)  14 us
  transfers between devices with their start and end apart: 15, of which 10 were waited for; matrix products, arithmetic and copies ran while one was open for 3% of the time, Pallas kernels for 0%

profile of v4, /device:TPU:6, one launch (start us, length us, event | category | flops | bytes accessed | tf_op | source)
XLA Modules:
  0.0 333.9 jit_solution(11090767581295203811)
XLA Ops:
  7.2 0.7 convert_element_type.20
  7.9 0.8 reshape.93
  8.8 0.1 reshape.94
  8.9 0.1 pad_maximum_fusion.5
  9.0 0.7 broadcast_in_dim.25
  9.8 9.5 %all-to-all-start = ((f32[32,16,128]{2,1,0:T(8,128)}), f32[32,16,128]{2,1,0:T(8,128)S(1)}, u32[]{:S(2)}, u32[]{:S(2)}) async-start(f32[32,16,128]{2,1,0:T(8,128)} %bitcast.1), calls=%async_computation | async-start | bytes 524288 | tf_op jit(solution)/shard_map/all_to_all | solution.py:138
  19.3 8.6 %collective-permute-start = (f32[48,768]{1,0:T(8,128)S(1)}, f32[48,768]{1,0:T(8,128)S(1)}, u32[]{:S(2)}, u32[]{:S(2)}) collective-permute-start(f32[48,768]{1,0:T(8,128)S(1)} %copy-done), channel_id=1, source_target_pairs={{0,4},{1,5},{2,6},{3,7},{4,0},{5,1},{6,2},{7,3},{8,12},{9,13},{10,... | collective-permute-start | bytes 442376 | tf_op jit(solution)/shard_map/ppermute | solution.py:129
  27.9 9.7 %collective-permute-done = f32[48,768]{1,0:T(8,128)S(1)} collective-permute-done((f32[48,768]{1,0:T(8,128)S(1)}, f32[48,768]{1,0:T(8,128)S(1)}, u32[]{:S(2)}, u32[]{:S(2)}) %collective-permute-start) | collective-permute-done | bytes 147488 | tf_op jit(solution)/shard_map/ppermute | solution.py:129
  37.6 1.9 fusion
  39.6 4.5 %all-to-all-start.1 = ((f32[4,128,768]{2,1,0:T(8,128)}), f32[4,128,768]{2,1,0:T(8,128)S(1)}, u32[]{:S(2)}, u32[]{:S(2)}) async-start(f32[4,128,768]{2,1,0:T(8,128)} %bitcast.6), calls=%async_computation.1 | async-start | bytes 3145728 | tf_op jit(solution)/shard_map/all_to_all | solution.py:73
  44.0 0.7 all-gather.6.cloned.1.call-update
  44.7 15.9 %all-to-all-done.1 = f32[4,128,768]{2,1,0:T(8,128)S(1)} async-done(((f32[4,128,768]{2,1,0:T(8,128)}), f32[4,128,768]{2,1,0:T(8,128)S(1)}, u32[]{:S(2)}, u32[]{:S(2)}) %all-to-all-start.1) | async-done | bytes 1572896 | tf_op jit(solution)/shard_map/all_to_all | solution.py:73
  60.6 0.1 reduce_sum.90
  60.8 33.1 %all_to_all.55 = f32[4,32,768]{2,1,0:T(8,128)S(1)} all-to-all(f32[4,32,768]{2,1,0:T(8,128)S(1)} %bitcast.79), channel_id=1, replica_groups={{0,1,2,3},{4,5,6,7},{8,9,10,11},{12,13,14,15},{16,17,18,19},{20,21,22,2..., dimensions={0} | all-to-all | bytes 786432 | tf_op jit(solution)/shard_map/all_to_all | solution.py:73
  93.9 8.2 %collective-permute-start.1 = (f32[32,768]{1,0:T(8,128)S(1)}, f32[32,768]{1,0:T(8,128)S(1)}, u32[]{:S(2)}, u32[]{:S(2)}) collective-permute-start(f32[32,768]{1,0:T(8,128)S(1)} %reduce_sum.91), channel_id=1, source_target_pairs={{0,256},{64,320},{128,384},{192,448},{256,0},{320,64},{384,128},{4... | collective-permute-start | bytes 294920 | tf_op jit(solution)/shard_map/ppermute | solution.py:86
  102.1 10.9 %collective-permute-done.1 = f32[32,768]{1,0:T(8,128)S(1)} collective-permute-done((f32[32,768]{1,0:T(8,128)S(1)}, f32[32,768]{1,0:T(8,128)S(1)}, u32[]{:S(2)}, u32[]{:S(2)}) %collective-permute-start.1) | collective-permute-done | bytes 98336 | tf_op jit(solution)/shard_map/ppermute | solution.py:86
  113.1 0.8 broadcast_in_dim.26
  113.9 3.5 %all-to-all-start.3 = ((f32[4,32,768]{2,1,0:T(8,128)}), f32[4,32,768]{2,1,0:T(8,128)S(1)}, u32[]{:S(2)}, u32[]{:S(2)}) async-start(f32[4,32,768]{2,1,0:T(8,128)} %broadcast_in_dim.26), calls=%async_computation.3 | async-start | bytes 786432 | tf_op jit(solution)/shard_map/all_to_all | solution.py:78
  117.4 7.3 %all-to-all-done.3 = f32[4,32,768]{2,1,0:T(8,128)S(1)} async-done(((f32[4,32,768]{2,1,0:T(8,128)}), f32[4,32,768]{2,1,0:T(8,128)S(1)}, u32[]{:S(2)}, u32[]{:S(2)}) %all-to-all-start.3) | async-done | bytes 393248 | tf_op jit(solution)/shard_map/all_to_all | solution.py:78
  124.7 1.3 slice_bitcast_fusion.2
  126.1 0.5 fusion.20
  126.7 9.9 %all_to_all.56 = f32[8,16,384]{2,1,0:T(8,128)S(1)} all-to-all(f32[8,16,384]{2,1,0:T(8,128)S(1)} %fusion.20), channel_id=1, replica_groups=mesh['inp'=8,'hid'=8,'tok'=8] {'hid'}, dimensions={0} | all-to-all | bytes 393216 | tf_op jit(solution)/shard_map/all_to_all | solution.py:73
  136.6 0.7 broadcast_in_dim.27
  137.3 5.4 %all-to-all-start.5 = ((f32[8,16,384]{2,1,0:T(8,128)}), f32[8,16,384]{2,1,0:T(8,128)S(1)}, u32[]{:S(2)}, u32[]{:S(2)}) async-start(f32[8,16,384]{2,1,0:T(8,128)} %broadcast_in_dim.27), calls=%async_computation.5 | async-start | bytes 393216 | tf_op jit(solution)/shard_map/all_to_all | solution.py:78
  142.7 0.2 slice_reduce_fusion
  142.9 0.1 reshape_squeeze.3
  143.0 0.1 convert_element_type.22
  143.1 4.3 %all-to-all-done.5 = f32[8,16,384]{2,1,0:T(8,128)S(1)} async-done(((f32[8,16,384]{2,1,0:T(8,128)}), f32[8,16,384]{2,1,0:T(8,128)S(1)}, u32[]{:S(2)}, u32[]{:S(2)}) %all-to-all-start.5) | async-done | bytes 196640 | tf_op jit(solution)/shard_map/all_to_all | solution.py:78
  147.4 0.1 multiply_reduce_fusion
  147.5 0.1 mul.242
  147.6 1.4 fusion.21
  149.0 3.6 %all-to-all-start.6 = ((f32[4,32,768]{2,1,0:T(8,128)}), f32[4,32,768]{2,1,0:T(8,128)S(1)}, u32[]{:S(2)}, u32[]{:S(2)}) async-start(f32[4,32,768]{2,1,0:T(8,128)} %fusion.21), calls=%async_computation.6 | async-start | bytes 786432 | tf_op jit(solution)/shard_map/all_to_all | solution.py:73
  152.6 0.1 select_reduce_fusion.1
  152.8 7.8 %all-to-all-done.6 = f32[4,32,768]{2,1,0:T(8,128)S(1)} async-done(((f32[4,32,768]{2,1,0:T(8,128)}), f32[4,32,768]{2,1,0:T(8,128)S(1)}, u32[]{:S(2)}, u32[]{:S(2)}) %all-to-all-start.6) | async-done | bytes 393248 | tf_op jit(solution)/shard_map/all_to_all | solution.py:73
  160.6 0.6 broadcast_in_dim.31
  161.3 12.2 %all-to-all-start.7 = ((f32[64,1,128]{2,1,0:T(1,128)}), f32[64,1,128]{2,1,0:T(1,128)S(1)}, u32[]{:S(2)}, u32[]{:S(2)}) async-start(f32[64,1,128]{2,1,0:T(1,128)} %broadcast_in_dim.31), calls=%async_computation.7 | async-start | bytes 65536 | tf_op jit(solution)/shard_map/all_to_all | solution.py:78
  173.5 0.2 copy.52
  173.7 12.3 %collective-permute-start.2 = (f32[32,768]{1,0:T(8,128)S(1)}, f32[32,768]{1,0:T(8,128)S(1)}, u32[]{:S(2)}, u32[]{:S(2)}) collective-permute-start(f32[32,768]{1,0:T(8,128)S(1)} %reduce_sum.96), channel_id=1, source_target_pairs={{0,256},{64,320},{128,384},{192,448},{256,0},{320,64},{384,128},{4... | collective-permute-start | bytes 294920 | tf_op jit(solution)/shard_map/ppermute | solution.py:86
  186.0 2.4 all-to-all-done.7
  188.4 0.1 multiply_divide_fusion
  188.5 0.1 select_reduce_fusion
  188.6 0.1 mul.258
  188.7 0.1 broadcast_multiply_fusion
  188.8 0.6 fusion.22
  189.6 0.1 dynamic-slice.3
  189.7 1.1 pad_maximum_fusion.1
  190.7 0.5 collective-permute-done.2
  191.2 0.1 fusion.14
  191.4 14.4 %all_to_all.57 = f32[4,32,768]{2,1,0:T(8,128)S(1)} all-to-all(f32[4,32,768]{2,1,0:T(8,128)S(1)} %broadcast_in_dim.32), channel_id=1, replica_groups={{0,1,2,3},{4,5,6,7},{8,9,10,11},{12,13,14,15},{16,17,18,19},{20,21,22,2..., dimensions={0} | all-to-all | bytes 786432 | tf_op jit(solution)/shard_map/all_to_all | solution.py:78
  205.8 1.3 broadcast_in_dim.34
  207.1 4.5 %all-to-all-start.9 = ((f32[4,128,768]{2,1,0:T(8,128)}), f32[4,128,768]{2,1,0:T(8,128)S(1)}, u32[]{:S(2)}, u32[]{:S(2)}) async-start(f32[4,128,768]{2,1,0:T(8,128)} %broadcast_in_dim.34), calls=%async_computation.9 | async-start | bytes 3145728 | tf_op jit(solution)/shard_map/all_to_all | solution.py:78
  211.6 33.9 %reduce-scatter.2.cloned.1.call-done = f32[96,384]{1,0:T(8,128)} async-done(((f32[768,384]{1,0:T(8,128)}), f32[96,384]{1,0:T(8,128)}) %reduce-scatter.2.cloned.1.call-update) | async-done | bytes 147472 | tf_op jit(solution)/shard_map/reduce_scatter | solution.py:108
  245.5 1.8 multiply_add_fusion.1
  247.3 0.6 fusion.4
  248.0 5.7 %collective-permute-start.3 = (f32[48,768]{1,0:T(8,128)S(1)}, f32[48,768]{1,0:T(8,128)S(1)}, u32[]{:S(2)}, u32[]{:S(2)}) collective-permute-start(f32[48,768]{1,0:T(8,128)S(1)} %slice_select_fusion), channel_id=1, source_target_pairs={{0,4},{1,5},{2,6},{3,7},{4,0},{5,1},{6,2},{7,3},{8,12},{9,13},{10,... | collective-permute-start | bytes 442376 | tf_op jit(solution)/shard_map/ppermute | solution.py:153
  253.6 0.6 multiply_reduce_fusion.1
  254.9 9.5 %collective-permute-done.3 = f32[48,768]{1,0:T(8,128)S(1)} collective-permute-done((f32[48,768]{1,0:T(8,128)S(1)}, f32[48,768]{1,0:T(8,128)S(1)}, u32[]{:S(2)}, u32[]{:S(2)}) %collective-permute-start.3) | collective-permute-done | bytes 147488 | tf_op jit(solution)/shard_map/ppermute | solution.py:153
  264.4 0.9 multiply_add_fusion.2
  265.2 0.7 broadcast_in_dim.35
  265.9 6.0 %all-to-all-start.10 = ((f32[8,8,768]{2,1,0:T(8,128)}), f32[8,8,768]{2,1,0:T(8,128)S(1)}, u32[]{:S(2)}, u32[]{:S(2)}) async-start(f32[8,8,768]{2,1,0:T(8,128)} %broadcast_in_dim.35), calls=%async_computation.10 | async-start | bytes 393216 | tf_op jit(solution)/shard_map/all_to_all | solution.py:78
  271.9 50.5 %all-gather.1 = f32[320,768]{1,0:T(8,128)S(1)} all-gather(f32[40,768]{1,0:T(8,128)S(1)} %slice.76), channel_id=3, replica_groups={{0,2,4,6,7,5,3,1},{8,10,12,14,15,13,11,9},{16,18,20,22,23,21,19,17},{24..., dimensions={0}, use_global_device_ids=true | all-gather | bytes 1105920 | tf_op jit(solution)/shard_map/all_gather | solution.py:120
  322.6 1.1 pad_maximum_fusion.2
  323.7 1.3 fusion.18
  325.1 1.1 copy.55
  (61 shorter events, 1.1 us)
Async XLA Ops:
  7.2 12.1 %copy-start = (f32[48,768]{1,0:T(8,128)S(1)}, f32[48,768]{1,0:T(8,128)}, u32[]{:S(2)}) copy-start(f32[48,768]{1,0:T(8,128)} %param.20) | copy-start | bytes 442372
  9.8 27.9 %all-to-all-start = ((f32[32,16,128]{2,1,0:T(8,128)}), f32[32,16,128]{2,1,0:T(8,128)S(1)}, u32[]{:S(2)}, u32[]{:S(2)}) async-start(f32[32,16,128]{2,1,0:T(8,128)} %bitcast.1), calls=%async_computation | async-start | bytes 524288 | tf_op jit(solution)/shard_map/all_to_all | solution.py:138
  19.3 18.3 %collective-permute-start = (f32[48,768]{1,0:T(8,128)S(1)}, f32[48,768]{1,0:T(8,128)S(1)}, u32[]{:S(2)}, u32[]{:S(2)}) collective-permute-start(f32[48,768]{1,0:T(8,128)S(1)} %copy-done), channel_id=1, source_target_pairs={{0,4},{1,5},{2,6},{3,7},{4,0},{5,1},{6,2},{7,3},{8,12},{9,13},{10,... | collective-permute-start | bytes 442376 | tf_op jit(solution)/shard_map/ppermute | solution.py:129
  39.6 21.1 %all-to-all-start.1 = ((f32[4,128,768]{2,1,0:T(8,128)}), f32[4,128,768]{2,1,0:T(8,128)S(1)}, u32[]{:S(2)}, u32[]{:S(2)}) async-start(f32[4,128,768]{2,1,0:T(8,128)} %bitcast.6), calls=%async_computation.1 | async-start | bytes 3145728 | tf_op jit(solution)/shard_map/all_to_all | solution.py:73
  44.0 73.3 %all-gather.6.cloned.1.call-start = ((), (), s32[]{:S(2)}) async-start(), calls=%async_computation.13 | async-start | bytes 1327104 | tf_op jit(solution)/shard_map/all_gather | solution.py:95
  93.9 19.1 %collective-permute-start.1 = (f32[32,768]{1,0:T(8,128)S(1)}, f32[32,768]{1,0:T(8,128)S(1)}, u32[]{:S(2)}, u32[]{:S(2)}) collective-permute-start(f32[32,768]{1,0:T(8,128)S(1)} %reduce_sum.91), channel_id=1, source_target_pairs={{0,256},{64,320},{128,384},{192,448},{256,0},{320,64},{384,128},{4... | collective-permute-start | bytes 294920 | tf_op jit(solution)/shard_map/ppermute | solution.py:86
  113.9 10.8 %all-to-all-start.3 = ((f32[4,32,768]{2,1,0:T(8,128)}), f32[4,32,768]{2,1,0:T(8,128)S(1)}, u32[]{:S(2)}, u32[]{:S(2)}) async-start(f32[4,32,768]{2,1,0:T(8,128)} %broadcast_in_dim.26), calls=%async_computation.3 | async-start | bytes 786432 | tf_op jit(solution)/shard_map/all_to_all | solution.py:78
  126.1 10.4 %copy-start.8 = (f32[16,384]{1,0:T(8,128)S(1)}, f32[16,384]{1,0:T(8,128)}, u32[]{:S(2)}) copy-start(f32[16,384]{1,0:T(8,128)} %param.15) | copy-start | bytes 73732
  137.3 10.1 %all-to-all-start.5 = ((f32[8,16,384]{2,1,0:T(8,128)}), f32[8,16,384]{2,1,0:T(8,128)S(1)}, u32[]{:S(2)}, u32[]{:S(2)}) async-start(f32[8,16,384]{2,1,0:T(8,128)} %broadcast_in_dim.27), calls=%async_computation.5 | async-start | bytes 393216 | tf_op jit(solution)/shard_map/all_to_all | solution.py:78
  148.9 39.5 %copy-start.9 = (s32[16]{0:T(128)S(1)}, s32[16]{0:T(128)}, u32[]{:S(2)}) copy-start(s32[16]{0:T(128)} %param.17) | copy-start | bytes 196
  149.0 39.5 %copy-start.10 = (f32[16]{0:T(128)S(1)}, f32[16]{0:T(128)}, u32[]{:S(2)}) copy-start(f32[16]{0:T(128)} %param.19) | copy-start | bytes 196
  149.0 39.5 %copy-start.11 = (f32[16]{0:T(128)S(1)}, f32[16]{0:T(128)}, u32[]{:S(2)}) copy-start(f32[16]{0:T(128)} %param.18) | copy-start | bytes 196
  149.0 11.6 %all-to-all-start.6 = ((f32[4,32,768]{2,1,0:T(8,128)}), f32[4,32,768]{2,1,0:T(8,128)S(1)}, u32[]{:S(2)}, u32[]{:S(2)}) async-start(f32[4,32,768]{2,1,0:T(8,128)} %fusion.21), calls=%async_computation.6 | async-start | bytes 786432 | tf_op jit(solution)/shard_map/all_to_all | solution.py:73
  161.3 27.1 %all-to-all-start.7 = ((f32[64,1,128]{2,1,0:T(1,128)}), f32[64,1,128]{2,1,0:T(1,128)S(1)}, u32[]{:S(2)}, u32[]{:S(2)}) async-start(f32[64,1,128]{2,1,0:T(1,128)} %broadcast_in_dim.31), calls=%async_computation.7 | async-start | bytes 65536 | tf_op jit(solution)/shard_map/all_to_all | solution.py:78
  173.5 72.0 %reduce-scatter.2.cloned.1.call-start = ((), (), s32[]{:S(2)}) async-start(), calls=%async_computation.12 | async-start | bytes 1327104 | tf_op jit(solution)/shard_map/reduce_scatter | solution.py:108
  173.7 17.5 %collective-permute-start.2 = (f32[32,768]{1,0:T(8,128)S(1)}, f32[32,768]{1,0:T(8,128)S(1)}, u32[]{:S(2)}, u32[]{:S(2)}) collective-permute-start(f32[32,768]{1,0:T(8,128)S(1)} %reduce_sum.96), channel_id=1, source_target_pairs={{0,256},{64,320},{128,384},{192,448},{256,0},{320,64},{384,128},{4... | collective-permute-start | bytes 294920 | tf_op jit(solution)/shard_map/ppermute | solution.py:86
  207.1 38.4 %copy-start.1 = (f32[96,384]{1,0:T(8,128)S(1)}, f32[96,384]{1,0:T(8,128)}, u32[]{:S(2)}) copy-start(f32[96,384]{1,0:T(8,128)} %param.21) | copy-start | bytes 442372
  207.1 38.4 %copy-start.5 = (f32[96,384]{1,0:T(8,128)S(1)}, f32[96,384]{1,0:T(8,128)}, u32[]{:S(2)}) copy-start(f32[96,384]{1,0:T(8,128)} %param.27) | copy-start | bytes 442372
  207.1 38.4 %copy-start.6 = (f32[96,384]{1,0:T(8,128)S(1)}, f32[96,384]{1,0:T(8,128)}, u32[]{:S(2)}) copy-start(f32[96,384]{1,0:T(8,128)} %param.23) | copy-start | bytes 442372
  207.1 38.4 %copy-start.7 = (f32[96,384]{1,0:T(8,128)S(1)}, f32[96,384]{1,0:T(8,128)}, u32[]{:S(2)}) copy-start(f32[96,384]{1,0:T(8,128)} %param.25) | copy-start | bytes 442372
  207.1 40.2 %all-to-all-start.9 = ((f32[4,128,768]{2,1,0:T(8,128)}), f32[4,128,768]{2,1,0:T(8,128)S(1)}, u32[]{:S(2)}, u32[]{:S(2)}) async-start(f32[4,128,768]{2,1,0:T(8,128)} %broadcast_in_dim.34), calls=%async_computation.9 | async-start | bytes 3145728 | tf_op jit(solution)/shard_map/all_to_all | solution.py:78
  211.6 112.1 %all-gather.8.cloned.1.call-start = ((), (), s32[]{:S(2)}) async-start(), calls=%async_computation.14 | async-start | bytes 1327104 | tf_op jit(solution)/shard_map/all_gather | solution.py:95
  247.3 17.1 %copy-start.2 = (f32[48,768]{1,0:T(8,128)S(1)}, f32[48,768]{1,0:T(8,128)}, u32[]{:S(2)}) copy-start(f32[48,768]{1,0:T(8,128)} %param.26) | copy-start | bytes 442372
  247.3 17.1 %copy-start.3 = (f32[48,768]{1,0:T(8,128)S(1)}, f32[48,768]{1,0:T(8,128)}, u32[]{:S(2)}) copy-start(f32[48,768]{1,0:T(8,128)} %param.22) | copy-start | bytes 442372
  247.3 17.0 %copy-start.4 = (f32[48,768]{1,0:T(8,128)S(1)}, f32[48,768]{1,0:T(8,128)}, u32[]{:S(2)}) copy-start(f32[48,768]{1,0:T(8,128)} %param.24) | copy-start | bytes 442372
  248.0 16.4 %collective-permute-start.3 = (f32[48,768]{1,0:T(8,128)S(1)}, f32[48,768]{1,0:T(8,128)S(1)}, u32[]{:S(2)}, u32[]{:S(2)}) collective-permute-start(f32[48,768]{1,0:T(8,128)S(1)} %slice_select_fusion), channel_id=1, source_target_pairs={{0,4},{1,5},{2,6},{3,7},{4,0},{5,1},{6,2},{7,3},{8,12},{9,13},{10,... | collective-permute-start | bytes 442376 | tf_op jit(solution)/shard_map/ppermute | solution.py:153
  265.9 56.6 %all-to-all-start.10 = ((f32[8,8,768]{2,1,0:T(8,128)}), f32[8,8,768]{2,1,0:T(8,128)S(1)}, u32[]{:S(2)}, u32[]{:S(2)}) async-start(f32[8,8,768]{2,1,0:T(8,128)} %broadcast_in_dim.35), calls=%async_computation.10 | async-start | bytes 393216 | tf_op jit(solution)/shard_map/all_to_all | solution.py:78
Sparse Core Ops, SparseCore 0:
  46.9 64.1 all-gather.5
  191.5 53.9 reduce-scatter.1
  247.6 60.8 all-gather.7

commit v5 on v2

--- a/solution.py
+++ b/solution.py
@@ -79,6 +79,17 @@
 
 def y_sum(part):
     return scatter_sum(part, "inp", 4, QUADS)
+
+
+def y_sum_hops(part):
+    blocks = part.reshape(4, part.shape[0] // 4, part.shape[1])
+    y = lax.rem(lax.axis_index("inp"), 4)
+    total = lax.dynamic_index_in_dim(blocks, y, axis=0, keepdims=False)
+    for step in (1, 3, 2):
+        sent = lax.dynamic_index_in_dim(blocks, lax.rem(y + step, 4), axis=0, keepdims=False)
+        pairs = [(i, (i // 4) * 4 + (i % 4 + step) % 4) for i in range(8)]
+        total = total + lax.ppermute(sent, "inp", pairs)
+    return total
 
 
 def far_sum(quarter):
@@ -192,10 +203,9 @@
     leading = lax.axis_index("inp") == 0
     local_counts = jnp.sum(onehot, axis=0) * jnp.where(leading, 1.0, 0.0)
     stats = jnp.concatenate([local_sq, local_counts, jnp.zeros((96,), jnp.float32)])[None, :]
-    d_quarter = y_sum(product(error, w_out_block, 1, 1))
-    stats, d_quarter = lax.optimization_barrier((stats, d_quarter))
-    stats = jnp.sum(spread(stats, ("inp", "tok"), 64), axis=(0, 1))
-    d_active = far_sum(d_quarter)
+    stats = spread(stats, ("inp", "tok"), 64)
+    stats = jnp.sum(stats, axis=(0, 1))
+    d_quarter = y_sum_hops(product(error, w_out_block, 1, 1))
     loss, sample_coef = kto_terms(
         stats[:SAMPLES], stats[SAMPLES : 2 * SAMPLES], labels, utility, ref_loss
     )
@@ -204,9 +214,9 @@
     own_coef = lax.dynamic_slice(coef, (own_rows, 0), (32, 1))
 
     grad_fold = fold_rows(product(active, error * coef, 0, 0))
-    d_rows = d_active * own_coef * slope_rows
-    grad_fold, d_rows = lax.optimization_barrier((grad_fold, d_rows))
+    grad_fold, d_quarter = lax.optimization_barrier((grad_fold, d_quarter))
     grad_out = queue_scatter(grad_fold)
+    d_rows = far_sum(d_quarter) * own_coef * slope_rows
     grad_in, grad_out = half_sum(product(columns, quad_rows(d_rows), 0, 0), grad_out)
 
     weight_out, new_m_out, new_v_out, new_e_out = adamw(w_out, m_out, v_out, e_out, grad_out)

time: 346 us -> 352 us (1.017)
  waiting for transfers between devices: 109 us -> 120 us
    ppermute x2, waiting for transfers between devices: 7.58 us -> 21.4 us  [far_sum(): return quarter + lax.ppermute(quarter, 'inp', FAR_HALF)]
    all_to_all x6, waiting for transfers between devices: 27.5 us -> 39.6 us  [spread(): return lax.all_to_all(copies, axis, 0, 0, axis_index_groups=groups)]
    ppermute x2, starting transfers between devices: 25.6 us -> 15.9 us  [far_sum(): return quarter + lax.ppermute(quarter, 'inp', FAR_HALF)]
    ppermute x0 -> x3, starting transfers between devices: none -> 8.97 us  [y_sum_hops(): total = total + lax.ppermute(sent, 'inp', pairs)]
    all_to_all x2 -> x1, waiting for transfers between devices: 27.5 us -> 19.6 us  [scatter_sum(): lax.all_to_all(blocks, axis, 0, 0, axis_index_groups=groups)]
    reduce_scatter x1, waiting for transfers between devices: 27.7 us -> 21 us  [queue_scatter(): lax.psum_scatter(folded, 'tok', scatter_dimension=0, tiled=True, axis_ind...]
    all_to_all x2 -> x1, starting transfers between devices: 8.05 us -> 4.46 us  [scatter_sum(): lax.all_to_all(blocks, axis, 0, 0, axis_index_groups=groups)]
  transfers between devices with their start and end apart: 16 -> 18, of which waited for: 12 -> 11; matrix products, arithmetic and copies ran while one was open for 3% -> 3% of each run, Pallas kernels for 0% -> 0%
where the time goes in v5:
time: 352 us; the launch traced here: 351 us
  waiting for transfers between devices  120 us (34%)
  blocking collectives  100 us (28%)
  starting transfers between devices  91.5 us (26%)
  between operations  16 us (5%)
  local copies, waits for them, and re-layouts  10.4 us (3%)
  other arithmetic  8.01 us (2%)
  matrix products  4.3 us (1%)
    all_gather x1, blocking collectives, core_gather(): lax.all_gather(shard[:split], 'tok', axis=0, tiled=False, axis_index_grou...  52 us
    all_to_all x6, starting transfers between devices, spread(): return lax.all_to_all(copies, axis, 0, 0, axis_index_groups=groups)  41.8 us
    all_to_all x6, waiting for transfers between devices, spread(): return lax.all_to_all(copies, axis, 0, 0, axis_index_groups=groups)  39.6 us
    all_to_all x2, blocking collectives, scatter_sum(): lax.all_to_all(blocks, axis, 0, 0, axis_index_groups=groups)  31.8 us
    ppermute x2, waiting for transfers between devices, far_sum(): return quarter + lax.ppermute(quarter, 'inp', FAR_HALF)  21.4 us
    reduce_scatter x1, waiting for transfers between devices, queue_scatter(): lax.psum_scatter(folded, 'tok', scatter_dimension=0, tiled=True, axis_ind...  21 us
    all_to_all x1, waiting for transfers between devices, scatter_sum(): lax.all_to_all(blocks, axis, 0, 0, axis_index_groups=groups)  19.6 us
    all_to_all x1, blocking collectives, spread(): return lax.all_to_all(copies, axis, 0, 0, axis_index_groups=groups)  16.1 us
  transfers between devices with their start and end apart: 18, of which 11 were waited for; matrix products, arithmetic and copies ran while one was open for 3% of the time, Pallas kernels for 0%

profile of v5, /device:TPU:6, one launch (start us, length us, event | category | flops | bytes accessed | tf_op | source)
XLA Modules:
  0.0 350.5 jit_solution(57014880530396862)
XLA Ops:
  7.2 9.2 %collective-permute-start = (f32[48,768]{1,0:T(8,128)}, f32[48,768]{1,0:T(8,128)S(1)}, u32[]{:S(2)}, u32[]{:S(2)}) collective-permute-start(f32[48,768]{1,0:T(8,128)} %param.20), channel_id=1, source_target_pairs={{0,4},{1,5},{2,6},{3,7},{4,0},{5,1},{6,2},{7,3},{8,12},{9,13},{10,... | collective-permute-start | bytes 442376 | tf_op jit(solution)/shard_map/ppermute | solution.py:139
  16.4 0.8 reshape.90
  17.3 0.1 reshape.91
  17.4 0.7 convert_element_type.20
  18.1 0.7 pad_maximum_fusion.5
  18.8 5.9 %all-to-all-start = ((f32[4,16,128]{2,1,0:T(8,128)}), f32[4,16,128]{2,1,0:T(8,128)S(1)}, u32[]{:S(2)}, u32[]{:S(2)}) async-start(f32[4,16,128]{2,1,0:T(8,128)} %pad_maximum_fusion.5), calls=%async_computation | async-start | bytes 65536 | tf_op jit(solution)/shard_map/all_to_all | solution.py:147
  24.7 5.9 %all-to-all-done = f32[4,16,128]{2,1,0:T(8,128)S(1)} async-done(((f32[4,16,128]{2,1,0:T(8,128)}), f32[4,16,128]{2,1,0:T(8,128)S(1)}, u32[]{:S(2)}, u32[]{:S(2)}) %all-to-all-start) | async-done | bytes 32800 | tf_op jit(solution)/shard_map/all_to_all | solution.py:147
  30.6 0.7 broadcast_in_dim.21
  31.4 4.8 %all-to-all-start.1 = ((f32[8,4,16,128]{3,2,1,0:T(8,128)}), f32[8,4,16,128]{3,2,1,0:T(8,128)S(1)}, u32[]{:S(2)}, u32[]{:S(2)}) async-start(f32[8,4,16,128]{3,2,1,0:T(8,128)} %broadcast_in_dim.21), calls=%async_computation.1 | async-start | bytes 524288 | tf_op jit(solution)/shard_map/all_to_all | solution.py:77
  36.2 5.4 %all-to-all-done.1 = f32[8,4,16,128]{3,2,1,0:T(8,128)S(1)} async-done(((f32[8,4,16,128]{3,2,1,0:T(8,128)}), f32[8,4,16,128]{3,2,1,0:T(8,128)S(1)}, u32[]{:S(2)}, u32[]{:S(2)}) %all-to-all-start.1) | async-done | bytes 262176 | tf_op jit(solution)/shard_map/all_to_all | solution.py:77
  41.6 1.9 fusion
  43.6 4.5 %all-to-all-start.2 = ((f32[4,128,768]{2,1,0:T(8,128)}), f32[4,128,768]{2,1,0:T(8,128)S(1)}, u32[]{:S(2)}, u32[]{:S(2)}) async-start(f32[4,128,768]{2,1,0:T(8,128)} %bitcast.5), calls=%async_computation.2 | async-start | bytes 3145728 | tf_op jit(solution)/shard_map/all_to_all | solution.py:72
  48.0 0.7 all-gather.6.cloned.1.call-update
  48.7 19.6 %all-to-all-done.2 = f32[4,128,768]{2,1,0:T(8,128)S(1)} async-done(((f32[4,128,768]{2,1,0:T(8,128)}), f32[4,128,768]{2,1,0:T(8,128)S(1)}, u32[]{:S(2)}, u32[]{:S(2)}) %all-to-all-start.2) | async-done | bytes 1572896 | tf_op jit(solution)/shard_map/all_to_all | solution.py:72
  68.4 0.1 reduce_sum.81
  68.5 22.8 %all_to_all.55 = f32[4,32,768]{2,1,0:T(8,128)S(1)} all-to-all(f32[4,32,768]{2,1,0:T(8,128)S(1)} %bitcast.87), channel_id=1, replica_groups={{0,1,2,3},{4,5,6,7},{8,9,10,11},{12,13,14,15},{16,17,18,19},{20,21,22,2..., dimensions={0} | all-to-all | bytes 786432 | tf_op jit(solution)/shard_map/all_to_all | solution.py:72
  91.3 13.3 %collective-permute-start.1 = (f32[32,768]{1,0:T(8,128)S(1)}, f32[32,768]{1,0:T(8,128)S(1)}, u32[]{:S(2)}, u32[]{:S(2)}) collective-permute-start(f32[32,768]{1,0:T(8,128)S(1)} %reduce_sum.82), channel_id=1, source_target_pairs={{0,256},{64,320},{128,384},{192,448},{256,0},{320,64},{384,128},{4... | collective-permute-start | bytes 294920 | tf_op jit(solution)/shard_map/ppermute | solution.py:96
  104.6 7.1 %collective-permute-done.1 = f32[32,768]{1,0:T(8,128)S(1)} collective-permute-done((f32[32,768]{1,0:T(8,128)S(1)}, f32[32,768]{1,0:T(8,128)S(1)}, u32[]{:S(2)}, u32[]{:S(2)}) %collective-permute-start.1) | collective-permute-done | bytes 98336 | tf_op jit(solution)/shard_map/ppermute | solution.py:96
  111.8 0.8 broadcast_in_dim.22
  112.6 3.5 all-to-all-start.4
  116.1 7.3 %all-to-all-done.4 = f32[4,32,768]{2,1,0:T(8,128)S(1)} async-done(((f32[4,32,768]{2,1,0:T(8,128)}), f32[4,32,768]{2,1,0:T(8,128)S(1)}, u32[]{:S(2)}, u32[]{:S(2)}) %all-to-all-start.4) | async-done | bytes 393248 | tf_op jit(solution)/shard_map/all_to_all | solution.py:77
  123.4 1.3 slice_bitcast_fusion.2
  124.9 0.5 fusion.22
  125.4 9.0 %all_to_all.56 = f32[8,16,384]{2,1,0:T(8,128)S(1)} all-to-all(f32[8,16,384]{2,1,0:T(8,128)S(1)} %fusion.22), channel_id=1, replica_groups=mesh['inp'=8,'hid'=8,'tok'=8] {'hid'}, dimensions={0} | all-to-all | bytes 393216 | tf_op jit(solution)/shard_map/all_to_all | solution.py:72
  134.5 0.7 broadcast_in_dim.23
  135.2 5.4 %all-to-all-start.6 = ((f32[8,16,384]{2,1,0:T(8,128)}), f32[8,16,384]{2,1,0:T(8,128)S(1)}, u32[]{:S(2)}, u32[]{:S(2)}) async-start(f32[8,16,384]{2,1,0:T(8,128)} %broadcast_in_dim.23), calls=%async_computation.6 | async-start | bytes 393216 | tf_op jit(solution)/shard_map/all_to_all | solution.py:77
  140.6 0.2 slice_reduce_fusion
  141.0 0.2 copy.52
  141.2 4.1 %all-to-all-done.6 = f32[8,16,384]{2,1,0:T(8,128)S(1)} async-done(((f32[8,16,384]{2,1,0:T(8,128)}), f32[8,16,384]{2,1,0:T(8,128)S(1)}, u32[]{:S(2)}, u32[]{:S(2)}) %all-to-all-start.6) | async-done | bytes 196640 | tf_op jit(solution)/shard_map/all_to_all | solution.py:77
  145.3 0.6 fusion.24
  146.0 2.5 collective-permute-start.2
  148.5 4.6 %collective-permute-start.3 = (f32[32,768]{1,0:T(8,128)S(1)}, f32[32,768]{1,0:T(8,128)S(1)}, u32[]{:S(2)}, u32[]{:S(2)}) collective-permute-start(f32[32,768]{1,0:T(8,128)S(1)} %get-tuple-element.43), channel_id=1, source_target_pairs={{0,192},{64,0},{128,64},{192,128},{256,448},{320,256},{384,320},{4... | collective-permute-start | bytes 294920 | tf_op jit(solution)/shard_map/ppermute | solution.py:91
  153.0 1.9 collective-permute-start.4
  155.0 0.1 multiply_reduce_fusion
  155.1 0.1 select_reduce_fusion.1
  155.4 0.6 broadcast_in_dim.25
  156.0 17.7 %all-to-all-start.7 = ((f32[64,1,128]{2,1,0:T(1,128)}), f32[64,1,128]{2,1,0:T(1,128)S(1)}, u32[]{:S(2)}, u32[]{:S(2)}) async-start(f32[64,1,128]{2,1,0:T(1,128)} %broadcast_in_dim.25), calls=%async_computation.7 | async-start | bytes 65536 | tf_op jit(solution)/shard_map/all_to_all | solution.py:77
  173.8 14.6 %all-to-all-done.7 = f32[64,1,128]{2,1,0:T(1,128)S(1)} async-done(((f32[64,1,128]{2,1,0:T(1,128)}), f32[64,1,128]{2,1,0:T(1,128)S(1)}, u32[]{:S(2)}, u32[]{:S(2)}) %all-to-all-start.7) | async-done | bytes 32800 | tf_op jit(solution)/shard_map/all_to_all | solution.py:77
  188.4 0.1 multiply_divide_fusion
  188.5 0.1 select_reduce_fusion
  188.7 0.1 broadcast_multiply_fusion
  188.8 0.6 fusion.23
  189.6 1.1 pad_maximum_fusion.1
  190.7 2.6 collective-permute-start.5
  193.3 14.3 %collective-permute-done.5 = f32[32,768]{1,0:T(8,128)S(1)} collective-permute-done((f32[32,768]{1,0:T(8,128)S(1)}, f32[32,768]{1,0:T(8,128)S(1)}, u32[]{:S(2)}, u32[]{:S(2)}) %collective-permute-start.5) | collective-permute-done | bytes 98336 | tf_op jit(solution)/shard_map/ppermute | solution.py:96
  207.7 0.8 broadcast_in_dim.26
  208.5 5.3 %all-to-all-start.8 = ((f32[4,32,768]{2,1,0:T(8,128)}), f32[4,32,768]{2,1,0:T(8,128)S(1)}, u32[]{:S(2)}, u32[]{:S(2)}) async-start(f32[4,32,768]{2,1,0:T(8,128)} %broadcast_in_dim.26), calls=%async_computation.8 | async-start | bytes 786432 | tf_op jit(solution)/shard_map/all_to_all | solution.py:77
  213.8 0.7 reduce-scatter.2.cloned.1.call-update
  214.6 8.1 %all-to-all-done.8 = f32[4,32,768]{2,1,0:T(8,128)S(1)} async-done(((f32[4,32,768]{2,1,0:T(8,128)}), f32[4,32,768]{2,1,0:T(8,128)S(1)}, u32[]{:S(2)}, u32[]{:S(2)}) %all-to-all-start.8) | async-done | bytes 393248 | tf_op jit(solution)/shard_map/all_to_all | solution.py:77
  222.7 0.1 broadcast_in_dim.28
  222.8 16.1 %all_to_all.57 = f32[4,128,768]{2,1,0:T(8,128)S(1)} all-to-all(f32[4,128,768]{2,1,0:T(8,128)S(1)} %broadcast_in_dim.28), channel_id=1, replica_groups={{0,64,128,192},{256,320,384,448},{1,65,129,193},{257,321,385,449},{2,66..., dimensions={0} | all-to-all | bytes 3145728 | tf_op jit(solution)/shard_map/all_to_all | solution.py:77
  238.9 0.6 fusion.4
  239.6 21.0 %reduce-scatter.2.cloned.1.call-done = f32[96,384]{1,0:T(8,128)} async-done(((f32[768,384]{1,0:T(8,128)}), f32[96,384]{1,0:T(8,128)}) %reduce-scatter.2.cloned.1.call-update) | async-done | bytes 147472 | tf_op jit(solution)/shard_map/reduce_scatter | solution.py:118
  260.6 1.8 multiply_add_fusion.1
  262.4 5.2 %collective-permute-start.6 = (f32[48,768]{1,0:T(8,128)S(1)}, f32[48,768]{1,0:T(8,128)S(1)}, u32[]{:S(2)}, u32[]{:S(2)}) collective-permute-start(f32[48,768]{1,0:T(8,128)S(1)} %get-tuple-element.44), channel_id=1, source_target_pairs={{0,4},{1,5},{2,6},{3,7},{4,0},{5,1},{6,2},{7,3},{8,12},{9,13},{10,... | collective-permute-start | bytes 442376 | tf_op jit(solution)/shard_map/ppermute | solution.py:163
  267.6 0.6 multiply_reduce_fusion.1
  268.9 11.4 %collective-permute-done.6 = f32[48,768]{1,0:T(8,128)S(1)} collective-permute-done((f32[48,768]{1,0:T(8,128)S(1)}, f32[48,768]{1,0:T(8,128)S(1)}, u32[]{:S(2)}, u32[]{:S(2)}) %collective-permute-start.6) | collective-permute-done | bytes 147488 | tf_op jit(solution)/shard_map/ppermute | solution.py:163
  280.3 0.8 multiply_add_fusion.2
  281.1 0.7 broadcast_in_dim.29
  281.8 5.2 %all-to-all-start.10 = ((f32[8,8,768]{2,1,0:T(8,128)}), f32[8,8,768]{2,1,0:T(8,128)S(1)}, u32[]{:S(2)}, u32[]{:S(2)}) async-start(f32[8,8,768]{2,1,0:T(8,128)} %broadcast_in_dim.29), calls=%async_computation.11 | async-start | bytes 393216 | tf_op jit(solution)/shard_map/all_to_all | solution.py:77
  287.0 52.0 %all-gather.1 = f32[320,768]{1,0:T(8,128)S(1)} all-gather(f32[40,768]{1,0:T(8,128)S(1)} %slice.76), channel_id=3, replica_groups={{0,2,4,6,7,5,3,1},{8,10,12,14,15,13,11,9},{16,18,20,22,23,21,19,17},{24..., dimensions={0}, use_global_device_ids=true | all-gather | bytes 1105920 | tf_op jit(solution)/shard_map/all_gather | solution.py:130
  339.2 1.1 pad_maximum_fusion.2
  340.3 1.3 fusion.20
  341.8 1.1 copy.55
  (68 shorter events, 1.6 us)
Async XLA Ops:
  7.2 29.0 %copy-start = (f32[48,768]{1,0:T(8,128)S(1)}, f32[48,768]{1,0:T(8,128)}, u32[]{:S(2)}) copy-start(f32[48,768]{1,0:T(8,128)} %param.20) | copy-start | bytes 442372
  7.2 29.0 %collective-permute-start = (f32[48,768]{1,0:T(8,128)}, f32[48,768]{1,0:T(8,128)S(1)}, u32[]{:S(2)}, u32[]{:S(2)}) collective-permute-start(f32[48,768]{1,0:T(8,128)} %param.20), channel_id=1, source_target_pairs={{0,4},{1,5},{2,6},{3,7},{4,0},{5,1},{6,2},{7,3},{8,12},{9,13},{10,... | collective-permute-start | bytes 442376 | tf_op jit(solution)/shard_map/ppermute | solution.py:139
  18.8 11.8 %all-to-all-start = ((f32[4,16,128]{2,1,0:T(8,128)}), f32[4,16,128]{2,1,0:T(8,128)S(1)}, u32[]{:S(2)}, u32[]{:S(2)}) async-start(f32[4,16,128]{2,1,0:T(8,128)} %pad_maximum_fusion.5), calls=%async_computation | async-start | bytes 65536 | tf_op jit(solution)/shard_map/all_to_all | solution.py:147
  31.4 10.2 %all-to-all-start.1 = ((f32[8,4,16,128]{3,2,1,0:T(8,128)}), f32[8,4,16,128]{3,2,1,0:T(8,128)S(1)}, u32[]{:S(2)}, u32[]{:S(2)}) async-start(f32[8,4,16,128]{3,2,1,0:T(8,128)} %broadcast_in_dim.21), calls=%async_computation.1 | async-start | bytes 524288 | tf_op jit(solution)/shard_map/all_to_all | solution.py:77
  43.6 24.8 %all-to-all-start.2 = ((f32[4,128,768]{2,1,0:T(8,128)}), f32[4,128,768]{2,1,0:T(8,128)S(1)}, u32[]{:S(2)}, u32[]{:S(2)}) async-start(f32[4,128,768]{2,1,0:T(8,128)} %bitcast.5), calls=%async_computation.2 | async-start | bytes 3145728 | tf_op jit(solution)/shard_map/all_to_all | solution.py:72
  48.0 68.1 %all-gather.6.cloned.1.call-start = ((), (), s32[]{:S(2)}) async-start(), calls=%async_computation.13 | async-start | bytes 1327104 | tf_op jit(solution)/shard_map/all_gather | solution.py:105
  91.3 20.5 %collective-permute-start.1 = (f32[32,768]{1,0:T(8,128)S(1)}, f32[32,768]{1,0:T(8,128)S(1)}, u32[]{:S(2)}, u32[]{:S(2)}) collective-permute-start(f32[32,768]{1,0:T(8,128)S(1)} %reduce_sum.82), channel_id=1, source_target_pairs={{0,256},{64,320},{128,384},{192,448},{256,0},{320,64},{384,128},{4... | collective-permute-start | bytes 294920 | tf_op jit(solution)/shard_map/ppermute | solution.py:96
  112.6 10.8 %all-to-all-start.4 = ((f32[4,32,768]{2,1,0:T(8,128)}), f32[4,32,768]{2,1,0:T(8,128)S(1)}, u32[]{:S(2)}, u32[]{:S(2)}) async-start(f32[4,32,768]{2,1,0:T(8,128)} %broadcast_in_dim.22), calls=%async_computation.4 | async-start | bytes 786432 | tf_op jit(solution)/shard_map/all_to_all | solution.py:77
  124.9 9.6 %copy-start.8 = (f32[16,384]{1,0:T(8,128)S(1)}, f32[16,384]{1,0:T(8,128)}, u32[]{:S(2)}) copy-start(f32[16,384]{1,0:T(8,128)} %param.15) | copy-start | bytes 73732
  135.2 10.1 %all-to-all-start.6 = ((f32[8,16,384]{2,1,0:T(8,128)}), f32[8,16,384]{2,1,0:T(8,128)S(1)}, u32[]{:S(2)}, u32[]{:S(2)}) async-start(f32[8,16,384]{2,1,0:T(8,128)} %broadcast_in_dim.23), calls=%async_computation.6 | async-start | bytes 393216 | tf_op jit(solution)/shard_map/all_to_all | solution.py:77
  145.3 43.1 %copy-start.9 = (s32[16]{0:T(128)S(1)}, s32[16]{0:T(128)}, u32[]{:S(2)}) copy-start(s32[16]{0:T(128)} %param.17) | copy-start | bytes 196
  145.3 43.1 %copy-start.10 = (f32[16]{0:T(128)S(1)}, f32[16]{0:T(128)}, u32[]{:S(2)}) copy-start(f32[16]{0:T(128)} %param.19) | copy-start | bytes 196
  145.3 43.1 %copy-start.11 = (f32[16]{0:T(128)S(1)}, f32[16]{0:T(128)}, u32[]{:S(2)}) copy-start(f32[16]{0:T(128)} %param.18) | copy-start | bytes 196
  146.0 27.7 %collective-permute-start.2 = (f32[32,768]{1,0:T(8,128)S(1)}, f32[32,768]{1,0:T(8,128)S(1)}, u32[]{:S(2)}, u32[]{:S(2)}) collective-permute-start(f32[32,768]{1,0:T(8,128)S(1)} %get-tuple-element.41), channel_id=1, source_target_pairs={{0,64},{64,128},{128,192},{192,0},{256,320},{320,384},{384,448},{4... | collective-permute-start | bytes 294920 | tf_op jit(solution)/shard_map/ppermute | solution.py:91
  148.5 25.2 %collective-permute-start.3 = (f32[32,768]{1,0:T(8,128)S(1)}, f32[32,768]{1,0:T(8,128)S(1)}, u32[]{:S(2)}, u32[]{:S(2)}) collective-permute-start(f32[32,768]{1,0:T(8,128)S(1)} %get-tuple-element.43), channel_id=1, source_target_pairs={{0,192},{64,0},{128,64},{192,128},{256,448},{320,256},{384,320},{4... | collective-permute-start | bytes 294920 | tf_op jit(solution)/shard_map/ppermute | solution.py:91
  153.0 20.7 %collective-permute-start.4 = (f32[32,768]{1,0:T(8,128)S(1)}, f32[32,768]{1,0:T(8,128)S(1)}, u32[]{:S(2)}, u32[]{:S(2)}) collective-permute-start(f32[32,768]{1,0:T(8,128)S(1)} %get-tuple-element.42), channel_id=1, source_target_pairs={{0,128},{64,192},{128,0},{192,64},{256,384},{320,448},{384,256},{4... | collective-permute-start | bytes 294920 | tf_op jit(solution)/shard_map/ppermute | solution.py:91
  156.0 32.4 %all-to-all-start.7 = ((f32[64,1,128]{2,1,0:T(1,128)}), f32[64,1,128]{2,1,0:T(1,128)S(1)}, u32[]{:S(2)}, u32[]{:S(2)}) async-start(f32[64,1,128]{2,1,0:T(1,128)} %broadcast_in_dim.25), calls=%async_computation.7 | async-start | bytes 65536 | tf_op jit(solution)/shard_map/all_to_all | solution.py:77
  190.7 17.0 %collective-permute-start.5 = (f32[32,768]{1,0:T(8,128)S(1)}, f32[32,768]{1,0:T(8,128)S(1)}, u32[]{:S(2)}, u32[]{:S(2)}) collective-permute-start(f32[32,768]{1,0:T(8,128)S(1)} %fusion.16), channel_id=1, source_target_pairs={{0,256},{64,320},{128,384},{192,448},{256,0},{320,64},{384,128},{4... | collective-permute-start | bytes 294920 | tf_op jit(solution)/shard_map/ppermute | solution.py:96
  208.5 14.2 %all-to-all-start.8 = ((f32[4,32,768]{2,1,0:T(8,128)}), f32[4,32,768]{2,1,0:T(8,128)S(1)}, u32[]{:S(2)}, u32[]{:S(2)}) async-start(f32[4,32,768]{2,1,0:T(8,128)} %broadcast_in_dim.26), calls=%async_computation.8 | async-start | bytes 786432 | tf_op jit(solution)/shard_map/all_to_all | solution.py:77
  213.8 46.8 %reduce-scatter.2.cloned.1.call-start = ((), (), s32[]{:S(2)}) async-start(), calls=%async_computation.12 | async-start | bytes 1327104 | tf_op jit(solution)/shard_map/reduce_scatter | solution.py:118
  214.5 125.8 %all-gather.8.cloned.1.call-start = ((), (), s32[]{:S(2)}) async-start(), calls=%async_computation.14 | async-start | bytes 1327104 | tf_op jit(solution)/shard_map/all_gather | solution.py:105
  238.9 21.7 %copy-start.1 = (f32[96,384]{1,0:T(8,128)S(1)}, f32[96,384]{1,0:T(8,128)}, u32[]{:S(2)}) copy-start(f32[96,384]{1,0:T(8,128)} %param.21) | copy-start | bytes 442372
  238.9 21.7 %copy-start.5 = (f32[96,384]{1,0:T(8,128)S(1)}, f32[96,384]{1,0:T(8,128)}, u32[]{:S(2)}) copy-start(f32[96,384]{1,0:T(8,128)} %param.27) | copy-start | bytes 442372
  238.9 21.7 %copy-start.6 = (f32[96,384]{1,0:T(8,128)S(1)}, f32[96,384]{1,0:T(8,128)}, u32[]{:S(2)}) copy-start(f32[96,384]{1,0:T(8,128)} %param.23) | copy-start | bytes 442372
  238.9 21.7 %copy-start.7 = (f32[96,384]{1,0:T(8,128)S(1)}, f32[96,384]{1,0:T(8,128)}, u32[]{:S(2)}) copy-start(f32[96,384]{1,0:T(8,128)} %param.25) | copy-start | bytes 442372
  239.5 40.7 %copy-start.2 = (f32[48,768]{1,0:T(8,128)S(1)}, f32[48,768]{1,0:T(8,128)}, u32[]{:S(2)}) copy-start(f32[48,768]{1,0:T(8,128)} %param.26) | copy-start | bytes 442372
  239.6 40.7 %copy-start.3 = (f32[48,768]{1,0:T(8,128)S(1)}, f32[48,768]{1,0:T(8,128)}, u32[]{:S(2)}) copy-start(f32[48,768]{1,0:T(8,128)} %param.22) | copy-start | bytes 442372
  239.6 40.7 %copy-start.4 = (f32[48,768]{1,0:T(8,128)S(1)}, f32[48,768]{1,0:T(8,128)}, u32[]{:S(2)}) copy-start(f32[48,768]{1,0:T(8,128)} %param.24) | copy-start | bytes 442372
  262.4 17.8 %collective-permute-start.6 = (f32[48,768]{1,0:T(8,128)S(1)}, f32[48,768]{1,0:T(8,128)S(1)}, u32[]{:S(2)}, u32[]{:S(2)}) collective-permute-start(f32[48,768]{1,0:T(8,128)S(1)} %get-tuple-element.44), channel_id=1, source_target_pairs={{0,4},{1,5},{2,6},{3,7},{4,0},{5,1},{6,2},{7,3},{8,12},{9,13},{10,... | collective-permute-start | bytes 442376 | tf_op jit(solution)/shard_map/ppermute | solution.py:163
  281.8 57.3 %all-to-all-start.10 = ((f32[8,8,768]{2,1,0:T(8,128)}), f32[8,8,768]{2,1,0:T(8,128)S(1)}, u32[]{:S(2)}, u32[]{:S(2)}) async-start(f32[8,8,768]{2,1,0:T(8,128)} %broadcast_in_dim.29), calls=%async_computation.11 | async-start | bytes 393216 | tf_op jit(solution)/shard_map/all_to_all | solution.py:77
Sparse Core Ops, SparseCore 0:
  50.9 64.2 all-gather.5
  218.0 42.5 reduce-scatter.1
  262.7 61.6 all-gather.7

commit v6 on v5

--- a/solution.py
+++ b/solution.py
@@ -154,14 +154,13 @@
     return spread(near, "inp", 4, QUADS).reshape(512, 768)
 
 
-def half_sum(pair, partner):
+def half_sum(pair):
     upper = lax.axis_index("tok") >= 4
     rows = pair.shape[0] // 2
     keep = jnp.where(upper, pair[rows:], pair[:rows])
     send = jnp.where(upper, pair[:rows], pair[rows:])
-    keep, partner = lax.optimization_barrier((keep, partner))
     other = lax.ppermute(send, "tok", FAR_HALF)
-    return keep + other, partner
+    return keep + other
 
 
 def on_device(
@@ -217,12 +216,13 @@
     grad_fold, d_quarter = lax.optimization_barrier((grad_fold, d_quarter))
     grad_out = queue_scatter(grad_fold)
     d_rows = far_sum(d_quarter) * own_coef * slope_rows
-    grad_in, grad_out = half_sum(product(columns, quad_rows(d_rows), 0, 0), grad_out)
+    d_hidden, grad_out = lax.optimization_barrier((quad_rows(d_rows), grad_out))
+    grad_in = half_sum(product(columns, d_hidden, 0, 0))
 
     weight_out, new_m_out, new_v_out, new_e_out = adamw(w_out, m_out, v_out, e_out, grad_out)
-    new_w_out, _ = queue_gather(weight_out)
+    new_w_out = core_gather(weight_out, 80)
     weight_in, new_m_in, new_v_in, new_e_in = adamw(w_in, m_in, v_in, e_in, grad_in)
-    new_w_in = core_gather(weight_in, 40)
+    new_w_in, _ = queue_gather(weight_in)
     return (
         loss,
         new_w_in,

time: 352 us -> 356 us (1.011)
  blocking collectives: 100 us -> 86.5 us
  waiting for transfers between devices: 120 us -> 132 us
  starting transfers between devices: 91.5 us -> 96.4 us
    all_to_all x1 -> x0, blocking collectives: 16.1 us -> none  [spread(): return lax.all_to_all(copies, axis, 0, 0, axis_index_groups=groups)]
    reduce_scatter x1, waiting for transfers between devices: 21 us -> 32.6 us  [queue_scatter(): lax.psum_scatter(folded, 'tok', scatter_dimension=0, tiled=True, axis_ind...]
    all_to_all x6 -> x7, starting transfers between devices: 41.8 us -> 46.4 us  [spread(): return lax.all_to_all(copies, axis, 0, 0, axis_index_groups=groups)]
    all_to_all x6 -> x7, waiting for transfers between devices: 39.6 us -> 39.6 us  [spread(): return lax.all_to_all(copies, axis, 0, 0, axis_index_groups=groups)]
  transfers between devices with their start and end apart: 18 -> 19, of which waited for: 11 -> 11; matrix products, arithmetic and copies ran while one was open for 3% -> 3% of each run, Pallas kernels for 0% -> 0%
where the time goes in v6:
time: 356 us; the launch traced here: 354 us
  waiting for transfers between devices  132 us (37%)
  starting transfers between devices  96.4 us (27%)
  blocking collectives  86.5 us (24%)
  between operations  16 us (4%)
  local copies, waits for them, and re-layouts  11.6 us (3%)
  other arithmetic  7.07 us (2%)
  matrix products  4.29 us (1%)
    all_gather x1, blocking collectives, core_gather(): lax.all_gather(shard[:split], 'tok', axis=0, tiled=False, axis_index_grou...  54.6 us
    all_to_all x7, starting transfers between devices, spread(): return lax.all_to_all(copies, axis, 0, 0, axis_index_groups=groups)  46.4 us
    all_to_all x7, waiting for transfers between devices, spread(): return lax.all_to_all(copies, axis, 0, 0, axis_index_groups=groups)  39.6 us
    reduce_scatter x1, waiting for transfers between devices, queue_scatter(): lax.psum_scatter(folded, 'tok', scatter_dimension=0, tiled=True, axis_ind...  32.6 us
    all_to_all x2, blocking collectives, scatter_sum(): lax.all_to_all(blocks, axis, 0, 0, axis_index_groups=groups)  31.8 us
    ppermute x2, waiting for transfers between devices, far_sum(): return quarter + lax.ppermute(quarter, 'inp', FAR_HALF)  21.3 us
    all_to_all x1, waiting for transfers between devices, scatter_sum(): lax.all_to_all(blocks, axis, 0, 0, axis_index_groups=groups)  19.6 us
    ppermute x2, starting transfers between devices, far_sum(): return quarter + lax.ppermute(quarter, 'inp', FAR_HALF)  15.9 us
  transfers between devices with their start and end apart: 19, of which 11 were waited for; matrix products, arithmetic and copies ran while one was open for 3% of the time, Pallas kernels for 0%

profile of v6, /device:TPU:6, one launch (start us, length us, event | category | flops | bytes accessed | tf_op | source)
XLA Modules:
  0.0 354.1 jit_solution(6736222024818874563)
XLA Ops:
  7.2 9.2 %collective-permute-start = (f32[48,768]{1,0:T(8,128)}, f32[48,768]{1,0:T(8,128)S(1)}, u32[]{:S(2)}, u32[]{:S(2)}) collective-permute-start(f32[48,768]{1,0:T(8,128)} %param.20), channel_id=1, source_target_pairs={{0,4},{1,5},{2,6},{3,7},{4,0},{5,1},{6,2},{7,3},{8,12},{9,13},{10,... | collective-permute-start | bytes 442376 | tf_op jit(solution)/shard_map/ppermute | solution.py:139
  16.4 0.7 convert_element_type.20
  17.1 0.8 reshape.90
  18.0 0.1 reshape.91
  18.1 0.7 pad_maximum_fusion.5
  18.8 5.9 %all-to-all-start = ((f32[4,16,128]{2,1,0:T(8,128)}), f32[4,16,128]{2,1,0:T(8,128)S(1)}, u32[]{:S(2)}, u32[]{:S(2)}) async-start(f32[4,16,128]{2,1,0:T(8,128)} %pad_maximum_fusion.5), calls=%async_computation | async-start | bytes 65536 | tf_op jit(solution)/shard_map/all_to_all | solution.py:147
  24.7 5.9 %all-to-all-done = f32[4,16,128]{2,1,0:T(8,128)S(1)} async-done(((f32[4,16,128]{2,1,0:T(8,128)}), f32[4,16,128]{2,1,0:T(8,128)S(1)}, u32[]{:S(2)}, u32[]{:S(2)}) %all-to-all-start) | async-done | bytes 32800 | tf_op jit(solution)/shard_map/all_to_all | solution.py:147
  30.6 0.7 broadcast_in_dim.21
  31.4 4.8 %all-to-all-start.1 = ((f32[8,4,16,128]{3,2,1,0:T(8,128)}), f32[8,4,16,128]{3,2,1,0:T(8,128)S(1)}, u32[]{:S(2)}, u32[]{:S(2)}) async-start(f32[8,4,16,128]{3,2,1,0:T(8,128)} %broadcast_in_dim.21), calls=%async_computation.1 | async-start | bytes 524288 | tf_op jit(solution)/shard_map/all_to_all | solution.py:77
  36.2 5.4 %all-to-all-done.1 = f32[8,4,16,128]{3,2,1,0:T(8,128)S(1)} async-done(((f32[8,4,16,128]{3,2,1,0:T(8,128)}), f32[8,4,16,128]{3,2,1,0:T(8,128)S(1)}, u32[]{:S(2)}, u32[]{:S(2)}) %all-to-all-start.1) | async-done | bytes 262176 | tf_op jit(solution)/shard_map/all_to_all | solution.py:77
  41.6 1.9 fusion
  43.6 4.5 %all-to-all-start.2 = ((f32[4,128,768]{2,1,0:T(8,128)}), f32[4,128,768]{2,1,0:T(8,128)S(1)}, u32[]{:S(2)}, u32[]{:S(2)}) async-start(f32[4,128,768]{2,1,0:T(8,128)} %bitcast.5), calls=%async_computation.2 | async-start | bytes 3145728 | tf_op jit(solution)/shard_map/all_to_all | solution.py:72
  48.0 0.7 all-gather.6.cloned.1.call-update
  48.7 19.6 %all-to-all-done.2 = f32[4,128,768]{2,1,0:T(8,128)S(1)} async-done(((f32[4,128,768]{2,1,0:T(8,128)}), f32[4,128,768]{2,1,0:T(8,128)S(1)}, u32[]{:S(2)}, u32[]{:S(2)}) %all-to-all-start.2) | async-done | bytes 1572896 | tf_op jit(solution)/shard_map/all_to_all | solution.py:72
  68.4 0.1 reduce_sum.81
  68.5 22.8 %all_to_all.55 = f32[4,32,768]{2,1,0:T(8,128)S(1)} all-to-all(f32[4,32,768]{2,1,0:T(8,128)S(1)} %bitcast.85), channel_id=1, replica_groups={{0,1,2,3},{4,5,6,7},{8,9,10,11},{12,13,14,15},{16,17,18,19},{20,21,22,2..., dimensions={0} | all-to-all | bytes 786432 | tf_op jit(solution)/shard_map/all_to_all | solution.py:72
  91.3 13.3 %collective-permute-start.1 = (f32[32,768]{1,0:T(8,128)S(1)}, f32[32,768]{1,0:T(8,128)S(1)}, u32[]{:S(2)}, u32[]{:S(2)}) collective-permute-start(f32[32,768]{1,0:T(8,128)S(1)} %reduce_sum.82), channel_id=1, source_target_pairs={{0,256},{64,320},{128,384},{192,448},{256,0},{320,64},{384,128},{4... | collective-permute-start | bytes 294920 | tf_op jit(solution)/shard_map/ppermute | solution.py:96
  104.6 7.0 %collective-permute-done.1 = f32[32,768]{1,0:T(8,128)S(1)} collective-permute-done((f32[32,768]{1,0:T(8,128)S(1)}, f32[32,768]{1,0:T(8,128)S(1)}, u32[]{:S(2)}, u32[]{:S(2)}) %collective-permute-start.1) | collective-permute-done | bytes 98336 | tf_op jit(solution)/shard_map/ppermute | solution.py:96
  111.7 0.8 broadcast_in_dim.22
  112.5 3.5 all-to-all-start.4
  116.0 7.3 %all-to-all-done.4 = f32[4,32,768]{2,1,0:T(8,128)S(1)} async-done(((f32[4,32,768]{2,1,0:T(8,128)}), f32[4,32,768]{2,1,0:T(8,128)S(1)}, u32[]{:S(2)}, u32[]{:S(2)}) %all-to-all-start.4) | async-done | bytes 393248 | tf_op jit(solution)/shard_map/all_to_all | solution.py:77
  123.3 1.3 slice_bitcast_fusion.2
  124.8 0.5 fusion.22
  125.3 9.0 %all_to_all.56 = f32[8,16,384]{2,1,0:T(8,128)S(1)} all-to-all(f32[8,16,384]{2,1,0:T(8,128)S(1)} %fusion.22), channel_id=1, replica_groups=mesh['inp'=8,'hid'=8,'tok'=8] {'hid'}, dimensions={0} | all-to-all | bytes 393216 | tf_op jit(solution)/shard_map/all_to_all | solution.py:72
  134.4 0.7 broadcast_in_dim.23
  135.1 5.4 %all-to-all-start.6 = ((f32[8,16,384]{2,1,0:T(8,128)}), f32[8,16,384]{2,1,0:T(8,128)S(1)}, u32[]{:S(2)}, u32[]{:S(2)}) async-start(f32[8,16,384]{2,1,0:T(8,128)} %broadcast_in_dim.23), calls=%async_computation.6 | async-start | bytes 393216 | tf_op jit(solution)/shard_map/all_to_all | solution.py:77
  140.5 0.2 slice_reduce_fusion
  140.9 0.2 copy.49
  141.1 4.1 %all-to-all-done.6 = f32[8,16,384]{2,1,0:T(8,128)S(1)} async-done(((f32[8,16,384]{2,1,0:T(8,128)}), f32[8,16,384]{2,1,0:T(8,128)S(1)}, u32[]{:S(2)}, u32[]{:S(2)}) %all-to-all-start.6) | async-done | bytes 196640 | tf_op jit(solution)/shard_map/all_to_all | solution.py:77
  145.2 0.1 multiply_reduce_fusion
  145.4 0.6 fusion.24
  146.1 2.5 collective-permute-start.4
  148.5 4.6 %collective-permute-start.3 = (f32[32,768]{1,0:T(8,128)S(1)}, f32[32,768]{1,0:T(8,128)S(1)}, u32[]{:S(2)}, u32[]{:S(2)}) collective-permute-start(f32[32,768]{1,0:T(8,128)S(1)} %get-tuple-element.43), channel_id=1, source_target_pairs={{0,192},{64,0},{128,64},{192,128},{256,448},{320,256},{384,320},{4... | collective-permute-start | bytes 294920 | tf_op jit(solution)/shard_map/ppermute | solution.py:91
  153.1 1.9 collective-permute-start.2
  155.1 0.1 select_reduce_fusion.1
  155.3 0.6 broadcast_in_dim.25
  155.9 17.4 %all-to-all-start.7 = ((f32[64,1,128]{2,1,0:T(1,128)}), f32[64,1,128]{2,1,0:T(1,128)S(1)}, u32[]{:S(2)}, u32[]{:S(2)}) async-start(f32[64,1,128]{2,1,0:T(1,128)} %broadcast_in_dim.25), calls=%async_computation.7 | async-start | bytes 65536 | tf_op jit(solution)/shard_map/all_to_all | solution.py:77
  173.4 14.6 %all-to-all-done.7 = f32[64,1,128]{2,1,0:T(1,128)S(1)} async-done(((f32[64,1,128]{2,1,0:T(1,128)}), f32[64,1,128]{2,1,0:T(1,128)S(1)}, u32[]{:S(2)}, u32[]{:S(2)}) %all-to-all-start.7) | async-done | bytes 32800 | tf_op jit(solution)/shard_map/all_to_all | solution.py:77
  188.2 0.1 select_reduce_fusion
  188.4 0.1 broadcast_multiply_fusion
  188.5 0.6 fusion.23
  189.2 1.1 pad_maximum_fusion.1
  190.3 2.6 collective-permute-start.5
  193.0 14.3 %collective-permute-done.5 = f32[32,768]{1,0:T(8,128)S(1)} collective-permute-done((f32[32,768]{1,0:T(8,128)S(1)}, f32[32,768]{1,0:T(8,128)S(1)}, u32[]{:S(2)}, u32[]{:S(2)}) %collective-permute-start.5) | collective-permute-done | bytes 98336 | tf_op jit(solution)/shard_map/ppermute | solution.py:96
  207.4 0.8 broadcast_in_dim.26
  208.1 5.3 %all-to-all-start.8 = ((f32[4,32,768]{2,1,0:T(8,128)}), f32[4,32,768]{2,1,0:T(8,128)S(1)}, u32[]{:S(2)}, u32[]{:S(2)}) async-start(f32[4,32,768]{2,1,0:T(8,128)} %broadcast_in_dim.26), calls=%async_computation.8 | async-start | bytes 786432 | tf_op jit(solution)/shard_map/all_to_all | solution.py:77
  213.5 0.7 reduce-scatter.2.cloned.1.call-update
  214.2 8.1 %all-to-all-done.8 = f32[4,32,768]{2,1,0:T(8,128)S(1)} async-done(((f32[4,32,768]{2,1,0:T(8,128)}), f32[4,32,768]{2,1,0:T(8,128)S(1)}, u32[]{:S(2)}, u32[]{:S(2)}) %all-to-all-start.8) | async-done | bytes 393248 | tf_op jit(solution)/shard_map/all_to_all | solution.py:77
  222.3 1.3 broadcast_in_dim.28
  223.6 3.6 %all-to-all-start.9 = ((f32[4,128,768]{2,1,0:T(8,128)}), f32[4,128,768]{2,1,0:T(8,128)S(1)}, u32[]{:S(2)}, u32[]{:S(2)}) async-start(f32[4,128,768]{2,1,0:T(8,128)} %broadcast_in_dim.28), calls=%async_computation.9 | async-start | bytes 3145728 | tf_op jit(solution)/shard_map/all_to_all | solution.py:77
  227.3 32.6 %reduce-scatter.2.cloned.1.call-done = f32[96,384]{1,0:T(8,128)} async-done(((f32[768,384]{1,0:T(8,128)}), f32[96,384]{1,0:T(8,128)}) %reduce-scatter.2.cloned.1.call-update) | async-done | bytes 147472 | tf_op jit(solution)/shard_map/reduce_scatter | solution.py:118
  259.9 0.6 fusion.4
  260.6 5.5 %collective-permute-start.6 = (f32[48,768]{1,0:T(8,128)S(1)}, f32[48,768]{1,0:T(8,128)S(1)}, u32[]{:S(2)}, u32[]{:S(2)}) collective-permute-start(f32[48,768]{1,0:T(8,128)S(1)} %slice_select_fusion), channel_id=1, source_target_pairs={{0,4},{1,5},{2,6},{3,7},{4,0},{5,1},{6,2},{7,3},{8,12},{9,13},{10,... | collective-permute-start | bytes 442376 | tf_op jit(solution)/shard_map/ppermute | solution.py:162
  266.1 11.6 %collective-permute-done.6 = f32[48,768]{1,0:T(8,128)S(1)} collective-permute-done((f32[48,768]{1,0:T(8,128)S(1)}, f32[48,768]{1,0:T(8,128)S(1)}, u32[]{:S(2)}, u32[]{:S(2)}) %collective-permute-start.6) | collective-permute-done | bytes 147488 | tf_op jit(solution)/shard_map/ppermute | solution.py:162
  277.7 0.9 multiply_add_fusion.2
  278.6 0.6 multiply_reduce_fusion.1
  279.9 0.8 multiply_add_fusion.1
  280.8 0.7 broadcast_in_dim.29
  281.5 6.4 %all-to-all-start.10 = ((f32[8,16,384]{2,1,0:T(8,128)}), f32[8,16,384]{2,1,0:T(8,128)S(1)}, u32[]{:S(2)}, u32[]{:S(2)}) async-start(f32[8,16,384]{2,1,0:T(8,128)} %broadcast_in_dim.29), calls=%async_computation.11 | async-start | bytes 393216 | tf_op jit(solution)/shard_map/all_to_all | solution.py:77
  287.9 54.6 %all-gather.2 = f32[640,384]{1,0:T(8,128)S(1)} all-gather(f32[80,384]{1,0:T(8,128)S(1)} %slice.78), channel_id=4, replica_groups={{0,2,4,6,7,5,3,1},{8,10,12,14,15,13,11,9},{16,18,20,22,23,21,19,17},{24..., dimensions={0}, use_global_device_ids=true | all-gather | bytes 1105920 | tf_op jit(solution)/shard_map/all_gather | solution.py:130
  342.7 1.1 pad_maximum_fusion.3
  343.8 1.3 fusion.20
  345.2 0.1 pad_maximum_fusion.2
  345.3 1.1 copy.51
  (71 shorter events, 1.6 us)
Async XLA Ops:
  7.2 29.0 %copy-start = (f32[48,768]{1,0:T(8,128)S(1)}, f32[48,768]{1,0:T(8,128)}, u32[]{:S(2)}) copy-start(f32[48,768]{1,0:T(8,128)} %param.20) | copy-start | bytes 442372
  7.2 29.0 %collective-permute-start = (f32[48,768]{1,0:T(8,128)}, f32[48,768]{1,0:T(8,128)S(1)}, u32[]{:S(2)}, u32[]{:S(2)}) collective-permute-start(f32[48,768]{1,0:T(8,128)} %param.20), channel_id=1, source_target_pairs={{0,4},{1,5},{2,6},{3,7},{4,0},{5,1},{6,2},{7,3},{8,12},{9,13},{10,... | collective-permute-start | bytes 442376 | tf_op jit(solution)/shard_map/ppermute | solution.py:139
  18.8 11.8 %all-to-all-start = ((f32[4,16,128]{2,1,0:T(8,128)}), f32[4,16,128]{2,1,0:T(8,128)S(1)}, u32[]{:S(2)}, u32[]{:S(2)}) async-start(f32[4,16,128]{2,1,0:T(8,128)} %pad_maximum_fusion.5), calls=%async_computation | async-start | bytes 65536 | tf_op jit(solution)/shard_map/all_to_all | solution.py:147
  31.4 10.2 %all-to-all-start.1 = ((f32[8,4,16,128]{3,2,1,0:T(8,128)}), f32[8,4,16,128]{3,2,1,0:T(8,128)S(1)}, u32[]{:S(2)}, u32[]{:S(2)}) async-start(f32[8,4,16,128]{3,2,1,0:T(8,128)} %broadcast_in_dim.21), calls=%async_computation.1 | async-start | bytes 524288 | tf_op jit(solution)/shard_map/all_to_all | solution.py:77
  43.6 24.8 %all-to-all-start.2 = ((f32[4,128,768]{2,1,0:T(8,128)}), f32[4,128,768]{2,1,0:T(8,128)S(1)}, u32[]{:S(2)}, u32[]{:S(2)}) async-start(f32[4,128,768]{2,1,0:T(8,128)} %bitcast.5), calls=%async_computation.2 | async-start | bytes 3145728 | tf_op jit(solution)/shard_map/all_to_all | solution.py:72
  48.0 68.0 %all-gather.6.cloned.1.call-start = ((), (), s32[]{:S(2)}) async-start(), calls=%async_computation.13 | async-start | bytes 1327104 | tf_op jit(solution)/shard_map/all_gather | solution.py:105
  91.3 20.4 %collective-permute-start.1 = (f32[32,768]{1,0:T(8,128)S(1)}, f32[32,768]{1,0:T(8,128)S(1)}, u32[]{:S(2)}, u32[]{:S(2)}) collective-permute-start(f32[32,768]{1,0:T(8,128)S(1)} %reduce_sum.82), channel_id=1, source_target_pairs={{0,256},{64,320},{128,384},{192,448},{256,0},{320,64},{384,128},{4... | collective-permute-start | bytes 294920 | tf_op jit(solution)/shard_map/ppermute | solution.py:96
  112.5 10.8 %all-to-all-start.4 = ((f32[4,32,768]{2,1,0:T(8,128)}), f32[4,32,768]{2,1,0:T(8,128)S(1)}, u32[]{:S(2)}, u32[]{:S(2)}) async-start(f32[4,32,768]{2,1,0:T(8,128)} %broadcast_in_dim.22), calls=%async_computation.4 | async-start | bytes 786432 | tf_op jit(solution)/shard_map/all_to_all | solution.py:77
  124.8 9.6 %copy-start.9 = (f32[16,384]{1,0:T(8,128)S(1)}, f32[16,384]{1,0:T(8,128)}, u32[]{:S(2)}) copy-start(f32[16,384]{1,0:T(8,128)} %param.15) | copy-start | bytes 73732
  135.1 10.1 %all-to-all-start.6 = ((f32[8,16,384]{2,1,0:T(8,128)}), f32[8,16,384]{2,1,0:T(8,128)S(1)}, u32[]{:S(2)}, u32[]{:S(2)}) async-start(f32[8,16,384]{2,1,0:T(8,128)} %broadcast_in_dim.23), calls=%async_computation.6 | async-start | bytes 393216 | tf_op jit(solution)/shard_map/all_to_all | solution.py:77
  145.4 42.7 %copy-start.10 = (s32[16]{0:T(128)S(1)}, s32[16]{0:T(128)}, u32[]{:S(2)}) copy-start(s32[16]{0:T(128)} %param.17) | copy-start | bytes 196
  145.4 42.7 %copy-start.11 = (f32[16]{0:T(128)S(1)}, f32[16]{0:T(128)}, u32[]{:S(2)}) copy-start(f32[16]{0:T(128)} %param.19) | copy-start | bytes 196
  145.4 42.7 %copy-start.12 = (f32[16]{0:T(128)S(1)}, f32[16]{0:T(128)}, u32[]{:S(2)}) copy-start(f32[16]{0:T(128)} %param.18) | copy-start | bytes 196
  146.1 27.3 %collective-permute-start.4 = (f32[32,768]{1,0:T(8,128)S(1)}, f32[32,768]{1,0:T(8,128)S(1)}, u32[]{:S(2)}, u32[]{:S(2)}) collective-permute-start(f32[32,768]{1,0:T(8,128)S(1)} %get-tuple-element.42), channel_id=1, source_target_pairs={{0,128},{64,192},{128,0},{192,64},{256,384},{320,448},{384,256},{4... | collective-permute-start | bytes 294920 | tf_op jit(solution)/shard_map/ppermute | solution.py:91
  148.5 24.8 %collective-permute-start.3 = (f32[32,768]{1,0:T(8,128)S(1)}, f32[32,768]{1,0:T(8,128)S(1)}, u32[]{:S(2)}, u32[]{:S(2)}) collective-permute-start(f32[32,768]{1,0:T(8,128)S(1)} %get-tuple-element.43), channel_id=1, source_target_pairs={{0,192},{64,0},{128,64},{192,128},{256,448},{320,256},{384,320},{4... | collective-permute-start | bytes 294920 | tf_op jit(solution)/shard_map/ppermute | solution.py:91
  153.1 20.3 %collective-permute-start.2 = (f32[32,768]{1,0:T(8,128)S(1)}, f32[32,768]{1,0:T(8,128)S(1)}, u32[]{:S(2)}, u32[]{:S(2)}) collective-permute-start(f32[32,768]{1,0:T(8,128)S(1)} %get-tuple-element.41), channel_id=1, source_target_pairs={{0,64},{64,128},{128,192},{192,0},{256,320},{320,384},{384,448},{4... | collective-permute-start | bytes 294920 | tf_op jit(solution)/shard_map/ppermute | solution.py:91
  155.9 32.1 %all-to-all-start.7 = ((f32[64,1,128]{2,1,0:T(1,128)}), f32[64,1,128]{2,1,0:T(1,128)S(1)}, u32[]{:S(2)}, u32[]{:S(2)}) async-start(f32[64,1,128]{2,1,0:T(1,128)} %broadcast_in_dim.25), calls=%async_computation.7 | async-start | bytes 65536 | tf_op jit(solution)/shard_map/all_to_all | solution.py:77
  190.3 17.0 %collective-permute-start.5 = (f32[32,768]{1,0:T(8,128)S(1)}, f32[32,768]{1,0:T(8,128)S(1)}, u32[]{:S(2)}, u32[]{:S(2)}) collective-permute-start(f32[32,768]{1,0:T(8,128)S(1)} %fusion.16), channel_id=1, source_target_pairs={{0,256},{64,320},{128,384},{192,448},{256,0},{320,64},{384,128},{4... | collective-permute-start | bytes 294920 | tf_op jit(solution)/shard_map/ppermute | solution.py:96
  208.1 14.2 %all-to-all-start.8 = ((f32[4,32,768]{2,1,0:T(8,128)}), f32[4,32,768]{2,1,0:T(8,128)S(1)}, u32[]{:S(2)}, u32[]{:S(2)}) async-start(f32[4,32,768]{2,1,0:T(8,128)} %broadcast_in_dim.26), calls=%async_computation.8 | async-start | bytes 786432 | tf_op jit(solution)/shard_map/all_to_all | solution.py:77
  213.5 46.4 %reduce-scatter.2.cloned.1.call-start = ((), (), s32[]{:S(2)}) async-start(), calls=%async_computation.12 | async-start | bytes 1327104 | tf_op jit(solution)/shard_map/reduce_scatter | solution.py:118
  223.6 36.3 %all-to-all-start.9 = ((f32[4,128,768]{2,1,0:T(8,128)}), f32[4,128,768]{2,1,0:T(8,128)S(1)}, u32[]{:S(2)}, u32[]{:S(2)}) async-start(f32[4,128,768]{2,1,0:T(8,128)} %broadcast_in_dim.28), calls=%async_computation.9 | async-start | bytes 3145728 | tf_op jit(solution)/shard_map/all_to_all | solution.py:77
  227.2 116.6 %all-gather.8.cloned.1.call-start = ((), (), s32[]{:S(2)}) async-start(), calls=%async_computation.14 | async-start | bytes 1327104 | tf_op jit(solution)/shard_map/all_gather | solution.py:105
  259.9 17.8 %copy-start.2 = (f32[48,768]{1,0:T(8,128)S(1)}, f32[48,768]{1,0:T(8,128)}, u32[]{:S(2)}) copy-start(f32[48,768]{1,0:T(8,128)} %param.26) | copy-start | bytes 442372
  259.9 17.8 %copy-start.3 = (f32[48,768]{1,0:T(8,128)S(1)}, f32[48,768]{1,0:T(8,128)}, u32[]{:S(2)}) copy-start(f32[48,768]{1,0:T(8,128)} %param.22) | copy-start | bytes 442372
  259.9 17.8 %copy-start.4 = (f32[48,768]{1,0:T(8,128)S(1)}, f32[48,768]{1,0:T(8,128)}, u32[]{:S(2)}) copy-start(f32[48,768]{1,0:T(8,128)} %param.24) | copy-start | bytes 442372
  260.5 19.4 %copy-start.1 = (f32[96,384]{1,0:T(8,128)S(1)}, f32[96,384]{1,0:T(8,128)}, u32[]{:S(2)}) copy-start(f32[96,384]{1,0:T(8,128)} %param.21) | copy-start | bytes 442372
  260.5 19.4 %copy-start.5 = (f32[96,384]{1,0:T(8,128)S(1)}, f32[96,384]{1,0:T(8,128)}, u32[]{:S(2)}) copy-start(f32[96,384]{1,0:T(8,128)} %param.27) | copy-start | bytes 442372
  260.5 19.4 %copy-start.6 = (f32[96,384]{1,0:T(8,128)S(1)}, f32[96,384]{1,0:T(8,128)}, u32[]{:S(2)}) copy-start(f32[96,384]{1,0:T(8,128)} %param.23) | copy-start | bytes 442372
  260.6 19.4 %copy-start.7 = (f32[96,384]{1,0:T(8,128)S(1)}, f32[96,384]{1,0:T(8,128)}, u32[]{:S(2)}) copy-start(f32[96,384]{1,0:T(8,128)} %param.25) | copy-start | bytes 442372
  260.6 19.4 %copy-start.8 = (f32[96,384]{1,0:T(8,128)S(1)}, f32[96,384]{1,0:T(8,128)}, u32[]{:S(2)}) copy-start(f32[96,384]{1,0:T(8,128)} %reduce-scatter.2.cloned.1.call-done) | copy-start | bytes 442372
  260.6 17.1 %collective-permute-start.6 = (f32[48,768]{1,0:T(8,128)S(1)}, f32[48,768]{1,0:T(8,128)S(1)}, u32[]{:S(2)}, u32[]{:S(2)}) collective-permute-start(f32[48,768]{1,0:T(8,128)S(1)} %slice_select_fusion), channel_id=1, source_target_pairs={{0,4},{1,5},{2,6},{3,7},{4,0},{5,1},{6,2},{7,3},{8,12},{9,13},{10,... | collective-permute-start | bytes 442376 | tf_op jit(solution)/shard_map/ppermute | solution.py:162
  281.5 61.2 %all-to-all-start.10 = ((f32[8,16,384]{2,1,0:T(8,128)}), f32[8,16,384]{2,1,0:T(8,128)S(1)}, u32[]{:S(2)}, u32[]{:S(2)}) async-start(f32[8,16,384]{2,1,0:T(8,128)} %broadcast_in_dim.29), calls=%async_computation.11 | async-start | bytes 393216 | tf_op jit(solution)/shard_map/all_to_all | solution.py:77
Sparse Core Ops, SparseCore 0:
  50.9 64.4 all-gather.5
  217.7 42.1 reduce-scatter.1
  278.8 63.2 all-gather.7
